TPU v7x, 512 devices: a whole 4x8x8 slice. The times are simulated.
512 devices in a mesh: sector: 16 (over y, z_hi), block: 16 (over z_lo, x), flame: 2 (over core).
Axes of the slice: x: 4, y: 8, z: 8 (z_hi: 2, z_lo: 4; z = z_hi * 4 + z_lo), core: 2. Of those that a mesh axis runs over, the one named last changes fastest.
Arguments:
- rhs_direct: float32 [128, 256, 512], P('sector', 'block', 'flame'), may hold values from -6 to 6
- rhs_adjoint: float32 [128, 256, 512], P('sector', 'block', 'flame'), may hold values from -6 to 6
- diag_shift: float32 [128, 256, 512], P('sector', 'block', 'flame'), may hold values from 1 to 3
- flame_gain: float32 [128, 256, 512], P('sector', 'block', 'flame'), may hold values from -0.6 to 0.6
- ref_owner: int32 [128, 256, 512], P('sector', 'block', 'flame'), may hold values from 0 to 255
Outputs:
- field_first: float32 [128, 256, 512], P('sector', 'block', 'flame')
- field_second: float32 [128, 256, 512], P('sector', 'block', 'flame')
All inputs are finite; a program needn't handle non-finite values.
Results may differ from a plain program's by a relative error of at most 0.00018.
Values sent between devices are 32-bit elements; how exact they have to be, the bound alone decides.
No kernel may reach another device: no remote copies, remote signals or barrier semaphores. Data moves between devices by JAX's collectives and lax.ppermute only.
A program may use at most 64 MiB of HBM per device.

v0:
```python
import jax
import jax.numpy as jnp
from jax import lax
from jax.sharding import PartitionSpec as P

REF_DEV = 8
ITERS = 6


def extended(cells, sides, width, closed):
    for axis, dim in sides:
        count = lax.axis_size(axis)
        ends = count if closed else count - 1
        head = lax.slice_in_dim(cells, 0, width, axis=dim)
        tail = lax.slice_in_dim(cells, cells.shape[dim] - width, cells.shape[dim], axis=dim)
        cells = jnp.concatenate(
            [
                lax.ppermute(tail, axis, [(i, (i + 1) % count) for i in range(ends)]),
                cells,
                lax.ppermute(head, axis, [((i + 1) % count, i) for i in range(ends)]),
            ],
            axis=dim,
        )
    return cells


def on_device(rhs_direct, rhs_adjoint, diag_shift, flame_gain, ref_owner):
    planes, axial, radial = rhs_direct.shape
    spacing = radial // REF_DEV
    ref_count = REF_DEV * lax.axis_size("block") * lax.axis_size("flame")
    owner_rows = ref_owner.reshape(planes, axial * radial)
    ref_ids = jnp.arange(ref_count, dtype=jnp.int32)[:, None]
    inverse = 1.0 / (6.0 + diag_shift)

    def lookup(table):

        def slab_lookup(owners_row):
            return jnp.sum(jnp.where(owners_row[None, :] == ref_ids, table[:, None], 0.0), axis=0)

        return lax.map(slab_lookup, owner_rows).reshape(planes, axial, radial)

    def flame_direct(field):
        local_refs = field[0, 0, ::spacing]
        table = lax.all_gather(local_refs, ("block", "flame"), axis=0, tiled=True)
        return flame_gain * lookup(table)

    def neighbours(stacked):
        cycle = extended(stacked, (("sector", 1),), 1, True)
        walls = extended(stacked, (("block", 2), ("flame", 3)), 1, False)
        total = cycle[:, 2:] + cycle[:, :-2]
        total = total + walls[:, :, 2:, 1:-1] + walls[:, :, :-2, 1:-1]
        return total + walls[:, :, 1:-1, 2:] + walls[:, :, 1:-1, :-2]

    direct = rhs_direct * inverse
    adjoint = rhs_adjoint * inverse
    for sweeps in range(ITERS):
        near_direct = neighbours(direct[None])[0]
        near_adjoint = neighbours(adjoint[None])[0]
        direct_next = (rhs_direct + near_direct + flame_direct(direct)) * inverse

        def slab_collect(slab_pair):
            owners_row, values_row = slab_pair
            return jnp.sum(
                jnp.where(owners_row[None, :] == ref_ids, values_row[None, :], 0.0), axis=1
            )

        partial_sums = lax.map(
            slab_collect, (owner_rows, (flame_gain * adjoint).reshape(planes, axial * radial))
        )
        partial_table = jnp.sum(partial_sums, axis=0)
        totals = lax.psum(partial_table, ("block", "flame"))
        mine = lax.dynamic_slice_in_dim(
            totals, lax.axis_index(("block", "flame")) * REF_DEV, REF_DEV
        )
        adjoint_next = (
            rhs_adjoint + near_adjoint + jnp.zeros_like(adjoint).at[0, 0, ::spacing].set(mine)
        ) * inverse
        direct, adjoint = (direct_next, adjoint_next)
    response = flame_direct(direct)
    direct_sq, adjoint_sq = lax.psum(
        (jnp.sum(direct * direct), jnp.sum(adjoint * adjoint)), ("sector", "block", "flame")
    )
    cell_count = (
        planes
        * axial
        * radial
        * lax.axis_size("sector")
        * lax.axis_size("block")
        * lax.axis_size("flame")
    )
    scale = lax.rsqrt(direct_sq / cell_count * (adjoint_sq / cell_count) + 1e-12)
    field_first = adjoint * direct * scale
    field_second = adjoint * response * scale
    return (field_first, field_second)


def solution(mesh):
    placed = (
        P("sector", "block", "flame"),
        P("sector", "block", "flame"),
        P("sector", "block", "flame"),
        P("sector", "block", "flame"),
        P("sector", "block", "flame"),
    )
    return jax.shard_map(
        on_device,
        mesh=mesh,
        in_specs=placed,
        out_specs=(P("sector", "block", "flame"), P("sector", "block", "flame")),
        check_vma=False,
    )
```

profile of v0, /device:TPU:1, one launch (start us, length us, event | category | flops | bytes accessed | tf_op | source)
XLA Modules:
  0.0 961.3 jit_solution(1872722840597201207)
XLA Ops:
  7.8 13.8 %collective-permute-start.36 = (f32[1,1,16,256]{3,2,1,0:T(8,128)S(1)}, f32[1,1,16,256]{3,2,1,0:T(8,128)S(1)}, u32[]{:S(2)}, u32[]{:S(2)}) collective-permute-start(f32[1,1,16,256]{3,2,1,0:T(8,128)S(1)} %get-tuple-element.701), channel_id=1, source_target_pairs={{32,0},{64,32},{96,64},{128,96},{160,128},{192,160},{224,192},{256... | collective-permute-start | bytes 49160 | tf_op jit(solution)/shard_map/ppermute | solution.py:20
  27.0 69.6 %all-reduce.1 = f32[256]{0:T(256)S(1)} all-reduce(f32[256]{0:T(256)S(1)} %bitcast_dynamic-update-slice_fusion.6), channel_id=2, replica_groups=mesh['sector'=16,'block'=16,'flame'=2] {'block','flame'}, use_global_device_ids=true, to_apply=%add.1 | all-reduce | flops 256 | bytes 2048 | tf_op jit(solution)/shard_map/all_gather | solution.py:44
  96.6 9.5 while.149
  113.4 9.7 %collective-permute-start = (f32[1,1,16,256]{3,2,1,0:T(8,128)S(1)}, f32[1,1,16,256]{3,2,1,0:T(8,128)S(1)}, u32[]{:S(2)}, u32[]{:S(2)}) collective-permute-start(f32[1,1,16,256]{3,2,1,0:T(8,128)S(1)} %get-tuple-element.696), channel_id=1, source_target_pairs={{32,0},{64,32},{96,64},{128,96},{160,128},{192,160},{224,192},{256... | collective-permute-start | bytes 49160 | tf_op jit(solution)/shard_map/ppermute | solution.py:20
  138.0 67.8 %all-reduce.14 = (f32[256]{0:T(256)S(1)}, f32[256]{0:T(256)S(1)}) all-reduce(f32[256]{0:T(256)S(1)} %reduce_sum.189, f32[256]{0:T(256)S(1)} %bitcast_dynamic-update-slice_fusion.5), channel_id=1, replica_groups=mesh['sector'=16,'block'=16,'flame'=2] {'block','flame'}, use_global_device_ids=true, to_apply=%region_4.5 | all-reduce | flops 512 | bytes 4096 | tf_op jit(solution)/shard_map/psum | solution.py:71
  217.8 9.5 while.150
  227.3 9.7 %collective-permute-start.42 = (f32[1,1,16,256]{3,2,1,0:T(8,128)S(1)}, f32[1,1,16,256]{3,2,1,0:T(8,128)S(1)}, u32[]{:S(2)}, u32[]{:S(2)}) collective-permute-start(f32[1,1,16,256]{3,2,1,0:T(8,128)S(1)} %get-tuple-element.692), channel_id=1, source_target_pairs={{32,0},{64,32},{96,64},{128,96},{160,128},{192,160},{224,192},{256... | collective-permute-start | bytes 49160 | tf_op jit(solution)/shard_map/ppermute | solution.py:20
  267.1 67.8 %all-reduce.13 = (f32[256]{0:T(256)S(1)}, f32[256]{0:T(256)S(1)}) all-reduce(f32[256]{0:T(256)S(1)} %reduce_sum.190, f32[256]{0:T(256)S(1)} %bitcast_dynamic-update-slice_fusion.4), channel_id=1, replica_groups=mesh['sector'=16,'block'=16,'flame'=2] {'block','flame'}, use_global_device_ids=true, to_apply=%region_10.11 | all-reduce | flops 512 | bytes 4096 | tf_op jit(solution)/shard_map/psum | solution.py:71
  346.8 9.5 while.151
  356.4 9.7 %collective-permute-start.48 = (f32[1,1,16,256]{3,2,1,0:T(8,128)S(1)}, f32[1,1,16,256]{3,2,1,0:T(8,128)S(1)}, u32[]{:S(2)}, u32[]{:S(2)}) collective-permute-start(f32[1,1,16,256]{3,2,1,0:T(8,128)S(1)} %get-tuple-element.684), channel_id=1, source_target_pairs={{32,0},{64,32},{96,64},{128,96},{160,128},{192,160},{224,192},{256... | collective-permute-start | bytes 49160 | tf_op jit(solution)/shard_map/ppermute | solution.py:20
  373.9 9.4 collective-permute-start.12
  396.1 67.8 %all-reduce.12 = (f32[256]{0:T(256)S(1)}, f32[256]{0:T(256)S(1)}) all-reduce(f32[256]{0:T(256)S(1)} %reduce_sum.191, f32[256]{0:T(256)S(1)} %bitcast_dynamic-update-slice_fusion.3), channel_id=1, replica_groups=mesh['sector'=16,'block'=16,'flame'=2] {'block','flame'}, use_global_device_ids=true, to_apply=%region_16.17 | all-reduce | flops 512 | bytes 4096 | tf_op jit(solution)/shard_map/psum | solution.py:71
  476.1 9.5 while.152
  485.6 9.7 %collective-permute-start.54 = (f32[1,1,16,256]{3,2,1,0:T(8,128)S(1)}, f32[1,1,16,256]{3,2,1,0:T(8,128)S(1)}, u32[]{:S(2)}, u32[]{:S(2)}) collective-permute-start(f32[1,1,16,256]{3,2,1,0:T(8,128)S(1)} %get-tuple-element.676), channel_id=1, source_target_pairs={{32,0},{64,32},{96,64},{128,96},{160,128},{192,160},{224,192},{256... | collective-permute-start | bytes 49160 | tf_op jit(solution)/shard_map/ppermute | solution.py:20
  503.1 9.4 collective-permute-start.18
  525.4 67.8 %all-reduce.11 = (f32[256]{0:T(256)S(1)}, f32[256]{0:T(256)S(1)}) all-reduce(f32[256]{0:T(256)S(1)} %reduce_sum.192, f32[256]{0:T(256)S(1)} %bitcast_dynamic-update-slice_fusion.2), channel_id=1, replica_groups=mesh['sector'=16,'block'=16,'flame'=2] {'block','flame'}, use_global_device_ids=true, to_apply=%region_22.23 | all-reduce | flops 512 | bytes 4096 | tf_op jit(solution)/shard_map/psum | solution.py:71
  605.2 9.5 while.153
  614.7 9.7 %collective-permute-start.60 = (f32[1,1,16,256]{3,2,1,0:T(8,128)S(1)}, f32[1,1,16,256]{3,2,1,0:T(8,128)S(1)}, u32[]{:S(2)}, u32[]{:S(2)}) collective-permute-start(f32[1,1,16,256]{3,2,1,0:T(8,128)S(1)} %get-tuple-element.668), channel_id=1, source_target_pairs={{32,0},{64,32},{96,64},{128,96},{160,128},{192,160},{224,192},{256... | collective-permute-start | bytes 49160 | tf_op jit(solution)/shard_map/ppermute | solution.py:20
  654.4 67.8 %all-reduce.10 = (f32[256]{0:T(256)S(1)}, f32[256]{0:T(256)S(1)}) all-reduce(f32[256]{0:T(256)S(1)} %reduce_sum.193, f32[256]{0:T(256)S(1)} %bitcast_dynamic-update-slice_fusion.1), channel_id=1, replica_groups=mesh['sector'=16,'block'=16,'flame'=2] {'block','flame'}, use_global_device_ids=true, to_apply=%region_28.29 | all-reduce | flops 512 | bytes 4096 | tf_op jit(solution)/shard_map/psum | solution.py:71
  734.2 9.5 while.154
  743.7 9.7 %collective-permute-start.66 = (f32[1,1,16,256]{3,2,1,0:T(8,128)S(1)}, f32[1,1,16,256]{3,2,1,0:T(8,128)S(1)}, u32[]{:S(2)}, u32[]{:S(2)}) collective-permute-start(f32[1,1,16,256]{3,2,1,0:T(8,128)S(1)} %get-tuple-element.660), channel_id=1, source_target_pairs={{32,0},{64,32},{96,64},{128,96},{160,128},{192,160},{224,192},{256... | collective-permute-start | bytes 49160 | tf_op jit(solution)/shard_map/ppermute | solution.py:20
  784.1 67.8 %all-reduce.9 = (f32[256]{0:T(256)S(1)}, f32[256]{0:T(256)S(1)}) all-reduce(f32[256]{0:T(256)S(1)} %reduce_sum.194, f32[256]{0:T(256)S(1)} %bitcast_dynamic-update-slice_fusion), channel_id=1, replica_groups=mesh['sector'=16,'block'=16,'flame'=2] {'block','flame'}, use_global_device_ids=true, to_apply=%region_34.35 | all-reduce | flops 512 | bytes 4096 | tf_op jit(solution)/shard_map/psum | solution.py:71
  853.8 95.9 %all-reduce.8 = (f32[]{:T(128)}, f32[]{:T(128)}) all-reduce(f32[]{:T(128)} %get-tuple-element.616, f32[]{:T(128)} %get-tuple-element.614), channel_id=1, replica_groups=mesh['sector'=16,'block'=16,'flame'=2] {'sector','block','flame'}, use_global_device_ids=true, to_apply=%region_55.56 | all-reduce | flops 2 | bytes 16 | tf_op jit(solution)/shard_map/psum | solution.py:80
  951.1 9.5 while.155
  (640 shorter events, 324.5 us)
Async XLA Ops:
  1.8 110.3 %collective-permute-start.38 = (f32[1,8,1,256]{3,2,1,0:T(1,128)S(1)}, f32[1,8,1,256]{3,2,1,0:T(1,128)S(1)}, u32[]{:S(2)}, u32[]{:S(2)}) collective-permute-start(f32[1,8,1,256]{3,2,1,0:T(1,128)S(1)} %get-tuple-element.704), channel_id=1, source_target_pairs={{2,0},{4,2},{6,4},{8,6},{10,8},{12,10},{14,12},{16,14},{18,16},{20... | collective-permute-start | bytes 24584 | tf_op jit(solution)/shard_map/ppermute | solution.py:20
  3.2 110.1 %collective-permute-start.39 = (f32[1,8,1,256]{3,2,1,0:T(1,128)S(1)}, f32[1,8,1,256]{3,2,1,0:T(1,128)S(1)}, u32[]{:S(2)}, u32[]{:S(2)}) collective-permute-start(f32[1,8,1,256]{3,2,1,0:T(1,128)S(1)} %get-tuple-element.703), channel_id=1, source_target_pairs={{0,2},{2,4},{4,6},{6,8},{8,10},{10,12},{12,14},{14,16},{16,18},{18... | collective-permute-start | bytes 24584 | tf_op jit(solution)/shard_map/ppermute | solution.py:18
  7.8 128.4 %collective-permute-start.36 = (f32[1,1,16,256]{3,2,1,0:T(8,128)S(1)}, f32[1,1,16,256]{3,2,1,0:T(8,128)S(1)}, u32[]{:S(2)}, u32[]{:S(2)}) collective-permute-start(f32[1,1,16,256]{3,2,1,0:T(8,128)S(1)} %get-tuple-element.701), channel_id=1, source_target_pairs={{32,0},{64,32},{96,64},{128,96},{160,128},{192,160},{224,192},{256... | collective-permute-start | bytes 49160 | tf_op jit(solution)/shard_map/ppermute | solution.py:20
  21.6 115.9 %collective-permute-start.37 = (f32[1,1,16,256]{3,2,1,0:T(8,128)S(1)}, f32[1,1,16,256]{3,2,1,0:T(8,128)S(1)}, u32[]{:S(2)}, u32[]{:S(2)}) collective-permute-start(f32[1,1,16,256]{3,2,1,0:T(8,128)S(1)} %get-tuple-element.702), channel_id=1, source_target_pairs={{0,32},{32,64},{64,96},{96,128},{128,160},{160,192},{192,224},{224... | collective-permute-start | bytes 49160 | tf_op jit(solution)/shard_map/ppermute | solution.py:18
  23.6 99.6 %collective-permute-start.2 = (f32[1,8,1,256]{3,2,1,0:T(1,128)S(1)}, f32[1,8,1,256]{3,2,1,0:T(1,128)S(1)}, u32[]{:S(2)}, u32[]{:S(2)}) collective-permute-start(f32[1,8,1,256]{3,2,1,0:T(1,128)S(1)} %get-tuple-element.699), channel_id=1, source_target_pairs={{2,0},{4,2},{6,4},{8,6},{10,8},{12,10},{14,12},{16,14},{18,16},{20... | collective-permute-start | bytes 24584 | tf_op jit(solution)/shard_map/ppermute | solution.py:20
  113.4 93.5 %collective-permute-start = (f32[1,1,16,256]{3,2,1,0:T(8,128)S(1)}, f32[1,1,16,256]{3,2,1,0:T(8,128)S(1)}, u32[]{:S(2)}, u32[]{:S(2)}) collective-permute-start(f32[1,1,16,256]{3,2,1,0:T(8,128)S(1)} %get-tuple-element.696), channel_id=1, source_target_pairs={{32,0},{64,32},{96,64},{128,96},{160,128},{192,160},{224,192},{256... | collective-permute-start | bytes 49160 | tf_op jit(solution)/shard_map/ppermute | solution.py:20
  131.1 75.8 %collective-permute-start.1 = (f32[1,1,16,256]{3,2,1,0:T(8,128)S(1)}, f32[1,1,16,256]{3,2,1,0:T(8,128)S(1)}, u32[]{:S(2)}, u32[]{:S(2)}) collective-permute-start(f32[1,1,16,256]{3,2,1,0:T(8,128)S(1)} %get-tuple-element.697), channel_id=1, source_target_pairs={{0,32},{32,64},{64,96},{96,128},{128,160},{160,192},{192,224},{224... | collective-permute-start | bytes 49160 | tf_op jit(solution)/shard_map/ppermute | solution.py:18
  133.1 73.7 %collective-permute-start.4 = (f32[1,8,18,1]{3,2,1,0:T(8,128)S(1)}, f32[1,8,18,1]{3,2,1,0:T(8,128)S(1)}, u32[]{:S(2)}, u32[]{:S(2)}) collective-permute-start(f32[1,8,18,1]{3,2,1,0:T(8,128)S(1)} %get-tuple-element.650), channel_id=1, source_target_pairs={{1,0},{3,2},{5,4},{7,6},{9,8},{11,10},{13,12},{15,14},{17,16},{19,... | collective-permute-start | bytes 1736 | tf_op jit(solution)/shard_map/ppermute | solution.py:20
  244.8 91.2 %collective-permute-start.6 = (f32[1,1,16,256]{3,2,1,0:T(8,128)S(1)}, f32[1,1,16,256]{3,2,1,0:T(8,128)S(1)}, u32[]{:S(2)}, u32[]{:S(2)}) collective-permute-start(f32[1,1,16,256]{3,2,1,0:T(8,128)S(1)} %get-tuple-element.688), channel_id=1, source_target_pairs={{32,0},{64,32},{96,64},{128,96},{160,128},{192,160},{224,192},{256... | collective-permute-start | bytes 49160 | tf_op jit(solution)/shard_map/ppermute | solution.py:20
  260.3 75.7 %collective-permute-start.7 = (f32[1,1,16,256]{3,2,1,0:T(8,128)S(1)}, f32[1,1,16,256]{3,2,1,0:T(8,128)S(1)}, u32[]{:S(2)}, u32[]{:S(2)}) collective-permute-start(f32[1,1,16,256]{3,2,1,0:T(8,128)S(1)} %get-tuple-element.689), channel_id=1, source_target_pairs={{0,32},{32,64},{64,96},{96,128},{128,160},{160,192},{192,224},{224... | collective-permute-start | bytes 49160 | tf_op jit(solution)/shard_map/ppermute | solution.py:18
  262.2 73.7 %collective-permute-start.10 = (f32[1,8,18,1]{3,2,1,0:T(8,128)S(1)}, f32[1,8,18,1]{3,2,1,0:T(8,128)S(1)}, u32[]{:S(2)}, u32[]{:S(2)}) collective-permute-start(f32[1,8,18,1]{3,2,1,0:T(8,128)S(1)} %get-tuple-element.646), channel_id=1, source_target_pairs={{1,0},{3,2},{5,4},{7,6},{9,8},{11,10},{13,12},{15,14},{17,16},{19,... | collective-permute-start | bytes 1736 | tf_op jit(solution)/shard_map/ppermute | solution.py:20
  373.9 91.2 %collective-permute-start.12 = (f32[1,1,16,256]{3,2,1,0:T(8,128)S(1)}, f32[1,1,16,256]{3,2,1,0:T(8,128)S(1)}, u32[]{:S(2)}, u32[]{:S(2)}) collective-permute-start(f32[1,1,16,256]{3,2,1,0:T(8,128)S(1)} %get-tuple-element.680), channel_id=1, source_target_pairs={{32,0},{64,32},{96,64},{128,96},{160,128},{192,160},{224,192},{256... | collective-permute-start | bytes 49160 | tf_op jit(solution)/shard_map/ppermute | solution.py:20
  389.4 75.7 %collective-permute-start.13 = (f32[1,1,16,256]{3,2,1,0:T(8,128)S(1)}, f32[1,1,16,256]{3,2,1,0:T(8,128)S(1)}, u32[]{:S(2)}, u32[]{:S(2)}) collective-permute-start(f32[1,1,16,256]{3,2,1,0:T(8,128)S(1)} %get-tuple-element.681), channel_id=1, source_target_pairs={{0,32},{32,64},{64,96},{96,128},{128,160},{160,192},{192,224},{224... | collective-permute-start | bytes 49160 | tf_op jit(solution)/shard_map/ppermute | solution.py:18
  391.3 73.7 %collective-permute-start.16 = (f32[1,8,18,1]{3,2,1,0:T(8,128)S(1)}, f32[1,8,18,1]{3,2,1,0:T(8,128)S(1)}, u32[]{:S(2)}, u32[]{:S(2)}) collective-permute-start(f32[1,8,18,1]{3,2,1,0:T(8,128)S(1)} %get-tuple-element.642), channel_id=1, source_target_pairs={{1,0},{3,2},{5,4},{7,6},{9,8},{11,10},{13,12},{15,14},{17,16},{19,... | collective-permute-start | bytes 1736 | tf_op jit(solution)/shard_map/ppermute | solution.py:20
  503.1 91.2 %collective-permute-start.18 = (f32[1,1,16,256]{3,2,1,0:T(8,128)S(1)}, f32[1,1,16,256]{3,2,1,0:T(8,128)S(1)}, u32[]{:S(2)}, u32[]{:S(2)}) collective-permute-start(f32[1,1,16,256]{3,2,1,0:T(8,128)S(1)} %get-tuple-element.672), channel_id=1, source_target_pairs={{32,0},{64,32},{96,64},{128,96},{160,128},{192,160},{224,192},{256... | collective-permute-start | bytes 49160 | tf_op jit(solution)/shard_map/ppermute | solution.py:20
  518.6 75.7 %collective-permute-start.19 = (f32[1,1,16,256]{3,2,1,0:T(8,128)S(1)}, f32[1,1,16,256]{3,2,1,0:T(8,128)S(1)}, u32[]{:S(2)}, u32[]{:S(2)}) collective-permute-start(f32[1,1,16,256]{3,2,1,0:T(8,128)S(1)} %get-tuple-element.673), channel_id=1, source_target_pairs={{0,32},{32,64},{64,96},{96,128},{128,160},{160,192},{192,224},{224... | collective-permute-start | bytes 49160 | tf_op jit(solution)/shard_map/ppermute | solution.py:18
  520.5 73.7 %collective-permute-start.22 = (f32[1,8,18,1]{3,2,1,0:T(8,128)S(1)}, f32[1,8,18,1]{3,2,1,0:T(8,128)S(1)}, u32[]{:S(2)}, u32[]{:S(2)}) collective-permute-start(f32[1,8,18,1]{3,2,1,0:T(8,128)S(1)} %get-tuple-element.638), channel_id=1, source_target_pairs={{1,0},{3,2},{5,4},{7,6},{9,8},{11,10},{13,12},{15,14},{17,16},{19,... | collective-permute-start | bytes 1736 | tf_op jit(solution)/shard_map/ppermute | solution.py:20
  632.2 91.2 %collective-permute-start.24 = (f32[1,1,16,256]{3,2,1,0:T(8,128)S(1)}, f32[1,1,16,256]{3,2,1,0:T(8,128)S(1)}, u32[]{:S(2)}, u32[]{:S(2)}) collective-permute-start(f32[1,1,16,256]{3,2,1,0:T(8,128)S(1)} %get-tuple-element.664), channel_id=1, source_target_pairs={{32,0},{64,32},{96,64},{128,96},{160,128},{192,160},{224,192},{256... | collective-permute-start | bytes 49160 | tf_op jit(solution)/shard_map/ppermute | solution.py:20
  647.7 75.7 %collective-permute-start.25 = (f32[1,1,16,256]{3,2,1,0:T(8,128)S(1)}, f32[1,1,16,256]{3,2,1,0:T(8,128)S(1)}, u32[]{:S(2)}, u32[]{:S(2)}) collective-permute-start(f32[1,1,16,256]{3,2,1,0:T(8,128)S(1)} %get-tuple-element.665), channel_id=1, source_target_pairs={{0,32},{32,64},{64,96},{96,128},{128,160},{160,192},{192,224},{224... | collective-permute-start | bytes 49160 | tf_op jit(solution)/shard_map/ppermute | solution.py:18
  649.6 73.7 %collective-permute-start.28 = (f32[1,8,18,1]{3,2,1,0:T(8,128)S(1)}, f32[1,8,18,1]{3,2,1,0:T(8,128)S(1)}, u32[]{:S(2)}, u32[]{:S(2)}) collective-permute-start(f32[1,8,18,1]{3,2,1,0:T(8,128)S(1)} %get-tuple-element.634), channel_id=1, source_target_pairs={{1,0},{3,2},{5,4},{7,6},{9,8},{11,10},{13,12},{15,14},{17,16},{19,... | collective-permute-start | bytes 1736 | tf_op jit(solution)/shard_map/ppermute | solution.py:20
  761.2 91.7 %collective-permute-start.30 = (f32[1,1,16,256]{3,2,1,0:T(8,128)S(1)}, f32[1,1,16,256]{3,2,1,0:T(8,128)S(1)}, u32[]{:S(2)}, u32[]{:S(2)}) collective-permute-start(f32[1,1,16,256]{3,2,1,0:T(8,128)S(1)} %get-tuple-element.656), channel_id=1, source_target_pairs={{32,0},{64,32},{96,64},{128,96},{160,128},{192,160},{224,192},{256... | collective-permute-start | bytes 49160 | tf_op jit(solution)/shard_map/ppermute | solution.py:20
  776.7 76.2 %collective-permute-start.31 = (f32[1,1,16,256]{3,2,1,0:T(8,128)S(1)}, f32[1,1,16,256]{3,2,1,0:T(8,128)S(1)}, u32[]{:S(2)}, u32[]{:S(2)}) collective-permute-start(f32[1,1,16,256]{3,2,1,0:T(8,128)S(1)} %get-tuple-element.657), channel_id=1, source_target_pairs={{0,32},{32,64},{64,96},{96,128},{128,160},{160,192},{192,224},{224... | collective-permute-start | bytes 49160 | tf_op jit(solution)/shard_map/ppermute | solution.py:18
  778.7 74.3 %collective-permute-start.34 = (f32[1,8,18,1]{3,2,1,0:T(8,128)S(1)}, f32[1,8,18,1]{3,2,1,0:T(8,128)S(1)}, u32[]{:S(2)}, u32[]{:S(2)}) collective-permute-start(f32[1,8,18,1]{3,2,1,0:T(8,128)S(1)} %get-tuple-element.630), channel_id=1, source_target_pairs={{1,0},{3,2},{5,4},{7,6},{9,8},{11,10},{13,12},{15,14},{17,16},{19,... | collective-permute-start | bytes 1736 | tf_op jit(solution)/shard_map/ppermute | solution.py:20
  781.7 71.2 %collective-permute-start.35 = (f32[1,8,18,1]{3,2,1,0:T(8,128)S(1)}, f32[1,8,18,1]{3,2,1,0:T(8,128)S(1)}, u32[]{:S(2)}, u32[]{:S(2)}) collective-permute-start(f32[1,8,18,1]{3,2,1,0:T(8,128)S(1)} %get-tuple-element.631), channel_id=1, source_target_pairs={{0,1},{2,3},{4,5},{6,7},{8,9},{10,11},{12,13},{14,15},{16,17},{18,... | collective-permute-start | bytes 1736 | tf_op jit(solution)/shard_map/ppermute | solution.py:18
  (53 other events, 1576.7 us)
where the time goes:
time: 963 us; the launch traced here: 961 us
  blocking collectives  573 us (60%)
  starting transfers between devices  266 us (28%)
  other arithmetic  77.4 us (8%)
  local copies, waits for them, and re-layouts  36.8 us (4%)
    psum x6, blocking collectives, on_device(): totals = lax.psum(partial_table, ('block', 'flame'))  407 us
    ppermute x36, starting transfers between devices, extended(): lax.ppermute(head, axis, [((i + 1) % count, i) for i in range(ends)])  182 us
    psum x1, blocking collectives, on_device(): lax.psum((jnp.sum(direct * direct), jnp.sum(adjoint * adjoint)), ('sector...  95.9 us
    ppermute x36, starting transfers between devices, extended(): lax.ppermute(tail, axis, [(i, (i + 1) % count) for i in range(ends)])  84.4 us
    all_gather x1, blocking collectives, flame_direct(): table = lax.all_gather(local_refs, ('block', 'flame'), axis=0, tiled=True)  69.6 us
    reduce_sum x56, other arithmetic, slab_lookup(): jnp.sum(jnp.where(owners_row[None, :] == ref_ids, table[:, None], 0.0), a...  41.6 us
    reduce_sum x48, other arithmetic, slab_collect(): jnp.sum(jnp.where(owners_row[None, :] == ref_ids, values_row[None, :], 0....  29.5 us
    dynamic_update_slice x56, local copies, waits for them, and re-layouts, lookup(): return lax.map(slab_lookup, owner_rows).reshape(planes, axial, radial)  21.9 us
  transfers between devices with their start and end apart: 72, of which 0 were waited for; matrix products, arithmetic and copies ran while one was open for 11% of the time, Pallas kernels for 0%

commit v1 on v0

v1 whole, which is shorter than its diff:
```python
import functools

import jax
import jax.numpy as jnp
from jax import lax
from jax.experimental import pallas as pl
from jax.experimental.pallas import tpu as pltpu
from jax.sharding import PartitionSpec as P

ITERS = 6
REF_DEV = 8
PAD = 8
LANES = 128
INTERPRET = False
BF = ("block", "flame")


def _call(kernel, out_shape, n_in, scratch=(), name=None):
    vmem = pl.BlockSpec(memory_space=pltpu.VMEM)
    single = not isinstance(out_shape, (tuple, list))
    return pl.pallas_call(
        kernel,
        out_shape=out_shape,
        in_specs=[pl.BlockSpec(memory_space=pltpu.SMEM)] + [vmem] * n_in,
        out_specs=vmem if single else [vmem] * len(out_shape),
        scratch_shapes=list(scratch),
        interpret=INTERPRET,
        name=name,
    )


def _lookup(table, owner):
    low = jnp.take_along_axis(table[0], owner & (LANES - 1), axis=1, mode="promise_in_bounds")
    high = jnp.take_along_axis(table[1], owner & (LANES - 1), axis=1, mode="promise_in_bounds")
    return jnp.where(owner < LANES, low, high)


def _table(total, row):
    return [jnp.broadcast_to(total[row + j : row + j + 1], (8, LANES)) for j in (0, 1)]


def _send_planes(core, refs, inner_ref, outer_ref, planes):
    inner = jnp.where(core == 0, planes - 1, 0)
    for i, ref in enumerate(refs):
        inner_ref[i] = ref[inner]
        outer_ref[i] = ref[planes - 1 - inner]


def init_kernel(scal_ref, ext_ref, inv_ref, own_ref, d_ref, a_ref, inner_ref, outer_ref, *, blocks):
    core, block = scal_ref[0], scal_ref[1]
    _, planes, rows, _ = ext_ref.shape
    for p in range(planes):
        for t in range(rows // 8):
            at = (p, slice(8 * t, 8 * t + 8))
            inv = 1.0 / (6.0 + ext_ref[(2,) + at])
            if t == 0:
                inv = jnp.where(block == 0, 0.0, inv)
            if t == rows // 8 - 1:
                inv = jnp.where(block == blocks - 1, 0.0, inv)
            inv_ref[at] = inv
            own_ref[at] = ext_ref[(4,) + at].astype(jnp.int32)
            d_ref[at] = ext_ref[(0,) + at] * inv
            a_ref[at] = ext_ref[(1,) + at] * inv
    _send_planes(core, (d_ref, a_ref), inner_ref, outer_ref, planes)


def step_kernel(scal_ref, recv_ref, inner_ref, outer_ref, d_ref, a_ref, ext_ref, inv_ref, own_ref,
                dn_ref, an_ref, inner_out, outer_out):
    core, block = scal_ref[0], scal_ref[1]
    planes, rows, width = d_ref.shape
    tiles = rows // 8
    total = jnp.sum(recv_ref[...], axis=0)
    table = _table(total, 0)
    sums = _table(total, 2)
    lane = lax.broadcasted_iota(jnp.int32, (8, LANES), 1)
    sub = lax.broadcasted_iota(jnp.int32, (8, LANES), 0)
    spot = (lane % 32 == 0) & (sub == 0) & (core == 0)
    first = lax.broadcasted_iota(jnp.int32, (8, width), 1) == 0
    last = lax.broadcasted_iota(jnp.int32, (8, width), 1) == width - 1

    def source(blk):
        tab = jnp.where(blk < 8, sums[0], sums[1])
        parts = []
        for j in range(width // LANES):
            at = jnp.bitwise_and(blk, 7) * 16 + 4 * j + lane // 32
            got = jnp.take_along_axis(tab, at & (LANES - 1), axis=1, mode="promise_in_bounds")
            parts.append(jnp.where(spot, got, 0.0))
        return jnp.concatenate(parts, axis=1)

    def near(ref, field, p, t):
        rng = slice(8 * t, 8 * t + 8)
        here = ref[p, rng]
        if p == 0:
            below = jnp.where(core == 0, outer_ref[field, rng], inner_ref[field, rng])
        else:
            below = ref[p - 1, rng]
        if p == planes - 1:
            above = jnp.where(core == 0, inner_ref[field, rng], outer_ref[field, rng])
        else:
            above = ref[p + 1, rng]
        if t == 0:
            back = pltpu.roll(here, 1, 0)
        else:
            back = ref[p, 8 * t - 1 : 8 * t + 7]
        if t == tiles - 1:
            front = pltpu.roll(here, 7, 0)
        else:
            front = ref[p, 8 * t + 1 : 8 * t + 9]
        left = jnp.where(first, 0.0, pltpu.roll(here, 1, 1))
        right = jnp.where(last, 0.0, pltpu.roll(here, width - 1, 1))
        return (below + above) + (back + front) + (left + right)

    for p in range(planes):
        for t in range(tiles):
            at = (p, slice(8 * t, 8 * t + 8))
            inv = inv_ref[at]
            own = own_ref[at]
            looked = jnp.concatenate(
                [_lookup(table, own[:, LANES * j : LANES * (j + 1)]) for j in range(width // LANES)],
                axis=1,
            )
            flame = ext_ref[(3,) + at] * looked
            dn_ref[at] = (ext_ref[(0,) + at] + near(d_ref, 0, p, t) + flame) * inv
            acc = ext_ref[(1,) + at] + near(a_ref, 1, p, t)
            if p == 0 and t == PAD // 8:
                acc = acc + source(block)
            if p == 0 and t == tiles - PAD // 8:
                acc = acc + source(block + 1)
            an_ref[at] = acc * inv
    _send_planes(core, (dn_ref, an_ref), inner_out, outer_out, planes)


def _write_refs(scal_ref, d_ref, out_ref):
    core, block = scal_ref[0], scal_ref[1]
    width = d_ref.shape[2]
    lane = lax.broadcasted_iota(jnp.int32, (8, LANES), 1)
    row = d_ref[0, PAD : PAD + 8]
    got = jnp.zeros((8, LANES), jnp.float32)
    for j in range(width // LANES):
        part = jnp.broadcast_to(row[0:1, LANES * j : LANES * (j + 1)], (8, LANES))
        pick = jnp.take_along_axis(part, (lane & 3) * 32, axis=1, mode="promise_in_bounds")
        got = jnp.where((lane & 15) // 4 == j, pick, got)
    for half in (0, 1):
        mine = (lane // 16 + 8 * half == block) & (core == 0)
        out_ref[:, half] = jnp.broadcast_to(
            jnp.where(mine, got, 0.0)[0:1], (out_ref.shape[0], LANES)
        )


def collect_kernel(scal_ref, d_ref, a_ref, ext_ref, own_ref, out_ref, *split_refs):
    planes, rows, width = d_ref.shape
    tiles = (rows - 2 * PAD) // 8
    _write_refs(scal_ref, d_ref, out_ref)
    for p in range(planes):
        for t in range(tiles):
            at = (p, slice(PAD + 8 * t, PAD + 8 * t + 8))
            y = ext_ref[(3,) + at] * a_ref[at]
            coarse = y.astype(jnp.bfloat16).astype(jnp.float32)
            fine = y - coarse
            upper = own_ref[at] >= LANES
            base = (p * tiles + t) * 64
            terms = (
                jnp.where(upper, 0.0, coarse),
                jnp.where(upper, 0.0, fine),
                jnp.where(upper, coarse, 0.0),
                jnp.where(upper, fine, 0.0),
            )
            for j in range(width // LANES):
                for k, term in enumerate(terms):
                    split_refs[j][pl.ds(base + k, 8, stride=8), :] = term[:, LANES * j : LANES * (j + 1)]
    ids = lax.broadcasted_iota(jnp.int32, (16, width), 0).astype(jnp.float32)
    one = jnp.ones((16, width), jnp.bfloat16)
    zero = jnp.zeros((16, width), jnp.bfloat16)
    groups = [(ids + 16.0 * g).astype(jnp.bfloat16) for g in range(LANES // 16)]
    acc = jnp.zeros((8, LANES), jnp.float32)
    for p in range(planes):
        for t in range(tiles):
            low = (own_ref[p, PAD + 8 * t : PAD + 8 * t + 8] & (LANES - 1)).astype(jnp.float32)
            for x in range(8):
                line = jnp.broadcast_to(low[x : x + 1], (16, width)).astype(jnp.bfloat16)
                hot = jnp.concatenate([jnp.where(line == g, one, zero) for g in groups], axis=0)
                base = ((p * tiles + t) * 8 + x) * 8
                vals = jnp.concatenate(
                    [ref[base : base + 8, :] for ref in split_refs], axis=1
                ).astype(jnp.bfloat16)
                acc = acc + lax.dot_general(
                    vals, hot, (((1,), (1,)), ((), ())), preferred_element_type=jnp.float32
                )
    count = out_ref.shape[0]
    out_ref[:, 2] = jnp.broadcast_to(acc[0:1] + acc[1:2], (count, LANES))
    out_ref[:, 3] = jnp.broadcast_to(acc[2:3] + acc[3:4], (count, LANES))


def norm_kernel(scal_ref, d_ref, a_ref, out_ref):
    planes, rows, width = d_ref.shape
    _write_refs(scal_ref, d_ref, out_ref)
    for i, ref in enumerate((d_ref, a_ref)):
        acc = jnp.zeros((8, width), jnp.float32)
        for p in range(planes):
            for t in range((rows - 2 * PAD) // 8):
                v = ref[p, PAD + 8 * t : PAD + 8 * t + 8]
                acc = acc + v * v
        acc = sum(acc[:, LANES * j : LANES * (j + 1)] for j in range(width // LANES))
        out_ref[:, 2 + i] = jnp.broadcast_to(
            jnp.sum(acc, axis=0, keepdims=True), (out_ref.shape[0], LANES)
        )


def fields_kernel(scal_ref, recv_ref, d_ref, a_ref, ext_ref, own_ref, out_ref, sums_ref):
    planes, rows, width = d_ref.shape
    total = jnp.sum(recv_ref[...], axis=0)
    table = _table(total, 0)
    sums_ref[...] = jnp.broadcast_to(total[None, 2:4], sums_ref.shape)
    for p in range(planes):
        for t in range((rows - 2 * PAD) // 8):
            at = (p, slice(PAD + 8 * t, PAD + 8 * t + 8))
            to = (p, slice(8 * t, 8 * t + 8))
            own = own_ref[at]
            looked = jnp.concatenate(
                [_lookup(table, own[:, LANES * j : LANES * (j + 1)]) for j in range(width // LANES)],
                axis=1,
            )
            adjoint = a_ref[at]
            out_ref[(0,) + to] = adjoint * d_ref[at]
            out_ref[(1,) + to] = adjoint * (ext_ref[(3,) + at] * looked)


def on_device(rhs_direct, rhs_adjoint, diag_shift, flame_gain, ref_owner):
    planes, axial, radial = rhs_direct.shape
    sectors, blocks = lax.axis_size("sector"), lax.axis_size("block")
    core, block = lax.axis_index("flame"), lax.axis_index("block")
    scal = jnp.stack([core, block]).astype(jnp.int32)
    half, width, rows = planes // 2, 2 * radial, axial + 2 * PAD
    f32 = jnp.float32
    swap = [(0, 1), (1, 0)]

    stack = jnp.stack([rhs_direct, rhs_adjoint, diag_shift, flame_gain, ref_owner.astype(f32)])
    keep = lax.dynamic_slice_in_dim(stack, core * half, half, axis=1)
    give = lax.dynamic_slice_in_dim(stack, (1 - core) * half, half, axis=1)
    got = lax.ppermute(give, "flame", swap)
    full = jnp.where(
        core == 0, jnp.concatenate([keep, got], axis=3), jnp.concatenate([got, keep], axis=3)
    )
    before = lax.ppermute(full[:, :, axial - PAD :], "block", [(i, i + 1) for i in range(blocks - 1)])
    after = lax.ppermute(full[:, :, :PAD], "block", [(i + 1, i) for i in range(blocks - 1)])
    ext = jnp.concatenate([before, full, after], axis=2)

    field = jax.ShapeDtypeStruct((half, rows, width), f32)
    owners = jax.ShapeDtypeStruct((half, rows, width), jnp.int32)
    plane = jax.ShapeDtypeStruct((2, rows, width), f32)
    peers = 2 * blocks
    message = jax.ShapeDtypeStruct((peers, 4, LANES), f32)
    ring = [(2 * s, (2 * s - 1) % (2 * sectors)) for s in range(sectors)]
    ring += [(2 * s + 1, (2 * s + 2) % (2 * sectors)) for s in range(sectors)]

    inverse, owner, direct, adjoint, inner, outer = _call(
        functools.partial(init_kernel, blocks=blocks),
        (field, owners, field, field, plane, plane), 1, name="init",
    )(scal, ext)
    step = _call(step_kernel, (field, field, plane, plane), 8, name="step")
    collect = _call(
        collect_kernel, message, 4,
        [pltpu.VMEM((half * axial * 8, LANES), f32)] * (width // LANES), name="collect",
    )
    for _ in range(ITERS):
        outer_in = lax.ppermute(outer, ("sector", "flame"), ring)
        inner_in = lax.ppermute(inner, "flame", swap)
        sent = collect(scal, direct, adjoint, ext, owner)
        recv = lax.all_to_all(sent, BF, 0, 0, tiled=True)
        direct, adjoint, inner, outer = step(
            scal, recv, inner_in, outer_in, direct, adjoint, ext, inverse, owner
        )

    sent = _call(norm_kernel, message, 2, name="norm")(scal, direct, adjoint)
    recv = lax.all_to_all(sent, BF, 0, 0, tiled=True)
    fields, sums = _call(
        fields_kernel,
        (
            jax.ShapeDtypeStruct((2, half, axial, width), f32),
            jax.ShapeDtypeStruct((sectors, 2, LANES), f32),
        ),
        5, name="fields",
    )(scal, recv, direct, adjoint, ext, owner)
    keep = lax.dynamic_slice_in_dim(fields, core * radial, radial, axis=3)
    give = lax.dynamic_slice_in_dim(fields, (1 - core) * radial, radial, axis=3)
    got = lax.ppermute(give, "flame", swap)
    squares = lax.all_to_all(sums, "sector", 0, 0, tiled=True)
    squares = jnp.sum(squares, axis=(0, 2))
    cells = planes * axial * radial * sectors * blocks * 2
    scale = lax.rsqrt(squares[0] / cells * (squares[1] / cells) + 1e-12)
    low = jnp.where(core == 0, keep, got)
    high = jnp.where(core == 0, got, keep)
    out = jnp.concatenate([low, high], axis=1) * scale
    return out[0], out[1]


def solution(mesh):
    spec = P("sector", "block", "flame")
    return jax.shard_map(
        on_device,
        mesh=mesh,
        in_specs=(spec,) * 5,
        out_specs=(spec, spec),
        check_vma=False,
    )
```

time: 963 us -> 252 us (0.26)
  blocking collectives: 573 us -> 82.2 us
  starting transfers between devices: 266 us -> 69.2 us
  other arithmetic: 77.4 us -> 3.93 us
  Pallas kernels: 0 us -> 53.4 us
  waiting for transfers between devices: 0.19 us -> 25.8 us
  local copies, waits for them, and re-layouts: 36.8 us -> 13.8 us
    psum x7 -> x0, blocking collectives: 503 us -> none  [the longest x6 407 us: on_device(): totals = lax.psum(partial_table, ('block', 'flame'))]
    ppermute x72 -> x16, starting transfers between devices: 266 us -> 56.4 us  [the longest x6 27.9 us: on_device(): outer_in = lax.ppermute(outer, ('sector', 'flame'), ring)]
    all_to_all x0 -> x6, blocking collectives: none -> 82.2 us  [on_device(): recv = lax.all_to_all(sent, BF, 0, 0, tiled=True)]
    reduce_sum x112 -> x1, other arithmetic: 72.9 us -> 0.13 us  [on_device(): squares = jnp.sum(squares, axis=(0, 2))]
    all_gather x1 -> x0, blocking collectives: 69.6 us -> none  [flame_direct(): table = lax.all_gather(local_refs, ('block', 'flame'), axis=0, tiled=True)]
    pallas_call x0 -> x15, Pallas kernels: none -> 53.4 us  [the longest x6 26.7 us: on_device(): sent = collect(scal, direct, adjoint, ext, owner)]
    dynamic_update_slice x104 -> x0, local copies, waits for them, and re-layouts: 23.6 us -> none  [the longest x56 21.9 us: lookup(): return lax.map(slab_lookup, owner_rows).reshape(planes, axial, radial)]
    all_to_all x0 -> x2, waiting for transfers between devices: none -> 15.7 us  [the longest x1 7.84 us: on_device(): recv = lax.all_to_all(sent, BF, 0, 0, tiled=True)]
  transfers between devices with their start and end apart: 72 -> 18, of which waited for: 0 -> 5; matrix products, arithmetic and copies ran while one was open for 11% -> 1% of each run, Pallas kernels for 0% -> 11%
where the time goes in v1:
time: 252 us; the launch traced here: 251 us
  blocking collectives  82.2 us (33%)
  starting transfers between devices  69.2 us (27%)
  Pallas kernels  53.4 us (21%)
  waiting for transfers between devices  25.8 us (10%)
  local copies, waits for them, and re-layouts  13.8 us (5%)
  other arithmetic  3.93 us (2%)
    all_to_all x6, blocking collectives, on_device(): recv = lax.all_to_all(sent, BF, 0, 0, tiled=True)  82.2 us
    ppermute x6, starting transfers between devices, on_device(): outer_in = lax.ppermute(outer, ('sector', 'flame'), ring)  27.9 us
    pallas_call x6, Pallas kernels, on_device(): sent = collect(scal, direct, adjoint, ext, owner)  26.7 us
    pallas_call x6, Pallas kernels, on_device(): step(scal, recv, inner_in, outer_in, direct, adjoint, ext, inverse, owner)  20.1 us
    ppermute x6, starting transfers between devices, on_device(): inner_in = lax.ppermute(inner, 'flame', swap)  14.6 us
    unnamed x30, local copies, waits for them, and re-layouts  11.5 us
    ppermute x2, starting transfers between devices, on_device(): got = lax.ppermute(give, 'flame', swap)  11.3 us
    all_to_all x1, starting transfers between devices, on_device(): squares = lax.all_to_all(sums, 'sector', 0, 0, tiled=True)  8.93 us
  transfers between devices with their start and end apart: 18, of which 5 were waited for; matrix products, arithmetic and copies ran while one was open for 1% of the time, Pallas kernels for 11%

profile of v1, /device:TPU:1, one launch (start us, length us, event | category | flops | bytes accessed | tf_op | source)
XLA Modules:
  0.0 250.7 jit_solution(14512897567987122116)
XLA Ops:
  5.3 8.7 %collective-permute-start = (f32[5,4,16,256]{3,2,1,0:T(8,128)S(1)}, f32[5,4,16,256]{3,2,1,0:T(8,128)S(1)}, u32[]{:S(2)}, u32[]{:S(2)}) collective-permute-start(f32[5,4,16,256]{3,2,1,0:T(8,128)S(1)} %get-tuple-element.65), channel_id=1, source_target_pairs={{0,1},{1,0},{2,3},{3,2},{4,5},{5,4},{6,7},{7,6},{8,9},{9,8},{10,11... | collective-permute-start | bytes 983048 | tf_op jit(solution)/shard_map/ppermute | solution.py:240
  18.6 5.0 %collective-permute-done.1 = f32[5,4,8,512]{3,2,1,0:T(8,128)S(1)} collective-permute-done((f32[5,4,8,512]{3,2,1,0:T(8,128)S(1)}, f32[5,4,8,512]{3,2,1,0:T(8,128)S(1)}, u32[]{:S(2)}, u32[]{:S(2)}) %collective-permute-start.1) | collective-permute-done | bytes 327712 | tf_op jit(solution)/shard_map/ppermute | solution.py:244
  23.7 3.9 %collective-permute-done.2 = f32[5,4,8,512]{3,2,1,0:T(8,128)S(1)} collective-permute-done((f32[5,4,8,512]{3,2,1,0:T(8,128)S(1)}, f32[5,4,8,512]{3,2,1,0:T(8,128)S(1)}, u32[]{:S(2)}, u32[]{:S(2)}) %collective-permute-start.2) | collective-permute-done | bytes 327712 | tf_op jit(solution)/shard_map/ppermute | solution.py:245
  34.3 7.0 %collective-permute-start.4 = (f32[2,32,512]{2,1,0:T(8,128)}, f32[2,32,512]{2,1,0:T(8,128)S(1)}, u32[]{:S(2)}, u32[]{:S(2)}) collective-permute-start(f32[2,32,512]{2,1,0:T(8,128)} %get-tuple-element.36), channel_id=1, source_target_pairs={{0,481},{32,1},{64,33},{96,65},{128,97},{160,129},{192,161},{224,1... | collective-permute-start | bytes 393224 | tf_op jit(solution)/shard_map/ppermute | solution.py:266
  41.3 4.4 %collect.6 = f32[32,4,128]{2,1,0:T(4,128)} custom-call(s32[2]{0:T(128)} %pad_add_fusion.scal_ref, f32[4,32,512]{2,1,0:T(8,128)} %get-tuple-element.32.d_ref, f32[4,32,512]{2,1,0:T(8,128)} %get-tuple-element.33.a_ref, f32[5,4,32,512]{3,2,1,0:T(8,128)} %pad_maximum_fusion.ext_ref, s32[4,32,512]{2,1,0:T(8,128)} %get-tuple-element.34.own_ref), custom_call_target="tpu_custom_call" | custom-call | tf_op jit(solution)/shard_map/collect/pallas_call | solution.py:268
  45.7 19.2 %all_to_all.40.recv_ref = f32[32,4,128]{2,1,0:T(4,128)} all-to-all(f32[32,4,128]{2,1,0:T(4,128)} %collect.6), channel_id=1, replica_groups=mesh['sector'=16,'block'=16,'flame'=2] {'block','flame'}, dimensions={0} | all-to-all | bytes 131072 | tf_op jit(solution)/shard_map/all_to_all | solution.py:269
  73.2 4.4 %collect.7 = f32[32,4,128]{2,1,0:T(4,128)} custom-call(s32[2]{0:T(128)} %pad_add_fusion.scal_ref, f32[4,32,512]{2,1,0:T(8,128)} %get-tuple-element.38.d_ref, f32[4,32,512]{2,1,0:T(8,128)} %get-tuple-element.39.a_ref, f32[5,4,32,512]{3,2,1,0:T(8,128)} %pad_maximum_fusion.ext_ref, s32[4,32,512]{2,1,0:T(8,128)} %get-tuple-element.34.own_ref), custom_call_target="tpu_custom_call" | custom-call | tf_op jit(solution)/shard_map/collect/pallas_call | solution.py:268
  77.7 12.1 %all_to_all.41.recv_ref = f32[32,4,128]{2,1,0:T(4,128)} all-to-all(f32[32,4,128]{2,1,0:T(4,128)} %collect.7), channel_id=1, replica_groups=mesh['sector'=16,'block'=16,'flame'=2] {'block','flame'}, dimensions={0} | all-to-all | bytes 131072 | tf_op jit(solution)/shard_map/all_to_all | solution.py:269
  91.1 3.4 %step.7 = (f32[4,32,512]{2,1,0:T(8,128)}, f32[4,32,512]{2,1,0:T(8,128)}, f32[2,32,512]{2,1,0:T(8,128)}, f32[2,32,512]{2,1,0:T(8,128)}) custom-call(s32[2]{0:T(128)} %pad_add_fusion.scal_ref, f32[32,4,128]{2,1,0:T(4,128)} %all_to_all.41.recv_ref, f32[2,32,512]{2,1,0:T(8,128)} %copy-done.3, f32[2,32,512]{2,1,0:T(8,128)} %copy-done.9, ...), custom_call_target="tpu_custom_call" | custom-call | tf_op jit(solution)/shard_map/step/pallas_call | solution.py:270
  96.8 7.5 %collective-permute-start.8 = (f32[2,32,512]{2,1,0:T(8,128)}, f32[2,32,512]{2,1,0:T(8,128)S(1)}, u32[]{:S(2)}, u32[]{:S(2)}) collective-permute-start(f32[2,32,512]{2,1,0:T(8,128)} %get-tuple-element.45), channel_id=1, source_target_pairs={{0,481},{32,1},{64,33},{96,65},{128,97},{160,129},{192,161},{224,1... | collective-permute-start | bytes 393224 | tf_op jit(solution)/shard_map/ppermute | solution.py:266
  104.4 4.4 %collect.8 = f32[32,4,128]{2,1,0:T(4,128)} custom-call(s32[2]{0:T(128)} %pad_add_fusion.scal_ref, f32[4,32,512]{2,1,0:T(8,128)} %get-tuple-element.42.d_ref, f32[4,32,512]{2,1,0:T(8,128)} %get-tuple-element.43.a_ref, f32[5,4,32,512]{3,2,1,0:T(8,128)} %pad_maximum_fusion.ext_ref, s32[4,32,512]{2,1,0:T(8,128)} %get-tuple-element.34.own_ref), custom_call_target="tpu_custom_call" | custom-call | tf_op jit(solution)/shard_map/collect/pallas_call | solution.py:268
  108.8 13.2 %all_to_all.42.recv_ref = f32[32,4,128]{2,1,0:T(4,128)} all-to-all(f32[32,4,128]{2,1,0:T(4,128)} %collect.8), channel_id=1, replica_groups=mesh['sector'=16,'block'=16,'flame'=2] {'block','flame'}, dimensions={0} | all-to-all | bytes 131072 | tf_op jit(solution)/shard_map/all_to_all | solution.py:269
  130.9 4.4 %collect.9 = f32[32,4,128]{2,1,0:T(4,128)} custom-call(s32[2]{0:T(128)} %pad_add_fusion.scal_ref, f32[4,32,512]{2,1,0:T(8,128)} %get-tuple-element.46.d_ref, f32[4,32,512]{2,1,0:T(8,128)} %get-tuple-element.47.a_ref, f32[5,4,32,512]{3,2,1,0:T(8,128)} %pad_maximum_fusion.ext_ref, s32[4,32,512]{2,1,0:T(8,128)} %get-tuple-element.34.own_ref), custom_call_target="tpu_custom_call" | custom-call | tf_op jit(solution)/shard_map/collect/pallas_call | solution.py:268
  135.4 12.1 %all_to_all.43.recv_ref = f32[32,4,128]{2,1,0:T(4,128)} all-to-all(f32[32,4,128]{2,1,0:T(4,128)} %collect.9), channel_id=1, replica_groups=mesh['sector'=16,'block'=16,'flame'=2] {'block','flame'}, dimensions={0} | all-to-all | bytes 131072 | tf_op jit(solution)/shard_map/all_to_all | solution.py:269
  148.8 3.4 %step.9 = (f32[4,32,512]{2,1,0:T(8,128)}, f32[4,32,512]{2,1,0:T(8,128)}, f32[2,32,512]{2,1,0:T(8,128)}, f32[2,32,512]{2,1,0:T(8,128)}) custom-call(s32[2]{0:T(128)} %pad_add_fusion.scal_ref, f32[32,4,128]{2,1,0:T(4,128)} %all_to_all.43.recv_ref, f32[2,32,512]{2,1,0:T(8,128)} %copy-done.5, f32[2,32,512]{2,1,0:T(8,128)} %copy-done.11, ...), custom_call_target="tpu_custom_call" | custom-call | tf_op jit(solution)/shard_map/step/pallas_call | solution.py:270
  154.5 7.5 %collective-permute-start.12 = (f32[2,32,512]{2,1,0:T(8,128)}, f32[2,32,512]{2,1,0:T(8,128)S(1)}, u32[]{:S(2)}, u32[]{:S(2)}) collective-permute-start(f32[2,32,512]{2,1,0:T(8,128)} %get-tuple-element.53), channel_id=1, source_target_pairs={{0,481},{32,1},{64,33},{96,65},{128,97},{160,129},{192,161},{224,1... | collective-permute-start | bytes 393224 | tf_op jit(solution)/shard_map/ppermute | solution.py:266
  162.0 4.4 %collect.10 = f32[32,4,128]{2,1,0:T(4,128)} custom-call(s32[2]{0:T(128)} %pad_add_fusion.scal_ref, f32[4,32,512]{2,1,0:T(8,128)} %get-tuple-element.50.d_ref, f32[4,32,512]{2,1,0:T(8,128)} %get-tuple-element.51.a_ref, f32[5,4,32,512]{3,2,1,0:T(8,128)} %pad_maximum_fusion.ext_ref, s32[4,32,512]{2,1,0:T(8,128)} %get-tuple-element.34.own_ref), custom_call_target="tpu_custom_call" | custom-call | tf_op jit(solution)/shard_map/collect/pallas_call | solution.py:268
  166.5 13.4 %all_to_all.44.recv_ref = f32[32,4,128]{2,1,0:T(4,128)} all-to-all(f32[32,4,128]{2,1,0:T(4,128)} %collect.10), channel_id=1, replica_groups=mesh['sector'=16,'block'=16,'flame'=2] {'block','flame'}, dimensions={0} | all-to-all | bytes 131072 | tf_op jit(solution)/shard_map/all_to_all | solution.py:269
  188.8 4.4 %collect.11 = f32[32,4,128]{2,1,0:T(4,128)} custom-call(s32[2]{0:T(128)} %pad_add_fusion.scal_ref, f32[4,32,512]{2,1,0:T(8,128)} %get-tuple-element.54.d_ref, f32[4,32,512]{2,1,0:T(8,128)} %get-tuple-element.55.a_ref, f32[5,4,32,512]{3,2,1,0:T(8,128)} %pad_maximum_fusion.ext_ref, s32[4,32,512]{2,1,0:T(8,128)} %get-tuple-element.34.own_ref), custom_call_target="tpu_custom_call" | custom-call | tf_op jit(solution)/shard_map/collect/pallas_call | solution.py:268
  193.2 12.1 %all_to_all.45.recv_ref = f32[32,4,128]{2,1,0:T(4,128)} all-to-all(f32[32,4,128]{2,1,0:T(4,128)} %collect.11), channel_id=1, replica_groups=mesh['sector'=16,'block'=16,'flame'=2] {'block','flame'}, dimensions={0} | all-to-all | bytes 131072 | tf_op jit(solution)/shard_map/all_to_all | solution.py:269
  211.8 3.9 %all-to-all-start.6 = ((f32[32,4,128]{2,1,0:T(4,128)}), f32[32,4,128]{2,1,0:T(4,128)S(1)}, u32[]{:S(2)}, u32[]{:S(2)}) async-start(f32[32,4,128]{2,1,0:T(4,128)} %norm.1), calls=%async_computation.6 | async-start | bytes 131072 | tf_op jit(solution)/shard_map/all_to_all | solution.py:275
  215.7 7.8 %all-to-all-done.6.recv_ref = f32[32,4,128]{2,1,0:T(4,128)S(1)} async-done(((f32[32,4,128]{2,1,0:T(4,128)}), f32[32,4,128]{2,1,0:T(4,128)S(1)}, u32[]{:S(2)}, u32[]{:S(2)}) %all-to-all-start.6) | async-done | bytes 65568 | tf_op jit(solution)/shard_map/all_to_all | solution.py:275
  226.7 8.9 %all-to-all-start.7 = ((f32[16,2,128]{2,1,0:T(2,128)}), f32[16,2,128]{2,1,0:T(2,128)S(1)}, u32[]{:S(2)}, u32[]{:S(2)}) async-start(f32[16,2,128]{2,1,0:T(2,128)} %get-tuple-element.61), calls=%async_computation.7 | async-start | bytes 32768 | tf_op jit(solution)/shard_map/all_to_all | solution.py:287
  239.1 7.8 %all-to-all-done.7 = f32[16,2,128]{2,1,0:T(2,128)S(1)} async-done(((f32[16,2,128]{2,1,0:T(2,128)}), f32[16,2,128]{2,1,0:T(2,128)S(1)}, u32[]{:S(2)}, u32[]{:S(2)}) %all-to-all-start.7) | async-done | bytes 16416 | tf_op jit(solution)/shard_map/all_to_all | solution.py:287
  (75 shorter events, 64.6 us)
Async XLA Ops:
  5.3 10.0 %collective-permute-start = (f32[5,4,16,256]{3,2,1,0:T(8,128)S(1)}, f32[5,4,16,256]{3,2,1,0:T(8,128)S(1)}, u32[]{:S(2)}, u32[]{:S(2)}) collective-permute-start(f32[5,4,16,256]{3,2,1,0:T(8,128)S(1)} %get-tuple-element.65), channel_id=1, source_target_pairs={{0,1},{1,0},{2,3},{3,2},{4,5},{5,4},{6,7},{7,6},{8,9},{9,8},{10,11... | collective-permute-start | bytes 983048 | tf_op jit(solution)/shard_map/ppermute | solution.py:240
  15.4 8.3 %collective-permute-start.1 = (f32[5,4,8,512]{3,2,1,0:T(8,128)S(1)}, f32[5,4,8,512]{3,2,1,0:T(8,128)S(1)}, u32[]{:S(2)}, u32[]{:S(2)}) collective-permute-start(f32[5,4,8,512]{3,2,1,0:T(8,128)S(1)} %get-tuple-element.62), channel_id=1, source_target_pairs={{0,2},{2,4},{4,6},{6,8},{8,10},{10,12},{12,14},{14,16},{16,18},{18... | collective-permute-start | bytes 983048 | tf_op jit(solution)/shard_map/ppermute | solution.py:244
  16.7 10.8 %collective-permute-start.2 = (f32[5,4,8,512]{3,2,1,0:T(8,128)S(1)}, f32[5,4,8,512]{3,2,1,0:T(8,128)S(1)}, u32[]{:S(2)}, u32[]{:S(2)}) collective-permute-start(f32[5,4,8,512]{3,2,1,0:T(8,128)S(1)} %get-tuple-element.63), channel_id=1, source_target_pairs={{2,0},{4,2},{6,4},{8,6},{10,8},{12,10},{14,12},{16,14},{18,16},{20... | collective-permute-start | bytes 983048 | tf_op jit(solution)/shard_map/ppermute | solution.py:245
  31.1 33.8 %collective-permute-start.3 = (f32[2,32,512]{2,1,0:T(8,128)}, f32[2,32,512]{2,1,0:T(8,128)S(1)}, u32[]{:S(2)}, u32[]{:S(2)}) collective-permute-start(f32[2,32,512]{2,1,0:T(8,128)} %get-tuple-element.35), channel_id=1, source_target_pairs={{0,1},{1,0},{2,3},{3,2},{4,5},{5,4},{6,7},{7,6},{8,9},{9,8},{10,11... | collective-permute-start | bytes 393224 | tf_op jit(solution)/shard_map/ppermute | solution.py:267
  34.3 30.7 %collective-permute-start.4 = (f32[2,32,512]{2,1,0:T(8,128)}, f32[2,32,512]{2,1,0:T(8,128)S(1)}, u32[]{:S(2)}, u32[]{:S(2)}) collective-permute-start(f32[2,32,512]{2,1,0:T(8,128)} %get-tuple-element.36), channel_id=1, source_target_pairs={{0,481},{32,1},{64,33},{96,65},{128,97},{160,129},{192,161},{224,1... | collective-permute-start | bytes 393224 | tf_op jit(solution)/shard_map/ppermute | solution.py:266
  65.0 0.7 copy-start.2
  65.0 0.7 copy-start.8
  69.0 20.8 %collective-permute-start.5 = (f32[2,32,512]{2,1,0:T(8,128)}, f32[2,32,512]{2,1,0:T(8,128)S(1)}, u32[]{:S(2)}, u32[]{:S(2)}) collective-permute-start(f32[2,32,512]{2,1,0:T(8,128)} %get-tuple-element.40), channel_id=1, source_target_pairs={{0,1},{1,0},{2,3},{3,2},{4,5},{5,4},{6,7},{7,6},{8,9},{9,8},{10,11... | collective-permute-start | bytes 393224 | tf_op jit(solution)/shard_map/ppermute | solution.py:267
  71.3 18.5 %collective-permute-start.6 = (f32[2,32,512]{2,1,0:T(8,128)}, f32[2,32,512]{2,1,0:T(8,128)S(1)}, u32[]{:S(2)}, u32[]{:S(2)}) collective-permute-start(f32[2,32,512]{2,1,0:T(8,128)} %get-tuple-element.41), channel_id=1, source_target_pairs={{0,481},{32,1},{64,33},{96,65},{128,97},{160,129},{192,161},{224,1... | collective-permute-start | bytes 393224 | tf_op jit(solution)/shard_map/ppermute | solution.py:266
  89.8 0.7 copy-start.3
  94.5 27.5 %collective-permute-start.7 = (f32[2,32,512]{2,1,0:T(8,128)}, f32[2,32,512]{2,1,0:T(8,128)S(1)}, u32[]{:S(2)}, u32[]{:S(2)}) collective-permute-start(f32[2,32,512]{2,1,0:T(8,128)} %get-tuple-element.44), channel_id=1, source_target_pairs={{0,1},{1,0},{2,3},{3,2},{4,5},{5,4},{6,7},{7,6},{8,9},{9,8},{10,11... | collective-permute-start | bytes 393224 | tf_op jit(solution)/shard_map/ppermute | solution.py:267
  96.8 25.2 %collective-permute-start.8 = (f32[2,32,512]{2,1,0:T(8,128)}, f32[2,32,512]{2,1,0:T(8,128)S(1)}, u32[]{:S(2)}, u32[]{:S(2)}) collective-permute-start(f32[2,32,512]{2,1,0:T(8,128)} %get-tuple-element.45), channel_id=1, source_target_pairs={{0,481},{32,1},{64,33},{96,65},{128,97},{160,129},{192,161},{224,1... | collective-permute-start | bytes 393224 | tf_op jit(solution)/shard_map/ppermute | solution.py:266
  122.0 0.7 copy-start.4
  126.7 20.8 %collective-permute-start.9 = (f32[2,32,512]{2,1,0:T(8,128)}, f32[2,32,512]{2,1,0:T(8,128)S(1)}, u32[]{:S(2)}, u32[]{:S(2)}) collective-permute-start(f32[2,32,512]{2,1,0:T(8,128)} %get-tuple-element.48), channel_id=1, source_target_pairs={{0,1},{1,0},{2,3},{3,2},{4,5},{5,4},{6,7},{7,6},{8,9},{9,8},{10,11... | collective-permute-start | bytes 393224 | tf_op jit(solution)/shard_map/ppermute | solution.py:267
  129.0 18.5 %collective-permute-start.10 = (f32[2,32,512]{2,1,0:T(8,128)}, f32[2,32,512]{2,1,0:T(8,128)S(1)}, u32[]{:S(2)}, u32[]{:S(2)}) collective-permute-start(f32[2,32,512]{2,1,0:T(8,128)} %get-tuple-element.49), channel_id=1, source_target_pairs={{0,481},{32,1},{64,33},{96,65},{128,97},{160,129},{192,161},{224,1... | collective-permute-start | bytes 393224 | tf_op jit(solution)/shard_map/ppermute | solution.py:266
  147.5 0.7 copy-start.5
  152.2 27.7 %collective-permute-start.11 = (f32[2,32,512]{2,1,0:T(8,128)}, f32[2,32,512]{2,1,0:T(8,128)S(1)}, u32[]{:S(2)}, u32[]{:S(2)}) collective-permute-start(f32[2,32,512]{2,1,0:T(8,128)} %get-tuple-element.52), channel_id=1, source_target_pairs={{0,1},{1,0},{2,3},{3,2},{4,5},{5,4},{6,7},{7,6},{8,9},{9,8},{10,11... | collective-permute-start | bytes 393224 | tf_op jit(solution)/shard_map/ppermute | solution.py:267
  154.5 25.4 %collective-permute-start.12 = (f32[2,32,512]{2,1,0:T(8,128)}, f32[2,32,512]{2,1,0:T(8,128)S(1)}, u32[]{:S(2)}, u32[]{:S(2)}) collective-permute-start(f32[2,32,512]{2,1,0:T(8,128)} %get-tuple-element.53), channel_id=1, source_target_pairs={{0,481},{32,1},{64,33},{96,65},{128,97},{160,129},{192,161},{224,1... | collective-permute-start | bytes 393224 | tf_op jit(solution)/shard_map/ppermute | solution.py:266
  179.9 0.7 copy-start.6
  184.5 20.8 %collective-permute-start.13 = (f32[2,32,512]{2,1,0:T(8,128)}, f32[2,32,512]{2,1,0:T(8,128)S(1)}, u32[]{:S(2)}, u32[]{:S(2)}) collective-permute-start(f32[2,32,512]{2,1,0:T(8,128)} %get-tuple-element.56), channel_id=1, source_target_pairs={{0,1},{1,0},{2,3},{3,2},{4,5},{5,4},{6,7},{7,6},{8,9},{9,8},{10,11... | collective-permute-start | bytes 393224 | tf_op jit(solution)/shard_map/ppermute | solution.py:267
  186.8 18.5 %collective-permute-start.14 = (f32[2,32,512]{2,1,0:T(8,128)}, f32[2,32,512]{2,1,0:T(8,128)S(1)}, u32[]{:S(2)}, u32[]{:S(2)}) collective-permute-start(f32[2,32,512]{2,1,0:T(8,128)} %get-tuple-element.57), channel_id=1, source_target_pairs={{0,481},{32,1},{64,33},{96,65},{128,97},{160,129},{192,161},{224,1... | collective-permute-start | bytes 393224 | tf_op jit(solution)/shard_map/ppermute | solution.py:266
  211.8 11.8 %all-to-all-start.6 = ((f32[32,4,128]{2,1,0:T(4,128)}), f32[32,4,128]{2,1,0:T(4,128)S(1)}, u32[]{:S(2)}, u32[]{:S(2)}) async-start(f32[32,4,128]{2,1,0:T(4,128)} %norm.1), calls=%async_computation.6 | async-start | bytes 131072 | tf_op jit(solution)/shard_map/all_to_all | solution.py:275
  226.7 20.3 %all-to-all-start.7 = ((f32[16,2,128]{2,1,0:T(2,128)}), f32[16,2,128]{2,1,0:T(2,128)S(1)}, u32[]{:S(2)}, u32[]{:S(2)}) async-start(f32[16,2,128]{2,1,0:T(2,128)} %get-tuple-element.61), calls=%async_computation.7 | async-start | bytes 32768 | tf_op jit(solution)/shard_map/all_to_all | solution.py:287
  236.5 12.5 %collective-permute-start.15 = (f32[2,4,16,256]{3,2,1,0:T(8,128)S(1)}, f32[2,4,16,256]{3,2,1,0:T(8,128)S(1)}, u32[]{:S(2)}, u32[]{:S(2)}) collective-permute-start(f32[2,4,16,256]{3,2,1,0:T(8,128)S(1)} %constant_dynamic-slice_fusion), channel_id=1, source_target_pairs={{0,1},{1,0},{2,3},{3,2},{4,5},{5,4},{6,7},{7,6},{8,9},{9,8},{10,11... | collective-permute-start | bytes 393224 | tf_op jit(solution)/shard_map/ppermute | solution.py:286
  (7 other events, 4.6 us)

commit v2 on v1

--- a/solution.py
+++ b/solution.py
@@ -10,6 +10,7 @@
 ITERS = 6
 REF_DEV = 8
 PAD = 8
+HALO = 6
 LANES = 128
 INTERPRET = False
 BF = ("block", "flame")
@@ -26,6 +27,7 @@
         scratch_shapes=list(scratch),
         interpret=INTERPRET,
         name=name,
+        compiler_params=pltpu.CompilerParams(vmem_limit_bytes=12 << 20),
     )
 
 
@@ -46,26 +48,65 @@
         outer_ref[i] = ref[planes - 1 - inner]
 
 
-def init_kernel(scal_ref, ext_ref, inv_ref, own_ref, d_ref, a_ref, inner_ref, outer_ref, *, blocks):
+def pack_kernel(scal_ref, *refs):
+    core = scal_ref[0]
+    ins, keep_ref, give_ref = refs[:-2], refs[-2], refs[-1]
+    half = keep_ref.shape[1]
+    for i, ref in enumerate(ins):
+        for p in range(half):
+            keep_ref[i, p] = ref[core * half + p].astype(jnp.float32)
+            give_ref[i, p] = ref[(1 - core) * half + p].astype(jnp.float32)
+
+
+def edges_kernel(scal_ref, keep_ref, got_ref, after_ref, before_ref):
+    core = scal_ref[0]
+    count, half, axial, radial = keep_ref.shape
+    for i in range(count):
+        for p in range(half):
+            to = slice(p * HALO, (p + 1) * HALO)
+            for ref, rng in ((after_ref, slice(0, HALO)), (before_ref, slice(axial - HALO, axial))):
+                mine, other = keep_ref[i, p, rng], got_ref[i, p, rng]
+                ref[i, to, :radial] = jnp.where(core == 0, mine, other)
+                ref[i, to, radial:] = jnp.where(core == 0, other, mine)
+
+
+def init_kernel(scal_ref, keep_ref, got_ref, before_ref, after_ref, bd_ref, ba_ref, gain_ref,
+                inv_ref, own_ref, d_ref, a_ref, inner_ref, outer_ref, shift_ref, id_ref, *, blocks):
     core, block = scal_ref[0], scal_ref[1]
-    _, planes, rows, _ = ext_ref.shape
-    for p in range(planes):
+    _, half, axial, radial = keep_ref.shape
+    rows = axial + 2 * PAD
+    for i, ref in enumerate((bd_ref, ba_ref, shift_ref, gain_ref, id_ref)):
+        for p in range(half):
+            ref[p, :PAD] = jnp.zeros((PAD, 2 * radial), jnp.float32)
+            ref[p, rows - PAD :] = jnp.zeros((PAD, 2 * radial), jnp.float32)
+            ref[p, PAD - HALO : PAD] = before_ref[i, p * HALO : (p + 1) * HALO]
+            ref[p, rows - PAD : rows - PAD + HALO] = after_ref[i, p * HALO : (p + 1) * HALO]
+            mine, other = keep_ref[i, p], got_ref[i, p]
+            ref[p, PAD : PAD + axial, :radial] = jnp.where(core == 0, mine, other)
+            ref[p, PAD : PAD + axial, radial:] = jnp.where(core == 0, other, mine)
+    for p in range(half):
         for t in range(rows // 8):
             at = (p, slice(8 * t, 8 * t + 8))
-            inv = 1.0 / (6.0 + ext_ref[(2,) + at])
-            if t == 0:
+            inv = 1.0 / (6.0 + shift_ref[at])
+            if t < PAD // 8:
                 inv = jnp.where(block == 0, 0.0, inv)
-            if t == rows // 8 - 1:
+            if t >= (rows - PAD) // 8:
                 inv = jnp.where(block == blocks - 1, 0.0, inv)
             inv_ref[at] = inv
-            own_ref[at] = ext_ref[(4,) + at].astype(jnp.int32)
-            d_ref[at] = ext_ref[(0,) + at] * inv
-            a_ref[at] = ext_ref[(1,) + at] * inv
-    _send_planes(core, (d_ref, a_ref), inner_ref, outer_ref, planes)
-
-
-def step_kernel(scal_ref, recv_ref, inner_ref, outer_ref, d_ref, a_ref, ext_ref, inv_ref, own_ref,
-                dn_ref, an_ref, inner_out, outer_out):
+            own_ref[at] = id_ref[at].astype(jnp.int32)
+            d_ref[at] = bd_ref[at] * inv
+            a_ref[at] = ba_ref[at] * inv
+    _send_planes(core, (d_ref, a_ref), inner_ref, outer_ref, half)
+
+
+def step_kernel(scal_ref, *refs):
+    dn_ref, an_ref, inner_out, outer_out = refs[-4:]
+    _sweep(scal_ref, *refs[:-2])
+    _send_planes(scal_ref[0], (dn_ref, an_ref), inner_out, outer_out, dn_ref.shape[0])
+
+
+def _sweep(scal_ref, recv_ref, inner_ref, outer_ref, d_ref, a_ref, bd_ref, ba_ref, gain_ref,
+           inv_ref, own_ref, dn_ref, an_ref):
     core, block = scal_ref[0], scal_ref[1]
     planes, rows, width = d_ref.shape
     tiles = rows // 8
@@ -119,15 +160,14 @@
                 [_lookup(table, own[:, LANES * j : LANES * (j + 1)]) for j in range(width // LANES)],
                 axis=1,
             )
-            flame = ext_ref[(3,) + at] * looked
-            dn_ref[at] = (ext_ref[(0,) + at] + near(d_ref, 0, p, t) + flame) * inv
-            acc = ext_ref[(1,) + at] + near(a_ref, 1, p, t)
+            flame = gain_ref[at] * looked
+            dn_ref[at] = (bd_ref[at] + near(d_ref, 0, p, t) + flame) * inv
+            acc = ba_ref[at] + near(a_ref, 1, p, t)
             if p == 0 and t == PAD // 8:
                 acc = acc + source(block)
             if p == 0 and t == tiles - PAD // 8:
                 acc = acc + source(block + 1)
             an_ref[at] = acc * inv
-    _send_planes(core, (dn_ref, an_ref), inner_out, outer_out, planes)
 
 
 def _write_refs(scal_ref, d_ref, out_ref):
@@ -147,14 +187,14 @@
         )
 
 
-def collect_kernel(scal_ref, d_ref, a_ref, ext_ref, own_ref, out_ref, *split_refs):
+def collect_kernel(scal_ref, d_ref, a_ref, gain_ref, own_ref, out_ref, *split_refs):
     planes, rows, width = d_ref.shape
     tiles = (rows - 2 * PAD) // 8
     _write_refs(scal_ref, d_ref, out_ref)
     for p in range(planes):
         for t in range(tiles):
             at = (p, slice(PAD + 8 * t, PAD + 8 * t + 8))
-            y = ext_ref[(3,) + at] * a_ref[at]
+            y = gain_ref[at] * a_ref[at]
             coarse = y.astype(jnp.bfloat16).astype(jnp.float32)
             fine = y - coarse
             upper = own_ref[at] >= LANES
@@ -191,38 +231,56 @@
     out_ref[:, 3] = jnp.broadcast_to(acc[2:3] + acc[3:4], (count, LANES))
 
 
-def norm_kernel(scal_ref, d_ref, a_ref, out_ref):
-    planes, rows, width = d_ref.shape
-    _write_refs(scal_ref, d_ref, out_ref)
-    for i, ref in enumerate((d_ref, a_ref)):
+def last_kernel(scal_ref, *refs):
+    ins, (keep_ref, give_ref, out_ref, dn_ref, an_ref) = refs[:-5], refs[-5:]
+    core = scal_ref[0]
+    _sweep(scal_ref, *ins, dn_ref, an_ref)
+    _write_refs(scal_ref, dn_ref, out_ref)
+    planes, rows, width = dn_ref.shape
+    radial = width // 2
+    for i, ref in enumerate((dn_ref, an_ref)):
         acc = jnp.zeros((8, width), jnp.float32)
         for p in range(planes):
             for t in range((rows - 2 * PAD) // 8):
                 v = ref[p, PAD + 8 * t : PAD + 8 * t + 8]
                 acc = acc + v * v
+                low, high = v[:, :radial], v[:, radial:]
+                keep_ref[i, p, 8 * t : 8 * t + 8] = jnp.where(core == 0, low, high)
+                give_ref[i, p, 8 * t : 8 * t + 8] = jnp.where(core == 0, high, low)
         acc = sum(acc[:, LANES * j : LANES * (j + 1)] for j in range(width // LANES))
         out_ref[:, 2 + i] = jnp.broadcast_to(
             jnp.sum(acc, axis=0, keepdims=True), (out_ref.shape[0], LANES)
         )
 
 
-def fields_kernel(scal_ref, recv_ref, d_ref, a_ref, ext_ref, own_ref, out_ref, sums_ref):
-    planes, rows, width = d_ref.shape
-    total = jnp.sum(recv_ref[...], axis=0)
-    table = _table(total, 0)
-    sums_ref[...] = jnp.broadcast_to(total[None, 2:4], sums_ref.shape)
+def squares_kernel(scal_ref, recv_ref, out_ref):
+    out_ref[...] = jnp.broadcast_to(
+        jnp.sum(recv_ref[...], axis=0)[None, 2:4], out_ref.shape
+    )
+
+
+def fields_kernel(scal_ref, recv_ref, squares_ref, keep_ref, got_ref, gain_ref, own_ref,
+                  first_ref, second_ref, *, cells):
+    core = scal_ref[0]
+    planes, axial, radial = gain_ref.shape
+    half = planes // 2
+    table = _table(jnp.sum(recv_ref[...], axis=0), 0)
+    squares = jnp.sum(jnp.sum(squares_ref[...], axis=0), axis=1, keepdims=True) / cells
+    scale = lax.rsqrt(squares[0:1] * squares[1:2] + 1e-12)
     for p in range(planes):
-        for t in range((rows - 2 * PAD) // 8):
-            at = (p, slice(PAD + 8 * t, PAD + 8 * t + 8))
-            to = (p, slice(8 * t, 8 * t + 8))
-            own = own_ref[at]
+        for t in range(axial // 8):
+            rng = slice(8 * t, 8 * t + 8)
+            mine = core == 0 if p < half else core == 1
+            direct, adjoint = (
+                jnp.where(mine, keep_ref[i, p % half, rng], got_ref[i, p % half, rng]) for i in (0, 1)
+            )
+            own = own_ref[p, rng]
             looked = jnp.concatenate(
-                [_lookup(table, own[:, LANES * j : LANES * (j + 1)]) for j in range(width // LANES)],
+                [_lookup(table, own[:, LANES * j : LANES * (j + 1)]) for j in range(radial // LANES)],
                 axis=1,
             )
-            adjoint = a_ref[at]
-            out_ref[(0,) + to] = adjoint * d_ref[at]
-            out_ref[(1,) + to] = adjoint * (ext_ref[(3,) + at] * looked)
+            first_ref[p, rng] = adjoint * direct * scale
+            second_ref[p, rng] = adjoint * (gain_ref[p, rng] * looked) * scale
 
 
 def on_device(rhs_direct, rhs_adjoint, diag_shift, flame_gain, ref_owner):
@@ -231,67 +289,61 @@
     core, block = lax.axis_index("flame"), lax.axis_index("block")
     scal = jnp.stack([core, block]).astype(jnp.int32)
     half, width, rows = planes // 2, 2 * radial, axial + 2 * PAD
-    f32 = jnp.float32
     swap = [(0, 1), (1, 0)]
-
-    stack = jnp.stack([rhs_direct, rhs_adjoint, diag_shift, flame_gain, ref_owner.astype(f32)])
-    keep = lax.dynamic_slice_in_dim(stack, core * half, half, axis=1)
-    give = lax.dynamic_slice_in_dim(stack, (1 - core) * half, half, axis=1)
-    got = lax.ppermute(give, "flame", swap)
-    full = jnp.where(
-        core == 0, jnp.concatenate([keep, got], axis=3), jnp.concatenate([got, keep], axis=3)
-    )
-    before = lax.ppermute(full[:, :, axial - PAD :], "block", [(i, i + 1) for i in range(blocks - 1)])
-    after = lax.ppermute(full[:, :, :PAD], "block", [(i + 1, i) for i in range(blocks - 1)])
-    ext = jnp.concatenate([before, full, after], axis=2)
-
-    field = jax.ShapeDtypeStruct((half, rows, width), f32)
-    owners = jax.ShapeDtypeStruct((half, rows, width), jnp.int32)
-    plane = jax.ShapeDtypeStruct((2, rows, width), f32)
-    peers = 2 * blocks
-    message = jax.ShapeDtypeStruct((peers, 4, LANES), f32)
     ring = [(2 * s, (2 * s - 1) % (2 * sectors)) for s in range(sectors)]
     ring += [(2 * s + 1, (2 * s + 2) % (2 * sectors)) for s in range(sectors)]
 
-    inverse, owner, direct, adjoint, inner, outer = _call(
+    def arr(*shape, dtype=jnp.float32):
+        return jax.ShapeDtypeStruct(shape, dtype)
+
+    quarter = arr(5, half, axial, radial)
+    keep, give = _call(pack_kernel, (quarter, quarter), 5, name="pack")(
+        scal, rhs_direct, rhs_adjoint, diag_shift, flame_gain, ref_owner
+    )
+    got = lax.ppermute(give, "flame", swap)
+    edge = arr(5, half * HALO, width)
+    first_rows, last_rows = _call(edges_kernel, (edge, edge), 2, name="edges")(scal, keep, got)
+    before = lax.ppermute(last_rows, "block", [(i, i + 1) for i in range(blocks - 1)])
+    after = lax.ppermute(first_rows, "block", [(i + 1, i) for i in range(blocks - 1)])
+
+    field, plane = arr(half, rows, width), arr(2, rows, width)
+    message = arr(2 * blocks, 4, LANES)
+    bd, ba, gain, inverse, owner, direct, adjoint, inner, outer = _call(
         functools.partial(init_kernel, blocks=blocks),
-        (field, owners, field, field, plane, plane), 1, name="init",
-    )(scal, ext)
-    step = _call(step_kernel, (field, field, plane, plane), 8, name="step")
+        (field,) * 4 + (arr(half, rows, width, dtype=jnp.int32), field, field, plane, plane),
+        4, [pltpu.VMEM((half, rows, width), jnp.float32)] * 2, name="init",
+    )(scal, keep, got, before, after)
+    step = _call(step_kernel, (field, field, plane, plane), 10, name="step")
+    last = _call(
+        last_kernel, (arr(2, half, axial, radial), arr(2, half, axial, radial), message), 10,
+        [pltpu.VMEM((half, rows, width), jnp.float32)] * 2, name="last",
+    )
     collect = _call(
         collect_kernel, message, 4,
-        [pltpu.VMEM((half * axial * 8, LANES), f32)] * (width // LANES), name="collect",
-    )
-    for _ in range(ITERS):
+        [pltpu.VMEM((half * axial * 8, LANES), jnp.float32)] * (width // LANES), name="collect",
+    )
+    for sweep in range(ITERS):
         outer_in = lax.ppermute(outer, ("sector", "flame"), ring)
         inner_in = lax.ppermute(inner, "flame", swap)
-        sent = collect(scal, direct, adjoint, ext, owner)
+        sent = collect(scal, direct, adjoint, gain, owner)
         recv = lax.all_to_all(sent, BF, 0, 0, tiled=True)
-        direct, adjoint, inner, outer = step(
-            scal, recv, inner_in, outer_in, direct, adjoint, ext, inverse, owner
+        args = (scal, recv, inner_in, outer_in, direct, adjoint, bd, ba, gain, inverse, owner)
+        if sweep < ITERS - 1:
+            direct, adjoint, inner, outer = step(*args)
+        else:
+            keep, give, sent = last(*args)
+
+    got = lax.ppermute(give, "flame", swap)
+    recv = lax.all_to_all(sent, BF, 0, 0, tiled=True)
+    squares = _call(squares_kernel, arr(sectors, 2, LANES), 1, name="squares")(scal, recv)
+    squares = lax.all_to_all(squares, "sector", 0, 0, tiled=True)
+    out = arr(planes, axial, radial)
+    cells = planes * axial * radial * sectors * blocks * 2
+    return tuple(
+        _call(functools.partial(fields_kernel, cells=cells), (out, out), 6, name="fields")(
+            scal, recv, squares, keep, got, flame_gain, ref_owner
         )
-
-    sent = _call(norm_kernel, message, 2, name="norm")(scal, direct, adjoint)
-    recv = lax.all_to_all(sent, BF, 0, 0, tiled=True)
-    fields, sums = _call(
-        fields_kernel,
-        (
-            jax.ShapeDtypeStruct((2, half, axial, width), f32),
-            jax.ShapeDtypeStruct((sectors, 2, LANES), f32),
-        ),
-        5, name="fields",
-    )(scal, recv, direct, adjoint, ext, owner)
-    keep = lax.dynamic_slice_in_dim(fields, core * radial, radial, axis=3)
-    give = lax.dynamic_slice_in_dim(fields, (1 - core) * radial, radial, axis=3)
-    got = lax.ppermute(give, "flame", swap)
-    squares = lax.all_to_all(sums, "sector", 0, 0, tiled=True)
-    squares = jnp.sum(squares, axis=(0, 2))
-    cells = planes * axial * radial * sectors * blocks * 2
-    scale = lax.rsqrt(squares[0] / cells * (squares[1] / cells) + 1e-12)
-    low = jnp.where(core == 0, keep, got)
-    high = jnp.where(core == 0, got, keep)
-    out = jnp.concatenate([low, high], axis=1) * scale
-    return out[0], out[1]
+    )
 
 
 def solution(mesh):

time: 252 us -> 208 us (0.83)
  Pallas kernels: 53.4 us -> 29.7 us
  local copies, waits for them, and re-layouts: 13.8 us -> 4.53 us
  other arithmetic: 3.93 us -> 0.08 us
  starting transfers between devices: 69.2 us -> 66.4 us
  blocking collectives: 82.2 us -> 79.5 us
    pallas_call x15 -> x17, Pallas kernels: 53.4 us -> 29.7 us  [the longest x6 17 us: on_device(): sent = collect(scal, direct, adjoint, gain, owner)]
    unnamed x30 -> x14, local copies, waits for them, and re-layouts: 11.5 us -> 4.53 us
    all_to_all x1, waiting for transfers between devices: 7.81 us -> 11.3 us  [on_device(): squares = lax.all_to_all(squares, 'sector', 0, 0, tiled=True)]
    all_to_all x6, blocking collectives: 82.2 us -> 79.5 us  [on_device(): recv = lax.all_to_all(sent, BF, 0, 0, tiled=True)]
  transfers between devices with their start and end apart: 18 -> 18, of which waited for: 5 -> 5; matrix products, arithmetic and copies ran while one was open for 1% -> 0% of each run, Pallas kernels for 11% -> 9%
where the time goes in v2:
time: 208 us; the launch traced here: 207 us
  blocking collectives  79.5 us (38%)
  starting transfers between devices  66.4 us (32%)
  Pallas kernels  29.7 us (14%)
  waiting for transfers between devices  25.9 us (12%)
  local copies, waits for them, and re-layouts  4.53 us (2%)
    all_to_all x6, blocking collectives, on_device(): recv = lax.all_to_all(sent, BF, 0, 0, tiled=True)  79.5 us
    ppermute x6, starting transfers between devices, on_device(): outer_in = lax.ppermute(outer, ('sector', 'flame'), ring)  25.9 us
    pallas_call x6, Pallas kernels, on_device(): sent = collect(scal, direct, adjoint, gain, owner)  17 us
    ppermute x6, starting transfers between devices, on_device(): inner_in = lax.ppermute(inner, 'flame', swap)  14.6 us
    all_to_all x1, waiting for transfers between devices, on_device(): squares = lax.all_to_all(squares, 'sector', 0, 0, tiled=True)  11.3 us
    ppermute x2, starting transfers between devices, on_device(): got = lax.ppermute(give, 'flame', swap)  11 us
    all_to_all x1, starting transfers between devices, on_device(): squares = lax.all_to_all(squares, 'sector', 0, 0, tiled=True)  8.13 us
    pallas_call x5, Pallas kernels, on_device(): direct, adjoint, inner, outer = step(*args)  6.38 us
  transfers between devices with their start and end apart: 18, of which 5 were waited for; matrix products, arithmetic and copies ran while one was open for 0% of the time, Pallas kernels for 9%

profile of v2, /device:TPU:1, one launch (start us, length us, event | category | flops | bytes accessed | tf_op | source)
XLA Modules:
  0.0 207.0 jit_solution(13734235540558819170)
XLA Ops:
  5.8 8.7 %collective-permute-start = (f32[5,4,16,256]{3,2,1,0:T(8,128)S(1)}, f32[5,4,16,256]{3,2,1,0:T(8,128)S(1)}, u32[]{:S(2)}, u32[]{:S(2)}) collective-permute-start(f32[5,4,16,256]{3,2,1,0:T(8,128)S(1)} %get-tuple-element.39), channel_id=1, source_target_pairs={{0,1},{1,0},{2,3},{3,2},{4,5},{5,4},{6,7},{7,6},{8,9},{9,8},{10,11... | collective-permute-start | bytes 983048 | tf_op jit(solution)/shard_map/ppermute | solution.py:303
  19.1 3.9 %collective-permute-done.1.before_ref = f32[5,24,512]{2,1,0:T(8,128)S(1)} collective-permute-done((f32[5,24,512]{2,1,0:T(8,128)S(1)}, f32[5,24,512]{2,1,0:T(8,128)S(1)}, u32[]{:S(2)}, u32[]{:S(2)}) %collective-permute-start.1) | collective-permute-done | bytes 245792 | tf_op jit(solution)/shard_map/ppermute | solution.py:306
  22.9 3.8 %collective-permute-done.2.after_ref = f32[5,24,512]{2,1,0:T(8,128)S(1)} collective-permute-done((f32[5,24,512]{2,1,0:T(8,128)S(1)}, f32[5,24,512]{2,1,0:T(8,128)S(1)}, u32[]{:S(2)}, u32[]{:S(2)}) %collective-permute-start.2) | collective-permute-done | bytes 245792 | tf_op jit(solution)/shard_map/ppermute | solution.py:307
  27.6 3.1 %collective-permute-start.3 = (f32[2,32,512]{2,1,0:T(8,128)S(1)}, f32[2,32,512]{2,1,0:T(8,128)S(1)}, u32[]{:S(2)}, u32[]{:S(2)}) collective-permute-start(f32[2,32,512]{2,1,0:T(8,128)S(1)} %get-tuple-element.46), channel_id=1, source_target_pairs={{0,1},{1,0},{2,3},{3,2},{4,5},{5,4},{6,7},{7,6},{8,9},{9,8},{10,11... | collective-permute-start | bytes 393224 | tf_op jit(solution)/shard_map/ppermute | solution.py:327
  30.7 7.0 %collective-permute-start.4 = (f32[2,32,512]{2,1,0:T(8,128)S(1)}, f32[2,32,512]{2,1,0:T(8,128)S(1)}, u32[]{:S(2)}, u32[]{:S(2)}) collective-permute-start(f32[2,32,512]{2,1,0:T(8,128)S(1)} %get-tuple-element.47), channel_id=1, source_target_pairs={{0,481},{32,1},{64,33},{96,65},{128,97},{160,129},{192,161},{224,1... | collective-permute-start | bytes 393224 | tf_op jit(solution)/shard_map/ppermute | solution.py:326
  37.8 2.8 %collect.6 = f32[32,4,128]{2,1,0:T(4,128)S(1)} custom-call(s32[2]{0:T(128)S(1)} %pad_add_fusion.scal_ref, f32[4,32,512]{2,1,0:T(8,128)S(1)} %get-tuple-element.42.d_ref.refs_3_, f32[4,32,512]{2,1,0:T(8,128)S(1)} %get-tuple-element.43.a_ref.refs_4_, f32[4,32,512]{2,1,0:T(8,128)S(1)} %get-tuple-element.44.gain_ref.refs_7_, ...), custom_call_target="tpu_custom_call" | custom-call | tf_op jit(solution)/shard_map/collect/pallas_call | solution.py:328
  40.6 18.9 %all_to_all.40.refs_0_ = f32[32,4,128]{2,1,0:T(4,128)S(1)} all-to-all(f32[32,4,128]{2,1,0:T(4,128)S(1)} %collect.6), channel_id=1, replica_groups=mesh['sector'=16,'block'=16,'flame'=2] {'block','flame'}, dimensions={0} | all-to-all | bytes 131072 | tf_op jit(solution)/shard_map/all_to_all | solution.py:329
  65.1 2.8 %collect.7 = f32[32,4,128]{2,1,0:T(4,128)S(1)} custom-call(s32[2]{0:T(128)S(1)} %pad_add_fusion.scal_ref, f32[4,32,512]{2,1,0:T(8,128)S(1)} %get-tuple-element.51.d_ref.refs_3_, f32[4,32,512]{2,1,0:T(8,128)S(1)} %get-tuple-element.52.a_ref.refs_4_, f32[4,32,512]{2,1,0:T(8,128)S(1)} %get-tuple-element.44.gain_ref.refs_7_, ...), custom_call_target="tpu_custom_call" | custom-call | tf_op jit(solution)/shard_map/collect/pallas_call | solution.py:328
  67.9 11.5 %all_to_all.41.refs_0_ = f32[32,4,128]{2,1,0:T(4,128)S(1)} all-to-all(f32[32,4,128]{2,1,0:T(4,128)S(1)} %collect.7), channel_id=1, replica_groups=mesh['sector'=16,'block'=16,'flame'=2] {'block','flame'}, dimensions={0} | all-to-all | bytes 131072 | tf_op jit(solution)/shard_map/all_to_all | solution.py:329
  83.0 6.8 %collective-permute-start.8 = (f32[2,32,512]{2,1,0:T(8,128)S(1)}, f32[2,32,512]{2,1,0:T(8,128)S(1)}, u32[]{:S(2)}, u32[]{:S(2)}) collective-permute-start(f32[2,32,512]{2,1,0:T(8,128)S(1)} %get-tuple-element.58), channel_id=1, source_target_pairs={{0,481},{32,1},{64,33},{96,65},{128,97},{160,129},{192,161},{224,1... | collective-permute-start | bytes 393224 | tf_op jit(solution)/shard_map/ppermute | solution.py:326
  89.7 2.8 %collect.8 = f32[32,4,128]{2,1,0:T(4,128)S(1)} custom-call(s32[2]{0:T(128)S(1)} %pad_add_fusion.scal_ref, f32[4,32,512]{2,1,0:T(8,128)S(1)} %get-tuple-element.55.d_ref.refs_3_, f32[4,32,512]{2,1,0:T(8,128)S(1)} %get-tuple-element.56.a_ref.refs_4_, f32[4,32,512]{2,1,0:T(8,128)S(1)} %get-tuple-element.44.gain_ref.refs_7_, ...), custom_call_target="tpu_custom_call" | custom-call | tf_op jit(solution)/shard_map/collect/pallas_call | solution.py:328
  92.6 12.8 %all_to_all.42.refs_0_ = f32[32,4,128]{2,1,0:T(4,128)S(1)} all-to-all(f32[32,4,128]{2,1,0:T(4,128)S(1)} %collect.8), channel_id=1, replica_groups=mesh['sector'=16,'block'=16,'flame'=2] {'block','flame'}, dimensions={0} | all-to-all | bytes 131072 | tf_op jit(solution)/shard_map/all_to_all | solution.py:329
  106.6 2.3 %collective-permute-start.9 = (f32[2,32,512]{2,1,0:T(8,128)S(1)}, f32[2,32,512]{2,1,0:T(8,128)S(1)}, u32[]{:S(2)}, u32[]{:S(2)}) collective-permute-start(f32[2,32,512]{2,1,0:T(8,128)S(1)} %get-tuple-element.61), channel_id=1, source_target_pairs={{0,1},{1,0},{2,3},{3,2},{4,5},{5,4},{6,7},{7,6},{8,9},{9,8},{10,11... | collective-permute-start | bytes 393224 | tf_op jit(solution)/shard_map/ppermute | solution.py:327
  110.9 2.8 %collect.9 = f32[32,4,128]{2,1,0:T(4,128)S(1)} custom-call(s32[2]{0:T(128)S(1)} %pad_add_fusion.scal_ref, f32[4,32,512]{2,1,0:T(8,128)S(1)} %get-tuple-element.59.d_ref.refs_3_, f32[4,32,512]{2,1,0:T(8,128)S(1)} %get-tuple-element.60.a_ref.refs_4_, f32[4,32,512]{2,1,0:T(8,128)S(1)} %get-tuple-element.44.gain_ref.refs_7_, ...), custom_call_target="tpu_custom_call" | custom-call | tf_op jit(solution)/shard_map/collect/pallas_call | solution.py:328
  113.7 11.8 %all_to_all.43.refs_0_ = f32[32,4,128]{2,1,0:T(4,128)S(1)} all-to-all(f32[32,4,128]{2,1,0:T(4,128)S(1)} %collect.9), channel_id=1, replica_groups=mesh['sector'=16,'block'=16,'flame'=2] {'block','flame'}, dimensions={0} | all-to-all | bytes 131072 | tf_op jit(solution)/shard_map/all_to_all | solution.py:329
  129.1 6.4 %collective-permute-start.12 = (f32[2,32,512]{2,1,0:T(8,128)S(1)}, f32[2,32,512]{2,1,0:T(8,128)S(1)}, u32[]{:S(2)}, u32[]{:S(2)}) collective-permute-start(f32[2,32,512]{2,1,0:T(8,128)S(1)} %get-tuple-element.66), channel_id=1, source_target_pairs={{0,481},{32,1},{64,33},{96,65},{128,97},{160,129},{192,161},{224,1... | collective-permute-start | bytes 393224 | tf_op jit(solution)/shard_map/ppermute | solution.py:326
  135.5 2.8 %collect.10 = f32[32,4,128]{2,1,0:T(4,128)S(1)} custom-call(s32[2]{0:T(128)S(1)} %pad_add_fusion.scal_ref, f32[4,32,512]{2,1,0:T(8,128)S(1)} %get-tuple-element.63.d_ref.refs_3_, f32[4,32,512]{2,1,0:T(8,128)S(1)} %get-tuple-element.64.a_ref.refs_4_, f32[4,32,512]{2,1,0:T(8,128)S(1)} %get-tuple-element.44.gain_ref.refs_7_, ...), custom_call_target="tpu_custom_call" | custom-call | tf_op jit(solution)/shard_map/collect/pallas_call | solution.py:328
  138.4 12.8 %all_to_all.44.refs_0_ = f32[32,4,128]{2,1,0:T(4,128)S(1)} all-to-all(f32[32,4,128]{2,1,0:T(4,128)S(1)} %collect.10), channel_id=1, replica_groups=mesh['sector'=16,'block'=16,'flame'=2] {'block','flame'}, dimensions={0} | all-to-all | bytes 131072 | tf_op jit(solution)/shard_map/all_to_all | solution.py:329
  156.7 2.8 %collect.11 = f32[32,4,128]{2,1,0:T(4,128)S(1)} custom-call(s32[2]{0:T(128)S(1)} %pad_add_fusion.scal_ref, f32[4,32,512]{2,1,0:T(8,128)S(1)} %get-tuple-element.67.d_ref.refs_3_, f32[4,32,512]{2,1,0:T(8,128)S(1)} %get-tuple-element.68.a_ref.refs_4_, f32[4,32,512]{2,1,0:T(8,128)S(1)} %get-tuple-element.44.gain_ref.refs_7_, ...), custom_call_target="tpu_custom_call" | custom-call | tf_op jit(solution)/shard_map/collect/pallas_call | solution.py:328
  159.5 11.8 %all_to_all.45.refs_0_ = f32[32,4,128]{2,1,0:T(4,128)S(1)} all-to-all(f32[32,4,128]{2,1,0:T(4,128)S(1)} %collect.11), channel_id=1, replica_groups=mesh['sector'=16,'block'=16,'flame'=2] {'block','flame'}, dimensions={0} | all-to-all | bytes 131072 | tf_op jit(solution)/shard_map/all_to_all | solution.py:329
  173.0 4.0 %all-to-all-start.6 = ((f32[32,4,128]{2,1,0:T(4,128)}), f32[32,4,128]{2,1,0:T(4,128)S(1)}, u32[]{:S(2)}, u32[]{:S(2)}) async-start(f32[32,4,128]{2,1,0:T(4,128)} %get-tuple-element.71), calls=%async_computation.6 | async-start | bytes 131072 | tf_op jit(solution)/shard_map/all_to_all | solution.py:337
  179.3 5.6 %all-to-all-done.6.recv_ref = f32[32,4,128]{2,1,0:T(4,128)S(1)} async-done(((f32[32,4,128]{2,1,0:T(4,128)}), f32[32,4,128]{2,1,0:T(4,128)S(1)}, u32[]{:S(2)}, u32[]{:S(2)}) %all-to-all-start.6) | async-done | bytes 65568 | tf_op jit(solution)/shard_map/all_to_all | solution.py:337
  186.0 8.1 %all-to-all-start.7 = ((f32[16,2,128]{2,1,0:T(2,128)}), f32[16,2,128]{2,1,0:T(2,128)S(1)}, u32[]{:S(2)}, u32[]{:S(2)}) async-start(f32[16,2,128]{2,1,0:T(2,128)} %squares.1), calls=%async_computation.7 | async-start | bytes 32768 | tf_op jit(solution)/shard_map/all_to_all | solution.py:339
  194.2 11.3 %all-to-all-done.7.squares_ref = f32[16,2,128]{2,1,0:T(2,128)S(1)} async-done(((f32[16,2,128]{2,1,0:T(2,128)}), f32[16,2,128]{2,1,0:T(2,128)S(1)}, u32[]{:S(2)}, u32[]{:S(2)}) %all-to-all-start.7) | async-done | bytes 16416 | tf_op jit(solution)/shard_map/all_to_all | solution.py:339
  (50 shorter events, 38.3 us)
Async XLA Ops:
  0.7 0.9 copy-start
  1.6 0.9 copy-start.2
  2.5 0.9 copy-start.4
  3.4 0.9 copy-start.5
  5.8 10.0 %collective-permute-start = (f32[5,4,16,256]{3,2,1,0:T(8,128)S(1)}, f32[5,4,16,256]{3,2,1,0:T(8,128)S(1)}, u32[]{:S(2)}, u32[]{:S(2)}) collective-permute-start(f32[5,4,16,256]{3,2,1,0:T(8,128)S(1)} %get-tuple-element.39), channel_id=1, source_target_pairs={{0,1},{1,0},{2,3},{3,2},{4,5},{5,4},{6,7},{7,6},{8,9},{9,8},{10,11... | collective-permute-start | bytes 983048 | tf_op jit(solution)/shard_map/ppermute | solution.py:303
  16.4 6.5 %collective-permute-start.1 = (f32[5,24,512]{2,1,0:T(8,128)S(1)}, f32[5,24,512]{2,1,0:T(8,128)S(1)}, u32[]{:S(2)}, u32[]{:S(2)}) collective-permute-start(f32[5,24,512]{2,1,0:T(8,128)S(1)} %get-tuple-element.40), channel_id=1, source_target_pairs={{0,2},{2,4},{4,6},{6,8},{8,10},{10,12},{12,14},{14,16},{16,18},{18... | collective-permute-start | bytes 737288 | tf_op jit(solution)/shard_map/ppermute | solution.py:306
  17.8 9.0 %collective-permute-start.2 = (f32[5,24,512]{2,1,0:T(8,128)S(1)}, f32[5,24,512]{2,1,0:T(8,128)S(1)}, u32[]{:S(2)}, u32[]{:S(2)}) collective-permute-start(f32[5,24,512]{2,1,0:T(8,128)S(1)} %get-tuple-element.41), channel_id=1, source_target_pairs={{2,0},{4,2},{6,4},{8,6},{10,8},{12,10},{14,12},{16,14},{18,16},{20... | collective-permute-start | bytes 737288 | tf_op jit(solution)/shard_map/ppermute | solution.py:307
  27.6 32.0 %collective-permute-start.3 = (f32[2,32,512]{2,1,0:T(8,128)S(1)}, f32[2,32,512]{2,1,0:T(8,128)S(1)}, u32[]{:S(2)}, u32[]{:S(2)}) collective-permute-start(f32[2,32,512]{2,1,0:T(8,128)S(1)} %get-tuple-element.46), channel_id=1, source_target_pairs={{0,1},{1,0},{2,3},{3,2},{4,5},{5,4},{6,7},{7,6},{8,9},{9,8},{10,11... | collective-permute-start | bytes 393224 | tf_op jit(solution)/shard_map/ppermute | solution.py:327
  30.7 28.8 %collective-permute-start.4 = (f32[2,32,512]{2,1,0:T(8,128)S(1)}, f32[2,32,512]{2,1,0:T(8,128)S(1)}, u32[]{:S(2)}, u32[]{:S(2)}) collective-permute-start(f32[2,32,512]{2,1,0:T(8,128)S(1)} %get-tuple-element.47), channel_id=1, source_target_pairs={{0,481},{32,1},{64,33},{96,65},{128,97},{160,129},{192,161},{224,1... | collective-permute-start | bytes 393224 | tf_op jit(solution)/shard_map/ppermute | solution.py:326
  60.8 18.6 %collective-permute-start.5 = (f32[2,32,512]{2,1,0:T(8,128)S(1)}, f32[2,32,512]{2,1,0:T(8,128)S(1)}, u32[]{:S(2)}, u32[]{:S(2)}) collective-permute-start(f32[2,32,512]{2,1,0:T(8,128)S(1)} %get-tuple-element.53), channel_id=1, source_target_pairs={{0,1},{1,0},{2,3},{3,2},{4,5},{5,4},{6,7},{7,6},{8,9},{9,8},{10,11... | collective-permute-start | bytes 393224 | tf_op jit(solution)/shard_map/ppermute | solution.py:327
  63.1 16.3 %collective-permute-start.6 = (f32[2,32,512]{2,1,0:T(8,128)S(1)}, f32[2,32,512]{2,1,0:T(8,128)S(1)}, u32[]{:S(2)}, u32[]{:S(2)}) collective-permute-start(f32[2,32,512]{2,1,0:T(8,128)S(1)} %get-tuple-element.54), channel_id=1, source_target_pairs={{0,481},{32,1},{64,33},{96,65},{128,97},{160,129},{192,161},{224,1... | collective-permute-start | bytes 393224 | tf_op jit(solution)/shard_map/ppermute | solution.py:326
  80.7 24.7 %collective-permute-start.7 = (f32[2,32,512]{2,1,0:T(8,128)S(1)}, f32[2,32,512]{2,1,0:T(8,128)S(1)}, u32[]{:S(2)}, u32[]{:S(2)}) collective-permute-start(f32[2,32,512]{2,1,0:T(8,128)S(1)} %get-tuple-element.57), channel_id=1, source_target_pairs={{0,1},{1,0},{2,3},{3,2},{4,5},{5,4},{6,7},{7,6},{8,9},{9,8},{10,11... | collective-permute-start | bytes 393224 | tf_op jit(solution)/shard_map/ppermute | solution.py:327
  83.0 22.4 %collective-permute-start.8 = (f32[2,32,512]{2,1,0:T(8,128)S(1)}, f32[2,32,512]{2,1,0:T(8,128)S(1)}, u32[]{:S(2)}, u32[]{:S(2)}) collective-permute-start(f32[2,32,512]{2,1,0:T(8,128)S(1)} %get-tuple-element.58), channel_id=1, source_target_pairs={{0,481},{32,1},{64,33},{96,65},{128,97},{160,129},{192,161},{224,1... | collective-permute-start | bytes 393224 | tf_op jit(solution)/shard_map/ppermute | solution.py:326
  106.6 18.9 %collective-permute-start.9 = (f32[2,32,512]{2,1,0:T(8,128)S(1)}, f32[2,32,512]{2,1,0:T(8,128)S(1)}, u32[]{:S(2)}, u32[]{:S(2)}) collective-permute-start(f32[2,32,512]{2,1,0:T(8,128)S(1)} %get-tuple-element.61), channel_id=1, source_target_pairs={{0,1},{1,0},{2,3},{3,2},{4,5},{5,4},{6,7},{7,6},{8,9},{9,8},{10,11... | collective-permute-start | bytes 393224 | tf_op jit(solution)/shard_map/ppermute | solution.py:327
  109.0 16.6 %collective-permute-start.10 = (f32[2,32,512]{2,1,0:T(8,128)S(1)}, f32[2,32,512]{2,1,0:T(8,128)S(1)}, u32[]{:S(2)}, u32[]{:S(2)}) collective-permute-start(f32[2,32,512]{2,1,0:T(8,128)S(1)} %get-tuple-element.62), channel_id=1, source_target_pairs={{0,481},{32,1},{64,33},{96,65},{128,97},{160,129},{192,161},{224,1... | collective-permute-start | bytes 393224 | tf_op jit(solution)/shard_map/ppermute | solution.py:326
  126.8 24.4 %collective-permute-start.11 = (f32[2,32,512]{2,1,0:T(8,128)S(1)}, f32[2,32,512]{2,1,0:T(8,128)S(1)}, u32[]{:S(2)}, u32[]{:S(2)}) collective-permute-start(f32[2,32,512]{2,1,0:T(8,128)S(1)} %get-tuple-element.65), channel_id=1, source_target_pairs={{0,1},{1,0},{2,3},{3,2},{4,5},{5,4},{6,7},{7,6},{8,9},{9,8},{10,11... | collective-permute-start | bytes 393224 | tf_op jit(solution)/shard_map/ppermute | solution.py:327
  129.1 22.1 %collective-permute-start.12 = (f32[2,32,512]{2,1,0:T(8,128)S(1)}, f32[2,32,512]{2,1,0:T(8,128)S(1)}, u32[]{:S(2)}, u32[]{:S(2)}) collective-permute-start(f32[2,32,512]{2,1,0:T(8,128)S(1)} %get-tuple-element.66), channel_id=1, source_target_pairs={{0,481},{32,1},{64,33},{96,65},{128,97},{160,129},{192,161},{224,1... | collective-permute-start | bytes 393224 | tf_op jit(solution)/shard_map/ppermute | solution.py:326
  152.5 18.9 %collective-permute-start.13 = (f32[2,32,512]{2,1,0:T(8,128)S(1)}, f32[2,32,512]{2,1,0:T(8,128)S(1)}, u32[]{:S(2)}, u32[]{:S(2)}) collective-permute-start(f32[2,32,512]{2,1,0:T(8,128)S(1)} %get-tuple-element.69), channel_id=1, source_target_pairs={{0,1},{1,0},{2,3},{3,2},{4,5},{5,4},{6,7},{7,6},{8,9},{9,8},{10,11... | collective-permute-start | bytes 393224 | tf_op jit(solution)/shard_map/ppermute | solution.py:327
  154.8 16.6 %collective-permute-start.14 = (f32[2,32,512]{2,1,0:T(8,128)S(1)}, f32[2,32,512]{2,1,0:T(8,128)S(1)}, u32[]{:S(2)}, u32[]{:S(2)}) collective-permute-start(f32[2,32,512]{2,1,0:T(8,128)S(1)} %get-tuple-element.70), channel_id=1, source_target_pairs={{0,481},{32,1},{64,33},{96,65},{128,97},{160,129},{192,161},{224,1... | collective-permute-start | bytes 393224 | tf_op jit(solution)/shard_map/ppermute | solution.py:326
  171.3 34.2 %copy-start.3 = (s32[8,16,256]{2,1,0:T(8,128)S(1)}, s32[8,16,256]{2,1,0:T(8,128)}, u32[]{:S(2)}) copy-start(s32[8,16,256]{2,1,0:T(8,128)} %own_ref.1) | copy-start | bytes 393220
  173.0 32.5 %copy-start.1 = (f32[8,16,256]{2,1,0:T(8,128)S(1)}, f32[8,16,256]{2,1,0:T(8,128)}, u32[]{:S(2)}) copy-start(f32[8,16,256]{2,1,0:T(8,128)} %gain_ref.1) | copy-start | bytes 393220
  173.0 11.9 %all-to-all-start.6 = ((f32[32,4,128]{2,1,0:T(4,128)}), f32[32,4,128]{2,1,0:T(4,128)S(1)}, u32[]{:S(2)}, u32[]{:S(2)}) async-start(f32[32,4,128]{2,1,0:T(4,128)} %get-tuple-element.71), calls=%async_computation.6 | async-start | bytes 131072 | tf_op jit(solution)/shard_map/all_to_all | solution.py:337
  177.0 17.2 %collective-permute-start.15 = (f32[2,4,16,256]{3,2,1,0:T(8,128)S(1)}, f32[2,4,16,256]{3,2,1,0:T(8,128)S(1)}, u32[]{:S(2)}, u32[]{:S(2)}) collective-permute-start(f32[2,4,16,256]{3,2,1,0:T(8,128)S(1)} %get-tuple-element.73), channel_id=1, source_target_pairs={{0,1},{1,0},{2,3},{3,2},{4,5},{5,4},{6,7},{7,6},{8,9},{9,8},{10,11... | collective-permute-start | bytes 393224 | tf_op jit(solution)/shard_map/ppermute | solution.py:336
  186.0 19.5 %all-to-all-start.7 = ((f32[16,2,128]{2,1,0:T(2,128)}), f32[16,2,128]{2,1,0:T(2,128)S(1)}, u32[]{:S(2)}, u32[]{:S(2)}) async-start(f32[16,2,128]{2,1,0:T(2,128)} %squares.1), calls=%async_computation.7 | async-start | bytes 32768 | tf_op jit(solution)/shard_map/all_to_all | solution.py:339
  (1 other events, 0.9 us)

commit v3 on v2

--- a/solution.py
+++ b/solution.py
@@ -16,18 +16,18 @@
 BF = ("block", "flame")
 
 
-def _call(kernel, out_shape, n_in, scratch=(), name=None):
+def _call(kernel, out_shape, n_in, scratch=(), name=None, space=pltpu.VMEM):
     vmem = pl.BlockSpec(memory_space=pltpu.VMEM)
     single = not isinstance(out_shape, (tuple, list))
     return pl.pallas_call(
         kernel,
         out_shape=out_shape,
-        in_specs=[pl.BlockSpec(memory_space=pltpu.SMEM)] + [vmem] * n_in,
+        in_specs=[pl.BlockSpec(memory_space=pltpu.SMEM)] + [pl.BlockSpec(memory_space=space)] * n_in,
         out_specs=vmem if single else [vmem] * len(out_shape),
         scratch_shapes=list(scratch),
         interpret=INTERPRET,
         name=name,
-        compiler_params=pltpu.CompilerParams(vmem_limit_bytes=12 << 20),
+        compiler_params=pltpu.CompilerParams(vmem_limit_bytes=24 << 20),
     )
 
 
@@ -41,21 +41,31 @@
     return [jnp.broadcast_to(total[row + j : row + j + 1], (8, LANES)) for j in (0, 1)]
 
 
-def _send_planes(core, refs, inner_ref, outer_ref, planes):
-    inner = jnp.where(core == 0, planes - 1, 0)
+def _send_planes(refs, inner_ref, outer_ref):
     for i, ref in enumerate(refs):
-        inner_ref[i] = ref[inner]
-        outer_ref[i] = ref[planes - 1 - inner]
+        inner_ref[i] = ref[ref.shape[0] - 1]
+        outer_ref[i] = ref[0]
 
 
 def pack_kernel(scal_ref, *refs):
     core = scal_ref[0]
-    ins, keep_ref, give_ref = refs[:-2], refs[-2], refs[-1]
+    ins, (keep_ref, give_ref, keep_id, give_id, sems) = refs[:5], refs[5:]
     half = keep_ref.shape[1]
+    copies = []
     for i, ref in enumerate(ins):
         for p in range(half):
-            keep_ref[i, p] = ref[core * half + p].astype(jnp.float32)
-            give_ref[i, p] = ref[(1 - core) * half + p].astype(jnp.float32)
+            step = 2 * half - 1 - 2 * p
+            for k, (dst, ids, at) in enumerate(
+                ((keep_ref, keep_id, core), (give_ref, give_id, 1 - core))
+            ):
+                to = dst.at[i, p] if i < 4 else ids.at[p]
+                copies.append(pltpu.make_async_copy(ref.at[p + at * step], to, sems.at[i, p, k]))
+    for copy in copies:
+        copy.start()
+    for copy in copies:
+        copy.wait()
+    keep_ref[4] = keep_id[...].astype(jnp.float32)
+    give_ref[4] = give_id[...].astype(jnp.float32)
 
 
 def edges_kernel(scal_ref, keep_ref, got_ref, after_ref, before_ref):
@@ -71,7 +81,8 @@
 
 
 def init_kernel(scal_ref, keep_ref, got_ref, before_ref, after_ref, bd_ref, ba_ref, gain_ref,
-                inv_ref, own_ref, d_ref, a_ref, inner_ref, outer_ref, shift_ref, id_ref, *, blocks):
+                inv_ref, own_ref, hot_ref, d_ref, a_ref, inner_ref, outer_ref, out_ref,
+                shift_ref, id_ref, *split_refs, blocks):
     core, block = scal_ref[0], scal_ref[1]
     _, half, axial, radial = keep_ref.shape
     rows = axial + 2 * PAD
@@ -96,13 +107,28 @@
             own_ref[at] = id_ref[at].astype(jnp.int32)
             d_ref[at] = bd_ref[at] * inv
             a_ref[at] = ba_ref[at] * inv
-    _send_planes(core, (d_ref, a_ref), inner_ref, outer_ref, half)
+    _send_planes((d_ref, a_ref), inner_ref, outer_ref)
+    width = 2 * radial
+    ids = lax.broadcasted_iota(jnp.int32, (16, width), 0).astype(jnp.float32)
+    one = jnp.ones((16, width), jnp.bfloat16)
+    zero = jnp.zeros((16, width), jnp.bfloat16)
+    for p in range(half):
+        for t in range(axial // 8):
+            low = (own_ref[p, PAD + 8 * t : PAD + 8 * t + 8] & (LANES - 1)).astype(jnp.float32)
+            for x in range(8):
+                line = jnp.broadcast_to(low[x : x + 1], (16, width)).astype(jnp.bfloat16)
+                for g in range(LANES // 16):
+                    hit = line == (ids + 16.0 * g).astype(jnp.bfloat16)
+                    hot_ref[(p * (axial // 8) + t) * 8 + x, 16 * g : 16 * g + 16] = jnp.where(hit, one, zero)
+    _collect(scal_ref, d_ref, a_ref, gain_ref, own_ref, hot_ref, out_ref, split_refs)
 
 
 def step_kernel(scal_ref, *refs):
-    dn_ref, an_ref, inner_out, outer_out = refs[-4:]
-    _sweep(scal_ref, *refs[:-2])
-    _send_planes(scal_ref[0], (dn_ref, an_ref), inner_out, outer_out, dn_ref.shape[0])
+    ins, hot_ref, refs = refs[:10], refs[10], refs[11:]
+    (dn_ref, an_ref, inner_out, outer_out, out_ref), split_refs = refs[:5], refs[5:]
+    _sweep(scal_ref, *ins, dn_ref, an_ref)
+    _send_planes((dn_ref, an_ref), inner_out, outer_out)
+    _collect(scal_ref, dn_ref, an_ref, ins[7], ins[9], hot_ref, out_ref, split_refs)
 
 
 def _sweep(scal_ref, recv_ref, inner_ref, outer_ref, d_ref, a_ref, bd_ref, ba_ref, gain_ref,
@@ -131,14 +157,8 @@
     def near(ref, field, p, t):
         rng = slice(8 * t, 8 * t + 8)
         here = ref[p, rng]
-        if p == 0:
-            below = jnp.where(core == 0, outer_ref[field, rng], inner_ref[field, rng])
-        else:
-            below = ref[p - 1, rng]
-        if p == planes - 1:
-            above = jnp.where(core == 0, inner_ref[field, rng], outer_ref[field, rng])
-        else:
-            above = ref[p + 1, rng]
+        below = outer_ref[field, rng] if p == 0 else ref[p - 1, rng]
+        above = inner_ref[field, rng] if p == planes - 1 else ref[p + 1, rng]
         if t == 0:
             back = pltpu.roll(here, 1, 0)
         else:
@@ -170,8 +190,7 @@
             an_ref[at] = acc * inv
 
 
-def _write_refs(scal_ref, d_ref, out_ref):
-    core, block = scal_ref[0], scal_ref[1]
+def _ref_values(d_ref):
     width = d_ref.shape[2]
     lane = lax.broadcasted_iota(jnp.int32, (8, LANES), 1)
     row = d_ref[0, PAD : PAD + 8]
@@ -180,6 +199,12 @@
         part = jnp.broadcast_to(row[0:1, LANES * j : LANES * (j + 1)], (8, LANES))
         pick = jnp.take_along_axis(part, (lane & 3) * 32, axis=1, mode="promise_in_bounds")
         got = jnp.where((lane & 15) // 4 == j, pick, got)
+    return lane, got
+
+
+def _write_refs(scal_ref, d_ref, out_ref):
+    core, block = scal_ref[0], scal_ref[1]
+    lane, got = _ref_values(d_ref)
     for half in (0, 1):
         mine = (lane // 16 + 8 * half == block) & (core == 0)
         out_ref[:, half] = jnp.broadcast_to(
@@ -187,7 +212,7 @@
         )
 
 
-def collect_kernel(scal_ref, d_ref, a_ref, gain_ref, own_ref, out_ref, *split_refs):
+def _collect(scal_ref, d_ref, a_ref, gain_ref, own_ref, hot_ref, out_ref, split_refs):
     planes, rows, width = d_ref.shape
     tiles = (rows - 2 * PAD) // 8
     _write_refs(scal_ref, d_ref, out_ref)
@@ -208,24 +233,13 @@
             for j in range(width // LANES):
                 for k, term in enumerate(terms):
                     split_refs[j][pl.ds(base + k, 8, stride=8), :] = term[:, LANES * j : LANES * (j + 1)]
-    ids = lax.broadcasted_iota(jnp.int32, (16, width), 0).astype(jnp.float32)
-    one = jnp.ones((16, width), jnp.bfloat16)
-    zero = jnp.zeros((16, width), jnp.bfloat16)
-    groups = [(ids + 16.0 * g).astype(jnp.bfloat16) for g in range(LANES // 16)]
     acc = jnp.zeros((8, LANES), jnp.float32)
-    for p in range(planes):
-        for t in range(tiles):
-            low = (own_ref[p, PAD + 8 * t : PAD + 8 * t + 8] & (LANES - 1)).astype(jnp.float32)
-            for x in range(8):
-                line = jnp.broadcast_to(low[x : x + 1], (16, width)).astype(jnp.bfloat16)
-                hot = jnp.concatenate([jnp.where(line == g, one, zero) for g in groups], axis=0)
-                base = ((p * tiles + t) * 8 + x) * 8
-                vals = jnp.concatenate(
-                    [ref[base : base + 8, :] for ref in split_refs], axis=1
-                ).astype(jnp.bfloat16)
-                acc = acc + lax.dot_general(
-                    vals, hot, (((1,), (1,)), ((), ())), preferred_element_type=jnp.float32
-                )
+    for line in range(hot_ref.shape[0]):
+        vals = jnp.concatenate([ref[8 * line : 8 * line + 8, :] for ref in split_refs], axis=1)
+        acc = acc + lax.dot_general(
+            vals.astype(jnp.bfloat16), hot_ref[line], (((1,), (1,)), ((), ())),
+            preferred_element_type=jnp.float32,
+        )
     count = out_ref.shape[0]
     out_ref[:, 2] = jnp.broadcast_to(acc[0:1] + acc[1:2], (count, LANES))
     out_ref[:, 3] = jnp.broadcast_to(acc[2:3] + acc[3:4], (count, LANES))
@@ -233,11 +247,12 @@
 
 def last_kernel(scal_ref, *refs):
     ins, (keep_ref, give_ref, out_ref, dn_ref, an_ref) = refs[:-5], refs[-5:]
-    core = scal_ref[0]
+    core, block = scal_ref[0], scal_ref[1]
     _sweep(scal_ref, *ins, dn_ref, an_ref)
-    _write_refs(scal_ref, dn_ref, out_ref)
     planes, rows, width = dn_ref.shape
     radial = width // 2
+    lane, values = _ref_values(dn_ref)
+    line = jnp.where((lane // 16 == jnp.bitwise_and(block, 3)) & (core == 0), values, 0.0)[0:1]
     for i, ref in enumerate((dn_ref, an_ref)):
         acc = jnp.zeros((8, width), jnp.float32)
         for p in range(planes):
@@ -248,31 +263,38 @@
                 keep_ref[i, p, 8 * t : 8 * t + 8] = jnp.where(core == 0, low, high)
                 give_ref[i, p, 8 * t : 8 * t + 8] = jnp.where(core == 0, high, low)
         acc = sum(acc[:, LANES * j : LANES * (j + 1)] for j in range(width // LANES))
-        out_ref[:, 2 + i] = jnp.broadcast_to(
-            jnp.sum(acc, axis=0, keepdims=True), (out_ref.shape[0], LANES)
-        )
-
-
-def squares_kernel(scal_ref, recv_ref, out_ref):
-    out_ref[...] = jnp.broadcast_to(
-        jnp.sum(recv_ref[...], axis=0)[None, 2:4], out_ref.shape
-    )
-
-
-def fields_kernel(scal_ref, recv_ref, squares_ref, keep_ref, got_ref, gain_ref, own_ref,
-                  first_ref, second_ref, *, cells):
-    core = scal_ref[0]
+        acc = acc + pltpu.roll(acc, 64, 1)
+        acc = jnp.sum(acc + pltpu.roll(acc, 32, 1), axis=0, keepdims=True)
+        line = jnp.where(lane[0:1] // 32 == 2 + i, acc, line)
+    out_ref[...] = jnp.broadcast_to(line, out_ref.shape)
+
+
+def fields_kernel(scal_ref, recv_ref, keep_ref, got_ref, gain_ref, own_ref, first_ref, second_ref,
+                  *, cells, group):
+    core, sector = scal_ref[0], scal_ref[2]
     planes, axial, radial = gain_ref.shape
     half = planes // 2
-    table = _table(jnp.sum(recv_ref[...], axis=0), 0)
-    squares = jnp.sum(jnp.sum(squares_ref[...], axis=0), axis=1, keepdims=True) / cells
-    scale = lax.rsqrt(squares[0:1] * squares[1:2] + 1e-12)
+    lane = lax.broadcasted_iota(jnp.int32, (8, LANES), 1)
+    quads = [
+        jnp.broadcast_to(
+            jnp.sum(recv_ref[pl.ds(pl.multiple_of(sector * group, 8) + 8 * j, 8), :], axis=0, keepdims=True),
+            (8, LANES),
+        )
+        for j in range(4)
+    ]
+    table = [jnp.where(lane < 64, quads[2 * j], pltpu.roll(quads[2 * j + 1], 64, 1)) for j in (0, 1)]
+    total = jnp.broadcast_to(jnp.sum(recv_ref[...], axis=0, keepdims=True), (8, LANES))
+    squares = [
+        jnp.sum(jnp.where(lane // 32 == 2 + i, total, 0.0), axis=1, keepdims=True)[0:1] / cells
+        for i in (0, 1)
+    ]
+    scale = lax.rsqrt(squares[0] * squares[1] + 1e-12)
     for p in range(planes):
         for t in range(axial // 8):
             rng = slice(8 * t, 8 * t + 8)
-            mine = core == 0 if p < half else core == 1
+            mine, at = (core == 0, p) if p < half else (core == 1, planes - 1 - p)
             direct, adjoint = (
-                jnp.where(mine, keep_ref[i, p % half, rng], got_ref[i, p % half, rng]) for i in (0, 1)
+                jnp.where(mine, keep_ref[i, at, rng], got_ref[i, at, rng]) for i in (0, 1)
             )
             own = own_ref[p, rng]
             looked = jnp.concatenate(
@@ -287,7 +309,7 @@
     planes, axial, radial = rhs_direct.shape
     sectors, blocks = lax.axis_size("sector"), lax.axis_size("block")
     core, block = lax.axis_index("flame"), lax.axis_index("block")
-    scal = jnp.stack([core, block]).astype(jnp.int32)
+    scal = jnp.stack([core, block, lax.axis_index("sector")]).astype(jnp.int32)
     half, width, rows = planes // 2, 2 * radial, axial + 2 * PAD
     swap = [(0, 1), (1, 0)]
     ring = [(2 * s, (2 * s - 1) % (2 * sectors)) for s in range(sectors)]
@@ -297,9 +319,11 @@
         return jax.ShapeDtypeStruct(shape, dtype)
 
     quarter = arr(5, half, axial, radial)
-    keep, give = _call(pack_kernel, (quarter, quarter), 5, name="pack")(
-        scal, rhs_direct, rhs_adjoint, diag_shift, flame_gain, ref_owner
-    )
+    ids = pltpu.VMEM((half, axial, radial), jnp.int32)
+    keep, give = _call(
+        pack_kernel, (quarter, quarter), 5, [ids, ids, pltpu.SemaphoreType.DMA((5, half, 2))],
+        name="pack", space=pltpu.HBM,
+    )(scal, rhs_direct, rhs_adjoint, diag_shift, flame_gain, ref_owner)
     got = lax.ppermute(give, "flame", swap)
     edge = arr(5, half * HALO, width)
     first_rows, last_rows = _call(edges_kernel, (edge, edge), 2, name="edges")(scal, keep, got)
@@ -307,42 +331,37 @@
     after = lax.ppermute(first_rows, "block", [(i + 1, i) for i in range(blocks - 1)])
 
     field, plane = arr(half, rows, width), arr(2, rows, width)
-    message = arr(2 * blocks, 4, LANES)
-    bd, ba, gain, inverse, owner, direct, adjoint, inner, outer = _call(
+    full = pltpu.VMEM((half, rows, width), jnp.float32)
+    split = [pltpu.VMEM((half * axial * 8, LANES), jnp.float32)] * (width // LANES)
+    moving = (field, field, plane, plane, arr(2 * blocks, 4, LANES))
+    owners = arr(half, rows, width, dtype=jnp.int32)
+    hot = arr(half * axial, LANES, width, dtype=jnp.bfloat16)
+    bd, ba, gain, inverse, owner, hot, direct, adjoint, inner, outer, sent = _call(
         functools.partial(init_kernel, blocks=blocks),
-        (field,) * 4 + (arr(half, rows, width, dtype=jnp.int32), field, field, plane, plane),
-        4, [pltpu.VMEM((half, rows, width), jnp.float32)] * 2, name="init",
+        (field, field, field, field, owners, hot) + moving, 4, [full, full] + split, name="init",
     )(scal, keep, got, before, after)
-    step = _call(step_kernel, (field, field, plane, plane), 10, name="step")
-    last = _call(
-        last_kernel, (arr(2, half, axial, radial), arr(2, half, axial, radial), message), 10,
-        [pltpu.VMEM((half, rows, width), jnp.float32)] * 2, name="last",
-    )
-    collect = _call(
-        collect_kernel, message, 4,
-        [pltpu.VMEM((half * axial * 8, LANES), jnp.float32)] * (width // LANES), name="collect",
-    )
+    step = _call(step_kernel, moving, 11, split, name="step")
+    cut = arr(2, half, axial, radial)
+    everyone = 2 * blocks * sectors
+    last = _call(last_kernel, (cut, cut, arr(everyone, LANES)), 10, [full, full], name="last")
     for sweep in range(ITERS):
         outer_in = lax.ppermute(outer, ("sector", "flame"), ring)
         inner_in = lax.ppermute(inner, "flame", swap)
-        sent = collect(scal, direct, adjoint, gain, owner)
         recv = lax.all_to_all(sent, BF, 0, 0, tiled=True)
         args = (scal, recv, inner_in, outer_in, direct, adjoint, bd, ba, gain, inverse, owner)
         if sweep < ITERS - 1:
-            direct, adjoint, inner, outer = step(*args)
+            direct, adjoint, inner, outer, sent = step(*args, hot)
         else:
             keep, give, sent = last(*args)
 
     got = lax.ppermute(give, "flame", swap)
-    recv = lax.all_to_all(sent, BF, 0, 0, tiled=True)
-    squares = _call(squares_kernel, arr(sectors, 2, LANES), 1, name="squares")(scal, recv)
-    squares = lax.all_to_all(squares, "sector", 0, 0, tiled=True)
+    recv = lax.all_to_all(sent, ("sector",) + BF, 0, 0, tiled=True)
     out = arr(planes, axial, radial)
-    cells = planes * axial * radial * sectors * blocks * 2
+    cells = planes * axial * radial * everyone
     return tuple(
-        _call(functools.partial(fields_kernel, cells=cells), (out, out), 6, name="fields")(
-            scal, recv, squares, keep, got, flame_gain, ref_owner
-        )
+        _call(
+            functools.partial(fields_kernel, cells=cells, group=2 * blocks), (out, out), 5, name="fields"
+        )(scal, recv, keep, got, flame_gain, ref_owner)
     )
 
 

time: 208 us -> 201 us (0.966)
  Pallas kernels: 29.7 us -> 24 us
  waiting for transfers between devices: 25.9 us -> 20.2 us
  blocking collectives: 79.5 us -> 84.4 us
    all_to_all x2 -> x1, waiting for transfers between devices: 16.9 us -> 10.3 us  [on_device(): recv = lax.all_to_all(sent, ('sector',) + BF, 0, 0, tiled=True)]
    pallas_call x15 -> x8, Pallas kernels: 27.5 us -> 21.6 us  [the longest x5 15.2 us: on_device(): direct, adjoint, inner, outer, sent = step(*args, hot)]
    all_to_all x6, blocking collectives: 79.5 us -> 84.4 us  [on_device(): recv = lax.all_to_all(sent, BF, 0, 0, tiled=True)]
    ppermute x2, starting transfers between devices: 11 us -> 15 us  [on_device(): got = lax.ppermute(give, 'flame', swap)]
    all_to_all x2 -> x1, starting transfers between devices: 12.2 us -> 9.7 us  [on_device(): recv = lax.all_to_all(sent, ('sector',) + BF, 0, 0, tiled=True)]
  transfers between devices with their start and end apart: 18 -> 17, of which waited for: 5 -> 5; matrix products, arithmetic and copies ran while one was open for 0% -> 0% of each run, Pallas kernels for 9% -> 0%
where the time goes in v3:
time: 201 us; the launch traced here: 200 us
  blocking collectives  84.4 us (42%)
  starting transfers between devices  66.1 us (33%)
  Pallas kernels  24 us (12%)
  waiting for transfers between devices  20.2 us (10%)
  local copies, waits for them, and re-layouts  4.53 us (2%)
    all_to_all x6, blocking collectives, on_device(): recv = lax.all_to_all(sent, BF, 0, 0, tiled=True)  84.4 us
    ppermute x6, starting transfers between devices, on_device(): outer_in = lax.ppermute(outer, ('sector', 'flame'), ring)  24.2 us
    pallas_call x5, Pallas kernels, on_device(): direct, adjoint, inner, outer, sent = step(*args, hot)  15.2 us
    ppermute x2, starting transfers between devices, on_device(): got = lax.ppermute(give, 'flame', swap)  15 us
    ppermute x6, starting transfers between devices, on_device(): inner_in = lax.ppermute(inner, 'flame', swap)  14.6 us
    all_to_all x1, waiting for transfers between devices, on_device(): recv = lax.all_to_all(sent, ('sector',) + BF, 0, 0, tiled=True)  10.3 us
    all_to_all x1, starting transfers between devices, on_device(): recv = lax.all_to_all(sent, ('sector',) + BF, 0, 0, tiled=True)  9.7 us
    unnamed x14, local copies, waits for them, and re-layouts  4.53 us
  transfers between devices with their start and end apart: 17, of which 5 were waited for; matrix products, arithmetic and copies ran while one was open for 0% of the time, Pallas kernels for 0%

profile of v3, /device:TPU:1, one launch (start us, length us, event | category | flops | bytes accessed | tf_op | source)
XLA Modules:
  0.0 200.2 jit_solution(7304622994591064840)
XLA Ops:
  7.1 8.7 %collective-permute-start = (f32[5,4,16,256]{3,2,1,0:T(8,128)S(1)}, f32[5,4,16,256]{3,2,1,0:T(8,128)S(1)}, u32[]{:S(2)}, u32[]{:S(2)}) collective-permute-start(f32[5,4,16,256]{3,2,1,0:T(8,128)S(1)} %get-tuple-element.46), channel_id=1, source_target_pairs={{0,1},{1,0},{2,3},{3,2},{4,5},{5,4},{6,7},{7,6},{8,9},{9,8},{10,11... | collective-permute-start | bytes 983048 | tf_op jit(solution)/shard_map/ppermute | solution.py:327
  20.3 3.9 %collective-permute-done.1.before_ref = f32[5,24,512]{2,1,0:T(8,128)S(1)} collective-permute-done((f32[5,24,512]{2,1,0:T(8,128)S(1)}, f32[5,24,512]{2,1,0:T(8,128)S(1)}, u32[]{:S(2)}, u32[]{:S(2)}) %collective-permute-start.1) | collective-permute-done | bytes 245792 | tf_op jit(solution)/shard_map/ppermute | solution.py:330
  24.2 3.8 %collective-permute-done.2.after_ref = f32[5,24,512]{2,1,0:T(8,128)S(1)} collective-permute-done((f32[5,24,512]{2,1,0:T(8,128)S(1)}, f32[5,24,512]{2,1,0:T(8,128)S(1)}, u32[]{:S(2)}, u32[]{:S(2)}) %collective-permute-start.2) | collective-permute-done | bytes 245792 | tf_op jit(solution)/shard_map/ppermute | solution.py:331
  28.1 3.0 %init.1 = (f32[4,32,512]{2,1,0:T(8,128)S(1)}, f32[4,32,512]{2,1,0:T(8,128)S(1)}, f32[4,32,512]{2,1,0:T(8,128)S(1)}, f32[4,32,512]{2,1,0:T(8,128)S(1)}, s32[4,32,...) custom-call(s32[3]{0:T(128)S(1)} %pad_add_fusion.scal_ref, ...), custom_call_target="tpu_custom_call" | custom-call | tf_op jit(solution)/shard_map/init/pallas_call | solution.py:339
  31.1 3.1 %collective-permute-start.3 = (f32[2,32,512]{2,1,0:T(8,128)S(1)}, f32[2,32,512]{2,1,0:T(8,128)S(1)}, u32[]{:S(2)}, u32[]{:S(2)}) collective-permute-start(f32[2,32,512]{2,1,0:T(8,128)S(1)} %get-tuple-element.50), channel_id=1, source_target_pairs={{0,1},{1,0},{2,3},{3,2},{4,5},{5,4},{6,7},{7,6},{8,9},{9,8},{10,11... | collective-permute-start | bytes 393224 | tf_op jit(solution)/shard_map/ppermute | solution.py:349
  34.2 7.0 %collective-permute-start.4 = (f32[2,32,512]{2,1,0:T(8,128)S(1)}, f32[2,32,512]{2,1,0:T(8,128)S(1)}, u32[]{:S(2)}, u32[]{:S(2)}) collective-permute-start(f32[2,32,512]{2,1,0:T(8,128)S(1)} %get-tuple-element.51), channel_id=1, source_target_pairs={{0,481},{32,1},{64,33},{96,65},{128,97},{160,129},{192,161},{224,1... | collective-permute-start | bytes 393224 | tf_op jit(solution)/shard_map/ppermute | solution.py:348
  41.3 18.9 %all_to_all.41.refs_0_ = f32[32,4,128]{2,1,0:T(4,128)S(1)} all-to-all(f32[32,4,128]{2,1,0:T(4,128)S(1)} %get-tuple-element.49), channel_id=1, replica_groups=mesh['sector'=16,'block'=16,'flame'=2] {'block','flame'}, dimensions={0} | all-to-all | bytes 131072 | tf_op jit(solution)/shard_map/all_to_all | solution.py:350
  60.2 3.0 %step.5 = (f32[4,32,512]{2,1,0:T(8,128)S(1)}, f32[4,32,512]{2,1,0:T(8,128)S(1)}, f32[2,32,512]{2,1,0:T(8,128)S(1)}, f32[2,32,512]{2,1,0:T(8,128)S(1)}, f32[32,4,128]{2,1,0:T(4,128)S(1)}) custom-call(s32[3]{0:T(128)S(1)} %pad_add_fusion.scal_ref, f32[32,4,128]{2,1,0:T(4,128)S(1)} %all_to_all.41.refs_0_, f32[2,32,512]{2,1,0:T(8,128)S(1)} %collective-permute-done.3.refs_1_, ...), custom_call_target="tpu_custom_call" | custom-call | tf_op jit(solution)/shard_map/step/pallas_call | solution.py:353
  67.5 13.5 %all_to_all.42.refs_0_ = f32[32,4,128]{2,1,0:T(4,128)S(1)} all-to-all(f32[32,4,128]{2,1,0:T(4,128)S(1)} %get-tuple-element.60), channel_id=1, replica_groups=mesh['sector'=16,'block'=16,'flame'=2] {'block','flame'}, dimensions={0} | all-to-all | bytes 131072 | tf_op jit(solution)/shard_map/all_to_all | solution.py:350
  81.0 3.0 %step.6 = (f32[4,32,512]{2,1,0:T(8,128)S(1)}, f32[4,32,512]{2,1,0:T(8,128)S(1)}, f32[2,32,512]{2,1,0:T(8,128)S(1)}, f32[2,32,512]{2,1,0:T(8,128)S(1)}, f32[32,4,128]{2,1,0:T(4,128)S(1)}) custom-call(s32[3]{0:T(128)S(1)} %pad_add_fusion.scal_ref, f32[32,4,128]{2,1,0:T(4,128)S(1)} %all_to_all.42.refs_0_, f32[2,32,512]{2,1,0:T(8,128)S(1)} %collective-permute-done.5.refs_1_, ...), custom_call_target="tpu_custom_call" | custom-call | tf_op jit(solution)/shard_map/step/pallas_call | solution.py:353
  86.2 4.9 %collective-permute-start.8 = (f32[2,32,512]{2,1,0:T(8,128)S(1)}, f32[2,32,512]{2,1,0:T(8,128)S(1)}, u32[]{:S(2)}, u32[]{:S(2)}) collective-permute-start(f32[2,32,512]{2,1,0:T(8,128)S(1)} %get-tuple-element.67), channel_id=1, source_target_pairs={{0,481},{32,1},{64,33},{96,65},{128,97},{160,129},{192,161},{224,1... | collective-permute-start | bytes 393224 | tf_op jit(solution)/shard_map/ppermute | solution.py:348
  91.1 12.8 %all_to_all.43.refs_0_ = f32[32,4,128]{2,1,0:T(4,128)S(1)} all-to-all(f32[32,4,128]{2,1,0:T(4,128)S(1)} %get-tuple-element.65), channel_id=1, replica_groups=mesh['sector'=16,'block'=16,'flame'=2] {'block','flame'}, dimensions={0} | all-to-all | bytes 131072 | tf_op jit(solution)/shard_map/all_to_all | solution.py:350
  103.9 3.0 %step.7 = (f32[4,32,512]{2,1,0:T(8,128)S(1)}, f32[4,32,512]{2,1,0:T(8,128)S(1)}, f32[2,32,512]{2,1,0:T(8,128)S(1)}, f32[2,32,512]{2,1,0:T(8,128)S(1)}, f32[32,4,128]{2,1,0:T(4,128)S(1)}) custom-call(s32[3]{0:T(128)S(1)} %pad_add_fusion.scal_ref, f32[32,4,128]{2,1,0:T(4,128)S(1)} %all_to_all.43.refs_0_, f32[2,32,512]{2,1,0:T(8,128)S(1)} %collective-permute-done.7.refs_1_, ...), custom_call_target="tpu_custom_call" | custom-call | tf_op jit(solution)/shard_map/step/pallas_call | solution.py:353
  109.2 2.9 %collective-permute-start.10 = (f32[2,32,512]{2,1,0:T(8,128)S(1)}, f32[2,32,512]{2,1,0:T(8,128)S(1)}, u32[]{:S(2)}, u32[]{:S(2)}) collective-permute-start(f32[2,32,512]{2,1,0:T(8,128)S(1)} %get-tuple-element.72), channel_id=1, source_target_pairs={{0,481},{32,1},{64,33},{96,65},{128,97},{160,129},{192,161},{224,1... | collective-permute-start | bytes 393224 | tf_op jit(solution)/shard_map/ppermute | solution.py:348
  112.1 13.3 %all_to_all.44.refs_0_ = f32[32,4,128]{2,1,0:T(4,128)S(1)} all-to-all(f32[32,4,128]{2,1,0:T(4,128)S(1)} %get-tuple-element.70), channel_id=1, replica_groups=mesh['sector'=16,'block'=16,'flame'=2] {'block','flame'}, dimensions={0} | all-to-all | bytes 131072 | tf_op jit(solution)/shard_map/all_to_all | solution.py:350
  125.4 3.0 %step.8 = (f32[4,32,512]{2,1,0:T(8,128)S(1)}, f32[4,32,512]{2,1,0:T(8,128)S(1)}, f32[2,32,512]{2,1,0:T(8,128)S(1)}, f32[2,32,512]{2,1,0:T(8,128)S(1)}, f32[32,4,128]{2,1,0:T(4,128)S(1)}) custom-call(s32[3]{0:T(128)S(1)} %pad_add_fusion.scal_ref, f32[32,4,128]{2,1,0:T(4,128)S(1)} %all_to_all.44.refs_0_, f32[2,32,512]{2,1,0:T(8,128)S(1)} %collective-permute-done.9.refs_1_, ...), custom_call_target="tpu_custom_call" | custom-call | tf_op jit(solution)/shard_map/step/pallas_call | solution.py:353
  130.9 3.9 %collective-permute-start.12 = (f32[2,32,512]{2,1,0:T(8,128)S(1)}, f32[2,32,512]{2,1,0:T(8,128)S(1)}, u32[]{:S(2)}, u32[]{:S(2)}) collective-permute-start(f32[2,32,512]{2,1,0:T(8,128)S(1)} %get-tuple-element.77), channel_id=1, source_target_pairs={{0,481},{32,1},{64,33},{96,65},{128,97},{160,129},{192,161},{224,1... | collective-permute-start | bytes 393224 | tf_op jit(solution)/shard_map/ppermute | solution.py:348
  134.9 12.8 %all_to_all.45.refs_0_ = f32[32,4,128]{2,1,0:T(4,128)S(1)} all-to-all(f32[32,4,128]{2,1,0:T(4,128)S(1)} %get-tuple-element.75), channel_id=1, replica_groups=mesh['sector'=16,'block'=16,'flame'=2] {'block','flame'}, dimensions={0} | all-to-all | bytes 131072 | tf_op jit(solution)/shard_map/all_to_all | solution.py:350
  147.7 3.0 %step.9 = (f32[4,32,512]{2,1,0:T(8,128)S(1)}, f32[4,32,512]{2,1,0:T(8,128)S(1)}, f32[2,32,512]{2,1,0:T(8,128)S(1)}, f32[2,32,512]{2,1,0:T(8,128)S(1)}, f32[32,4,128]{2,1,0:T(4,128)S(1)}) custom-call(s32[3]{0:T(128)S(1)} %pad_add_fusion.scal_ref, f32[32,4,128]{2,1,0:T(4,128)S(1)} %all_to_all.45.refs_0_, f32[2,32,512]{2,1,0:T(8,128)S(1)} %collective-permute-done.11.refs_1_, ...), custom_call_target="tpu_custom_call" | custom-call | tf_op jit(solution)/shard_map/step/pallas_call | solution.py:353
  153.0 3.6 %collective-permute-start.14 = (f32[2,32,512]{2,1,0:T(8,128)S(1)}, f32[2,32,512]{2,1,0:T(8,128)S(1)}, u32[]{:S(2)}, u32[]{:S(2)}) collective-permute-start(f32[2,32,512]{2,1,0:T(8,128)S(1)} %get-tuple-element.82), channel_id=1, source_target_pairs={{0,481},{32,1},{64,33},{96,65},{128,97},{160,129},{192,161},{224,1... | collective-permute-start | bytes 393224 | tf_op jit(solution)/shard_map/ppermute | solution.py:348
  156.6 13.1 %all_to_all.46.refs_0_ = f32[32,4,128]{2,1,0:T(4,128)S(1)} all-to-all(f32[32,4,128]{2,1,0:T(4,128)S(1)} %get-tuple-element.80), channel_id=1, replica_groups=mesh['sector'=16,'block'=16,'flame'=2] {'block','flame'}, dimensions={0} | all-to-all | bytes 131072 | tf_op jit(solution)/shard_map/all_to_all | solution.py:350
  171.5 9.7 %all-to-all-start.6 = ((f32[512,1,128]{2,1,0:T(1,128)}), f32[512,1,128]{2,1,0:T(1,128)S(1)}, u32[]{:S(2)}, u32[]{:S(2)}) async-start(f32[512,1,128]{2,1,0:T(1,128)} %bitcast.4), calls=%async_computation.6 | async-start | bytes 524288 | tf_op jit(solution)/shard_map/all_to_all | solution.py:358
  181.2 6.2 %collective-permute-start.15 = (f32[2,4,16,256]{3,2,1,0:T(8,128)S(1)}, f32[2,4,16,256]{3,2,1,0:T(8,128)S(1)}, u32[]{:S(2)}, u32[]{:S(2)}) collective-permute-start(f32[2,4,16,256]{3,2,1,0:T(8,128)S(1)} %get-tuple-element.87), channel_id=1, source_target_pairs={{0,1},{1,0},{2,3},{3,2},{4,5},{5,4},{6,7},{7,6},{8,9},{9,8},{10,11... | collective-permute-start | bytes 393224 | tf_op jit(solution)/shard_map/ppermute | solution.py:357
  188.4 10.3 %all-to-all-done.6 = f32[512,1,128]{2,1,0:T(1,128)S(1)} async-done(((f32[512,1,128]{2,1,0:T(1,128)}), f32[512,1,128]{2,1,0:T(1,128)S(1)}, u32[]{:S(2)}, u32[]{:S(2)}) %all-to-all-start.6) | async-done | bytes 262176 | tf_op jit(solution)/shard_map/all_to_all | solution.py:358
  (41 shorter events, 28.6 us)
Async XLA Ops:
  0.7 0.9 copy-start
  1.6 0.9 copy-start.2
  2.5 0.9 copy-start.4
  3.4 0.9 copy-start.5
  4.3 0.9 copy-start.6
  7.1 10.0 %collective-permute-start = (f32[5,4,16,256]{3,2,1,0:T(8,128)S(1)}, f32[5,4,16,256]{3,2,1,0:T(8,128)S(1)}, u32[]{:S(2)}, u32[]{:S(2)}) collective-permute-start(f32[5,4,16,256]{3,2,1,0:T(8,128)S(1)} %get-tuple-element.46), channel_id=1, source_target_pairs={{0,1},{1,0},{2,3},{3,2},{4,5},{5,4},{6,7},{7,6},{8,9},{9,8},{10,11... | collective-permute-start | bytes 983048 | tf_op jit(solution)/shard_map/ppermute | solution.py:327
  17.7 6.5 %collective-permute-start.1 = (f32[5,24,512]{2,1,0:T(8,128)S(1)}, f32[5,24,512]{2,1,0:T(8,128)S(1)}, u32[]{:S(2)}, u32[]{:S(2)}) collective-permute-start(f32[5,24,512]{2,1,0:T(8,128)S(1)} %get-tuple-element.47), channel_id=1, source_target_pairs={{0,2},{2,4},{4,6},{6,8},{8,10},{10,12},{12,14},{14,16},{16,18},{18... | collective-permute-start | bytes 737288 | tf_op jit(solution)/shard_map/ppermute | solution.py:330
  19.0 9.0 %collective-permute-start.2 = (f32[5,24,512]{2,1,0:T(8,128)S(1)}, f32[5,24,512]{2,1,0:T(8,128)S(1)}, u32[]{:S(2)}, u32[]{:S(2)}) collective-permute-start(f32[5,24,512]{2,1,0:T(8,128)S(1)} %get-tuple-element.48), channel_id=1, source_target_pairs={{2,0},{4,2},{6,4},{8,6},{10,8},{12,10},{14,12},{16,14},{18,16},{20... | collective-permute-start | bytes 737288 | tf_op jit(solution)/shard_map/ppermute | solution.py:331
  31.1 29.1 %collective-permute-start.3 = (f32[2,32,512]{2,1,0:T(8,128)S(1)}, f32[2,32,512]{2,1,0:T(8,128)S(1)}, u32[]{:S(2)}, u32[]{:S(2)}) collective-permute-start(f32[2,32,512]{2,1,0:T(8,128)S(1)} %get-tuple-element.50), channel_id=1, source_target_pairs={{0,1},{1,0},{2,3},{3,2},{4,5},{5,4},{6,7},{7,6},{8,9},{9,8},{10,11... | collective-permute-start | bytes 393224 | tf_op jit(solution)/shard_map/ppermute | solution.py:349
  34.2 26.0 %collective-permute-start.4 = (f32[2,32,512]{2,1,0:T(8,128)S(1)}, f32[2,32,512]{2,1,0:T(8,128)S(1)}, u32[]{:S(2)}, u32[]{:S(2)}) collective-permute-start(f32[2,32,512]{2,1,0:T(8,128)S(1)} %get-tuple-element.51), channel_id=1, source_target_pairs={{0,481},{32,1},{64,33},{96,65},{128,97},{160,129},{192,161},{224,1... | collective-permute-start | bytes 393224 | tf_op jit(solution)/shard_map/ppermute | solution.py:348
  63.3 17.8 %collective-permute-start.5 = (f32[2,32,512]{2,1,0:T(8,128)S(1)}, f32[2,32,512]{2,1,0:T(8,128)S(1)}, u32[]{:S(2)}, u32[]{:S(2)}) collective-permute-start(f32[2,32,512]{2,1,0:T(8,128)S(1)} %get-tuple-element.61), channel_id=1, source_target_pairs={{0,1},{1,0},{2,3},{3,2},{4,5},{5,4},{6,7},{7,6},{8,9},{9,8},{10,11... | collective-permute-start | bytes 393224 | tf_op jit(solution)/shard_map/ppermute | solution.py:349
  65.6 15.4 %collective-permute-start.6 = (f32[2,32,512]{2,1,0:T(8,128)S(1)}, f32[2,32,512]{2,1,0:T(8,128)S(1)}, u32[]{:S(2)}, u32[]{:S(2)}) collective-permute-start(f32[2,32,512]{2,1,0:T(8,128)S(1)} %get-tuple-element.62), channel_id=1, source_target_pairs={{0,481},{32,1},{64,33},{96,65},{128,97},{160,129},{192,161},{224,1... | collective-permute-start | bytes 393224 | tf_op jit(solution)/shard_map/ppermute | solution.py:348
  84.1 19.8 %collective-permute-start.7 = (f32[2,32,512]{2,1,0:T(8,128)S(1)}, f32[2,32,512]{2,1,0:T(8,128)S(1)}, u32[]{:S(2)}, u32[]{:S(2)}) collective-permute-start(f32[2,32,512]{2,1,0:T(8,128)S(1)} %get-tuple-element.66), channel_id=1, source_target_pairs={{0,1},{1,0},{2,3},{3,2},{4,5},{5,4},{6,7},{7,6},{8,9},{9,8},{10,11... | collective-permute-start | bytes 393224 | tf_op jit(solution)/shard_map/ppermute | solution.py:349
  86.2 17.6 %collective-permute-start.8 = (f32[2,32,512]{2,1,0:T(8,128)S(1)}, f32[2,32,512]{2,1,0:T(8,128)S(1)}, u32[]{:S(2)}, u32[]{:S(2)}) collective-permute-start(f32[2,32,512]{2,1,0:T(8,128)S(1)} %get-tuple-element.67), channel_id=1, source_target_pairs={{0,481},{32,1},{64,33},{96,65},{128,97},{160,129},{192,161},{224,1... | collective-permute-start | bytes 393224 | tf_op jit(solution)/shard_map/ppermute | solution.py:348
  106.9 18.5 %collective-permute-start.9 = (f32[2,32,512]{2,1,0:T(8,128)S(1)}, f32[2,32,512]{2,1,0:T(8,128)S(1)}, u32[]{:S(2)}, u32[]{:S(2)}) collective-permute-start(f32[2,32,512]{2,1,0:T(8,128)S(1)} %get-tuple-element.71), channel_id=1, source_target_pairs={{0,1},{1,0},{2,3},{3,2},{4,5},{5,4},{6,7},{7,6},{8,9},{9,8},{10,11... | collective-permute-start | bytes 393224 | tf_op jit(solution)/shard_map/ppermute | solution.py:349
  109.2 16.2 %collective-permute-start.10 = (f32[2,32,512]{2,1,0:T(8,128)S(1)}, f32[2,32,512]{2,1,0:T(8,128)S(1)}, u32[]{:S(2)}, u32[]{:S(2)}) collective-permute-start(f32[2,32,512]{2,1,0:T(8,128)S(1)} %get-tuple-element.72), channel_id=1, source_target_pairs={{0,481},{32,1},{64,33},{96,65},{128,97},{160,129},{192,161},{224,1... | collective-permute-start | bytes 393224 | tf_op jit(solution)/shard_map/ppermute | solution.py:348
  128.5 70.2 %copy-start.1 = (f32[8,16,256]{2,1,0:T(8,128)S(1)}, f32[8,16,256]{2,1,0:T(8,128)}, u32[]{:S(2)}) copy-start(f32[8,16,256]{2,1,0:T(8,128)} %gain_ref.1) | copy-start | bytes 393220
  128.5 70.2 %copy-start.3 = (s32[8,16,256]{2,1,0:T(8,128)S(1)}, s32[8,16,256]{2,1,0:T(8,128)}, u32[]{:S(2)}) copy-start(s32[8,16,256]{2,1,0:T(8,128)} %own_ref.1) | copy-start | bytes 393220
  128.5 19.2 %collective-permute-start.11 = (f32[2,32,512]{2,1,0:T(8,128)S(1)}, f32[2,32,512]{2,1,0:T(8,128)S(1)}, u32[]{:S(2)}, u32[]{:S(2)}) collective-permute-start(f32[2,32,512]{2,1,0:T(8,128)S(1)} %get-tuple-element.76), channel_id=1, source_target_pairs={{0,1},{1,0},{2,3},{3,2},{4,5},{5,4},{6,7},{7,6},{8,9},{9,8},{10,11... | collective-permute-start | bytes 393224 | tf_op jit(solution)/shard_map/ppermute | solution.py:349
  130.9 16.7 %collective-permute-start.12 = (f32[2,32,512]{2,1,0:T(8,128)S(1)}, f32[2,32,512]{2,1,0:T(8,128)S(1)}, u32[]{:S(2)}, u32[]{:S(2)}) collective-permute-start(f32[2,32,512]{2,1,0:T(8,128)S(1)} %get-tuple-element.77), channel_id=1, source_target_pairs={{0,481},{32,1},{64,33},{96,65},{128,97},{160,129},{192,161},{224,1... | collective-permute-start | bytes 393224 | tf_op jit(solution)/shard_map/ppermute | solution.py:348
  150.7 19.0 %collective-permute-start.13 = (f32[2,32,512]{2,1,0:T(8,128)S(1)}, f32[2,32,512]{2,1,0:T(8,128)S(1)}, u32[]{:S(2)}, u32[]{:S(2)}) collective-permute-start(f32[2,32,512]{2,1,0:T(8,128)S(1)} %get-tuple-element.81), channel_id=1, source_target_pairs={{0,1},{1,0},{2,3},{3,2},{4,5},{5,4},{6,7},{7,6},{8,9},{9,8},{10,11... | collective-permute-start | bytes 393224 | tf_op jit(solution)/shard_map/ppermute | solution.py:349
  153.0 16.7 %collective-permute-start.14 = (f32[2,32,512]{2,1,0:T(8,128)S(1)}, f32[2,32,512]{2,1,0:T(8,128)S(1)}, u32[]{:S(2)}, u32[]{:S(2)}) collective-permute-start(f32[2,32,512]{2,1,0:T(8,128)S(1)} %get-tuple-element.82), channel_id=1, source_target_pairs={{0,481},{32,1},{64,33},{96,65},{128,97},{160,129},{192,161},{224,1... | collective-permute-start | bytes 393224 | tf_op jit(solution)/shard_map/ppermute | solution.py:348
  171.5 27.2 %all-to-all-start.6 = ((f32[512,1,128]{2,1,0:T(1,128)}), f32[512,1,128]{2,1,0:T(1,128)S(1)}, u32[]{:S(2)}, u32[]{:S(2)}) async-start(f32[512,1,128]{2,1,0:T(1,128)} %bitcast.4), calls=%async_computation.6 | async-start | bytes 524288 | tf_op jit(solution)/shard_map/all_to_all | solution.py:358
  181.2 7.2 %collective-permute-start.15 = (f32[2,4,16,256]{3,2,1,0:T(8,128)S(1)}, f32[2,4,16,256]{3,2,1,0:T(8,128)S(1)}, u32[]{:S(2)}, u32[]{:S(2)}) collective-permute-start(f32[2,4,16,256]{3,2,1,0:T(8,128)S(1)} %get-tuple-element.87), channel_id=1, source_target_pairs={{0,1},{1,0},{2,3},{3,2},{4,5},{5,4},{6,7},{7,6},{8,9},{9,8},{10,11... | collective-permute-start | bytes 393224 | tf_op jit(solution)/shard_map/ppermute | solution.py:357

commit v4 on v3

--- a/solution.py
+++ b/solution.py
@@ -9,6 +9,7 @@
 
 ITERS = 6
 REF_DEV = 8
+INNER = 3
 PAD = 8
 HALO = 6
 LANES = 128
@@ -19,7 +20,7 @@
 def _call(kernel, out_shape, n_in, scratch=(), name=None, space=pltpu.VMEM):
     vmem = pl.BlockSpec(memory_space=pltpu.VMEM)
     single = not isinstance(out_shape, (tuple, list))
-    return pl.pallas_call(
+    call = pl.pallas_call(
         kernel,
         out_shape=out_shape,
         in_specs=[pl.BlockSpec(memory_space=pltpu.SMEM)] + [pl.BlockSpec(memory_space=space)] * n_in,
@@ -29,6 +30,11 @@
         name=name,
         compiler_params=pltpu.CompilerParams(vmem_limit_bytes=24 << 20),
     )
+    if space is pltpu.VMEM or INTERPRET:
+        return call
+    return lambda scal, *args: call(
+        scal, *(pltpu.with_memory_space_constraint(x, space) for x in args)
+    )
 
 
 def _lookup(table, owner):
@@ -39,12 +45,6 @@
 
 def _table(total, row):
     return [jnp.broadcast_to(total[row + j : row + j + 1], (8, LANES)) for j in (0, 1)]
-
-
-def _send_planes(refs, inner_ref, outer_ref):
-    for i, ref in enumerate(refs):
-        inner_ref[i] = ref[ref.shape[0] - 1]
-        outer_ref[i] = ref[0]
 
 
 def pack_kernel(scal_ref, *refs):
@@ -80,8 +80,30 @@
                 ref[i, to, radial:] = jnp.where(core == 0, other, mine)
 
 
-def init_kernel(scal_ref, keep_ref, got_ref, before_ref, after_ref, bd_ref, ba_ref, gain_ref,
-                inv_ref, own_ref, hot_ref, d_ref, a_ref, inner_ref, outer_ref, out_ref,
+def hot_kernel(scal_ref, keep_ref, got_ref, hot_ref):
+    core = scal_ref[0]
+    count, half, axial, radial = keep_ref.shape
+    ids = lax.broadcasted_iota(jnp.int32, (16, radial), 0).astype(jnp.float32)
+    one = jnp.ones((16, radial), jnp.bfloat16)
+    zero = jnp.zeros((16, radial), jnp.bfloat16)
+    groups = [(ids + 16.0 * g).astype(jnp.bfloat16) for g in range(LANES // 16)]
+    for p in range(half):
+        for t in range(axial // 8):
+            mine, other = (r[count - 1, p, 8 * t : 8 * t + 8] for r in (keep_ref, got_ref))
+            for h in (0, 1):
+                owner = jnp.where(core == h, mine, other)
+                low = jnp.where(owner >= LANES, owner - LANES, owner)
+                for x in range(8):
+                    line = jnp.broadcast_to(low[x : x + 1], (16, radial)).astype(jnp.bfloat16)
+                    for g, group in enumerate(groups):
+                        hot_ref[
+                            (p * (axial // 8) + t) * 8 + x, 16 * g : 16 * g + 16,
+                            radial * h : radial * (h + 1),
+                        ] = jnp.where(line == group, one, zero)
+
+
+def init_kernel(scal_ref, keep_ref, got_ref, before_ref, after_ref, hot_ref, bd_ref, ba_ref, gain_ref,
+                inv_ref, own_ref, d_ref, a_ref, inner_ref, outer_ref, out_ref,
                 shift_ref, id_ref, *split_refs, blocks):
     core, block = scal_ref[0], scal_ref[1]
     _, half, axial, radial = keep_ref.shape
@@ -107,32 +129,40 @@
             own_ref[at] = id_ref[at].astype(jnp.int32)
             d_ref[at] = bd_ref[at] * inv
             a_ref[at] = ba_ref[at] * inv
-    _send_planes((d_ref, a_ref), inner_ref, outer_ref)
-    width = 2 * radial
-    ids = lax.broadcasted_iota(jnp.int32, (16, width), 0).astype(jnp.float32)
-    one = jnp.ones((16, width), jnp.bfloat16)
-    zero = jnp.zeros((16, width), jnp.bfloat16)
-    for p in range(half):
-        for t in range(axial // 8):
-            low = (own_ref[p, PAD + 8 * t : PAD + 8 * t + 8] & (LANES - 1)).astype(jnp.float32)
-            for x in range(8):
-                line = jnp.broadcast_to(low[x : x + 1], (16, width)).astype(jnp.bfloat16)
-                for g in range(LANES // 16):
-                    hit = line == (ids + 16.0 * g).astype(jnp.bfloat16)
-                    hot_ref[(p * (axial // 8) + t) * 8 + x, 16 * g : 16 * g + 16] = jnp.where(hit, one, zero)
+    for i, ref in enumerate((bd_ref, ba_ref, inv_ref, gain_ref, id_ref)):
+        for depth in range(INNER):
+            inner_ref[i, depth] = ref[half - 1 - depth]
+    _send(outer_ref, d_ref, a_ref)
     _collect(scal_ref, d_ref, a_ref, gain_ref, own_ref, hot_ref, out_ref, split_refs)
 
 
-def step_kernel(scal_ref, *refs):
-    ins, hot_ref, refs = refs[:10], refs[10], refs[11:]
-    (dn_ref, an_ref, inner_out, outer_out, out_ref), split_refs = refs[:5], refs[5:]
-    _sweep(scal_ref, *ins, dn_ref, an_ref)
-    _send_planes((dn_ref, an_ref), inner_out, outer_out)
-    _collect(scal_ref, dn_ref, an_ref, ins[7], ins[9], hot_ref, out_ref, split_refs)
-
-
-def _sweep(scal_ref, recv_ref, inner_ref, outer_ref, d_ref, a_ref, bd_ref, ba_ref, gain_ref,
-           inv_ref, own_ref, dn_ref, an_ref):
+def _send(outer_ref, d_ref, a_ref):
+    outer_ref[0] = d_ref[0]
+    outer_ref[1] = a_ref[0]
+
+
+def step_kernel(scal_ref, *refs, extra, first):
+    refs = list(refs)
+    ins = [refs.pop(0) for _ in range(10)]
+    halo_ref = None if first else refs.pop(0)
+    hot_ref = refs.pop(0)
+    dn_ref, an_ref, hn_ref, outer_ref, out_ref = [refs.pop(0) for _ in range(5)]
+    if first:
+        halo_ref = refs.pop(0)
+        for i in (0, 1):
+            for depth in range(INNER):
+                halo_ref[i, depth] = ins[9][i, depth] * ins[9][2, depth]
+    _sweep(scal_ref, *ins, halo_ref, dn_ref, an_ref, hn_ref, extra)
+    if not extra:
+        for i, ref in enumerate((dn_ref, an_ref)):
+            for depth in range(INNER):
+                hn_ref[i, depth] = ref[ref.shape[0] - 1 - depth]
+    _send(outer_ref, dn_ref, an_ref)
+    _collect(scal_ref, dn_ref, an_ref, ins[6], ins[8], hot_ref, out_ref, refs)
+
+
+def _sweep(scal_ref, recv_ref, outer_ref, d_ref, a_ref, bd_ref, ba_ref, gain_ref,
+           inv_ref, own_ref, deep_ref, halo_ref, dn_ref, an_ref, hn_ref, extra, pad=0):
     core, block = scal_ref[0], scal_ref[1]
     planes, rows, width = d_ref.shape
     tiles = rows // 8
@@ -154,40 +184,48 @@
             parts.append(jnp.where(spot, got, 0.0))
         return jnp.concatenate(parts, axis=1)
 
+    def plane(ref, field, p, rng):
+        if p < 0:
+            return outer_ref[field, rng]
+        return ref[p, rng] if p < planes else halo_ref[field, p - planes, rng]
+
     def near(ref, field, p, t):
         rng = slice(8 * t, 8 * t + 8)
-        here = ref[p, rng]
-        below = outer_ref[field, rng] if p == 0 else ref[p - 1, rng]
-        above = inner_ref[field, rng] if p == planes - 1 else ref[p + 1, rng]
+        here = plane(ref, field, p, rng)
+        below, above = plane(ref, field, p - 1, rng), plane(ref, field, p + 1, rng)
         if t == 0:
             back = pltpu.roll(here, 1, 0)
         else:
-            back = ref[p, 8 * t - 1 : 8 * t + 7]
+            back = plane(ref, field, p, slice(8 * t - 1, 8 * t + 7))
         if t == tiles - 1:
             front = pltpu.roll(here, 7, 0)
         else:
-            front = ref[p, 8 * t + 1 : 8 * t + 9]
+            front = plane(ref, field, p, slice(8 * t + 1, 8 * t + 9))
         left = jnp.where(first, 0.0, pltpu.roll(here, 1, 1))
         right = jnp.where(last, 0.0, pltpu.roll(here, width - 1, 1))
         return (below + above) + (back + front) + (left + right)
 
-    for p in range(planes):
-        for t in range(tiles):
-            at = (p, slice(8 * t, 8 * t + 8))
-            inv = inv_ref[at]
-            own = own_ref[at]
+    for p in range(planes + extra):
+        for t in range(pad // 8, tiles - pad // 8):
+            rng = slice(8 * t, 8 * t + 8)
+            if p < planes:
+                to_d, to_a = dn_ref.at[p, rng], an_ref.at[p, rng]
+                bd, ba, gain, inv, own = (r[p, rng] for r in (bd_ref, ba_ref, gain_ref, inv_ref, own_ref))
+            else:
+                to_d, to_a = hn_ref.at[0, p - planes, rng], hn_ref.at[1, p - planes, rng]
+                bd, ba, inv, gain, own = (deep_ref[i, p - planes, rng] for i in range(5))
+                own = own.astype(jnp.int32)
             looked = jnp.concatenate(
                 [_lookup(table, own[:, LANES * j : LANES * (j + 1)]) for j in range(width // LANES)],
                 axis=1,
             )
-            flame = gain_ref[at] * looked
-            dn_ref[at] = (bd_ref[at] + near(d_ref, 0, p, t) + flame) * inv
-            acc = ba_ref[at] + near(a_ref, 1, p, t)
+            to_d[...] = (bd + near(d_ref, 0, p, t) + gain * looked) * inv
+            acc = ba + near(a_ref, 1, p, t)
             if p == 0 and t == PAD // 8:
                 acc = acc + source(block)
             if p == 0 and t == tiles - PAD // 8:
                 acc = acc + source(block + 1)
-            an_ref[at] = acc * inv
+            to_a[...] = acc * inv
 
 
 def _ref_values(d_ref):
@@ -248,7 +286,7 @@
 def last_kernel(scal_ref, *refs):
     ins, (keep_ref, give_ref, out_ref, dn_ref, an_ref) = refs[:-5], refs[-5:]
     core, block = scal_ref[0], scal_ref[1]
-    _sweep(scal_ref, *ins, dn_ref, an_ref)
+    _sweep(scal_ref, *ins, dn_ref, an_ref, None, 0, PAD)
     planes, rows, width = dn_ref.shape
     radial = width // 2
     lane, values = _ref_values(dn_ref)
@@ -333,26 +371,40 @@
     field, plane = arr(half, rows, width), arr(2, rows, width)
     full = pltpu.VMEM((half, rows, width), jnp.float32)
     split = [pltpu.VMEM((half * axial * 8, LANES), jnp.float32)] * (width // LANES)
-    moving = (field, field, plane, plane, arr(2 * blocks, 4, LANES))
+    message = arr(2 * blocks, 4, LANES)
     owners = arr(half, rows, width, dtype=jnp.int32)
-    hot = arr(half * axial, LANES, width, dtype=jnp.bfloat16)
-    bd, ba, gain, inverse, owner, hot, direct, adjoint, inner, outer, sent = _call(
+    hot = _call(hot_kernel, arr(half * axial, LANES, width, dtype=jnp.bfloat16), 2, name="hot")(
+        scal, keep, got
+    )
+    bd, ba, gain, inverse, owner, direct, adjoint, inner, outer, sent = _call(
         functools.partial(init_kernel, blocks=blocks),
-        (field, field, field, field, owners, hot) + moving, 4, [full, full] + split, name="init",
-    )(scal, keep, got, before, after)
-    step = _call(step_kernel, moving, 11, split, name="step")
-    cut = arr(2, half, axial, radial)
+        (field, field, field, field, owners, field, field, arr(5, INNER, rows, width), plane, message),
+        5, [full, full] + split, name="init",
+    )(scal, keep, got, before, after, hot)
+    cut, layers = arr(2, half, axial, radial), (2, INNER, rows, width)
     everyone = 2 * blocks * sectors
-    last = _call(last_kernel, (cut, cut, arr(everyone, LANES)), 10, [full, full], name="last")
+    deep = halo = None
     for sweep in range(ITERS):
         outer_in = lax.ppermute(outer, ("sector", "flame"), ring)
-        inner_in = lax.ppermute(inner, "flame", swap)
+        if sweep == 0:
+            deep = lax.ppermute(inner, "flame", swap)
+        elif sweep % INNER == 0:
+            halo = lax.ppermute(halo, "flame", swap)
         recv = lax.all_to_all(sent, BF, 0, 0, tiled=True)
-        args = (scal, recv, inner_in, outer_in, direct, adjoint, bd, ba, gain, inverse, owner)
+        args = (scal, recv, outer_in, direct, adjoint, bd, ba, gain, inverse, owner, deep)
+        args += () if halo is None else (halo,)
         if sweep < ITERS - 1:
-            direct, adjoint, inner, outer, sent = step(*args, hot)
+            step = functools.partial(
+                step_kernel, extra=INNER - 1 - sweep % INNER, first=sweep == 0
+            )
+            scratch = ([pltpu.VMEM(layers, jnp.float32)] if sweep == 0 else []) + split
+            direct, adjoint, halo, outer, sent = _call(
+                step, (field, field, arr(*layers), plane, message), len(args), scratch, name="step"
+            )(*args, hot)
         else:
-            keep, give, sent = last(*args)
+            keep, give, sent = _call(
+                last_kernel, (cut, cut, arr(everyone, LANES)), 11, [full, full], name="last"
+            )(*args)
 
     got = lax.ppermute(give, "flame", swap)
     recv = lax.all_to_all(sent, ("sector",) + BF, 0, 0, tiled=True)

time: 201 us -> 188 us (0.935)
  starting transfers between devices: 66.1 us -> 57.7 us
  local copies, waits for them, and re-layouts: 4.53 us -> 0.01 us
    ppermute x6 -> x2, starting transfers between devices: 14.6 us -> 5.44 us  [the longest x1 3.14 us: on_device(): deep = lax.ppermute(inner, 'flame', swap)]
    unnamed x14 -> x4, local copies, waits for them, and re-layouts: 4.53 us -> 0.01 us
    pallas_call x7 -> x8, Pallas kernels: 18.9 us -> 20.7 us  [the longest x5 15.5 us: on_device(): _call(step, (field, field, arr(*layers), plane, message), len(args), scra...]
  transfers between devices with their start and end apart: 17 -> 13, of which waited for: 5 -> 5; matrix products, arithmetic and copies ran while one was open for 0% -> 0% of each run, Pallas kernels for 0% -> 1%
where the time goes in v4:
time: 188 us; the launch traced here: 187 us
  blocking collectives  84.2 us (45%)
  starting transfers between devices  57.7 us (31%)
  Pallas kernels  25.9 us (14%)
  waiting for transfers between devices  18.8 us (10%)
    all_to_all x6, blocking collectives, on_device(): recv = lax.all_to_all(sent, BF, 0, 0, tiled=True)  84.2 us
    ppermute x6, starting transfers between devices, on_device(): outer_in = lax.ppermute(outer, ('sector', 'flame'), ring)  24.6 us
    pallas_call x5, Pallas kernels, on_device(): _call(step, (field, field, arr(*layers), plane, message), len(args), scra...  15.5 us
    ppermute x2, starting transfers between devices, on_device(): got = lax.ppermute(give, 'flame', swap)  15 us
    all_to_all x1, waiting for transfers between devices, on_device(): recv = lax.all_to_all(sent, ('sector',) + BF, 0, 0, tiled=True)  10.3 us
    all_to_all x1, starting transfers between devices, on_device(): recv = lax.all_to_all(sent, ('sector',) + BF, 0, 0, tiled=True)  10 us
    ppermute x1, waiting for transfers between devices, on_device(): lax.ppermute(first_rows, 'block', [(i + 1, i) for i in range(blocks - 1)])  3.85 us
  transfers between devices with their start and end apart: 13, of which 5 were waited for; matrix products, arithmetic and copies ran while one was open for 0% of the time, Pallas kernels for 1%

profile of v4, /device:TPU:1, one launch (start us, length us, event | category | flops | bytes accessed | tf_op | source)
XLA Modules:
  0.0 187.4 jit_solution(5709195230665814166)
XLA Ops:
  2.7 8.7 %collective-permute-start = (f32[5,4,16,256]{3,2,1,0:T(8,128)S(1)}, f32[5,4,16,256]{3,2,1,0:T(8,128)S(1)}, u32[]{:S(2)}, u32[]{:S(2)}) collective-permute-start(f32[5,4,16,256]{3,2,1,0:T(8,128)S(1)} %get-tuple-element.45), channel_id=1, source_target_pairs={{0,1},{1,0},{2,3},{3,2},{4,5},{5,4},{6,7},{7,6},{8,9},{9,8},{10,11... | collective-permute-start | bytes 983048 | tf_op jit(solution)/shard_map/ppermute | solution.py:365
  17.3 2.4 %collective-permute-done.1.before_ref = f32[5,24,512]{2,1,0:T(8,128)S(1)} collective-permute-done((f32[5,24,512]{2,1,0:T(8,128)S(1)}, f32[5,24,512]{2,1,0:T(8,128)S(1)}, u32[]{:S(2)}, u32[]{:S(2)}) %collective-permute-start.1) | collective-permute-done | bytes 245792 | tf_op jit(solution)/shard_map/ppermute | solution.py:368
  19.8 3.8 %collective-permute-done.2.after_ref = f32[5,24,512]{2,1,0:T(8,128)S(1)} collective-permute-done((f32[5,24,512]{2,1,0:T(8,128)S(1)}, f32[5,24,512]{2,1,0:T(8,128)S(1)}, u32[]{:S(2)}, u32[]{:S(2)}) %collective-permute-start.2) | collective-permute-done | bytes 245792 | tf_op jit(solution)/shard_map/ppermute | solution.py:369
  23.6 3.1 %init.1 = (f32[4,32,512]{2,1,0:T(8,128)S(1)}, f32[4,32,512]{2,1,0:T(8,128)S(1)}, f32[4,32,512]{2,1,0:T(8,128)S(1)}, f32[4,32,512]{2,1,0:T(8,128)S(1)}, s32[4,32,...) custom-call(s32[3]{0:T(128)S(1)} %pad_add_fusion.scal_ref, ...), custom_call_target="tpu_custom_call" | custom-call | tf_op jit(solution)/shard_map/init/pallas_call | solution.py:379
  26.7 3.1 %collective-permute-start.4 = (f32[5,3,32,512]{3,2,1,0:T(8,128)S(1)}, f32[5,3,32,512]{3,2,1,0:T(8,128)S(1)}, u32[]{:S(2)}, u32[]{:S(2)}) collective-permute-start(f32[5,3,32,512]{3,2,1,0:T(8,128)S(1)} %get-tuple-element.57), channel_id=1, source_target_pairs={{0,1},{1,0},{2,3},{3,2},{4,5},{5,4},{6,7},{7,6},{8,9},{9,8},{10,11... | collective-permute-start | bytes 2949128 | tf_op jit(solution)/shard_map/ppermute | solution.py:390
  29.8 7.0 %collective-permute-start.3 = (f32[2,32,512]{2,1,0:T(8,128)S(1)}, f32[2,32,512]{2,1,0:T(8,128)S(1)}, u32[]{:S(2)}, u32[]{:S(2)}) collective-permute-start(f32[2,32,512]{2,1,0:T(8,128)S(1)} %get-tuple-element.49), channel_id=1, source_target_pairs={{0,481},{32,1},{64,33},{96,65},{128,97},{160,129},{192,161},{224,1... | collective-permute-start | bytes 393224 | tf_op jit(solution)/shard_map/ppermute | solution.py:388
  36.9 18.9 %all_to_all.41.refs_0_ = f32[32,4,128]{2,1,0:T(4,128)S(1)} all-to-all(f32[32,4,128]{2,1,0:T(4,128)S(1)} %get-tuple-element.48), channel_id=1, replica_groups=mesh['sector'=16,'block'=16,'flame'=2] {'block','flame'}, dimensions={0} | all-to-all | bytes 131072 | tf_op jit(solution)/shard_map/all_to_all | solution.py:393
  55.8 3.2 %step.5 = (f32[4,32,512]{2,1,0:T(8,128)S(1)}, f32[4,32,512]{2,1,0:T(8,128)S(1)}, f32[2,3,32,512]{3,2,1,0:T(8,128)S(1)}, f32[2,32,512]{2,1,0:T(8,128)S(1)}, f32[32,4,128]{2,1,0:T(4,128)S(1)}) custom-call(s32[3]{0:T(128)S(1)} %pad_add_fusion.scal_ref, f32[32,4,128]{2,1,0:T(4,128)S(1)} %all_to_all.41.refs_0_, f32[2,32,512]{2,1,0:T(8,128)S(1)} %collective-permute-done.3.refs_1_, ...), custom_call_target="tpu_custom_call" | custom-call | tf_op jit(solution)/shard_map/step/pallas_call | solution.py:401
  60.9 13.5 %all_to_all.42.refs_0_ = f32[32,4,128]{2,1,0:T(4,128)S(1)} all-to-all(f32[32,4,128]{2,1,0:T(4,128)S(1)} %get-tuple-element.58), channel_id=1, replica_groups=mesh['sector'=16,'block'=16,'flame'=2] {'block','flame'}, dimensions={0} | all-to-all | bytes 131072 | tf_op jit(solution)/shard_map/all_to_all | solution.py:393
  74.4 3.1 %step.6 = (f32[4,32,512]{2,1,0:T(8,128)S(1)}, f32[4,32,512]{2,1,0:T(8,128)S(1)}, f32[2,3,32,512]{3,2,1,0:T(8,128)S(1)}, f32[2,32,512]{2,1,0:T(8,128)S(1)}, f32[32,4,128]{2,1,0:T(4,128)S(1)}) custom-call(s32[3]{0:T(128)S(1)} %pad_add_fusion.scal_ref, f32[32,4,128]{2,1,0:T(4,128)S(1)} %all_to_all.42.refs_0_, f32[2,32,512]{2,1,0:T(8,128)S(1)} %collective-permute-done.5.refs_1_, ...), custom_call_target="tpu_custom_call" | custom-call | tf_op jit(solution)/shard_map/step/pallas_call | solution.py:401
  77.5 5.0 %collective-permute-start.6 = (f32[2,32,512]{2,1,0:T(8,128)S(1)}, f32[2,32,512]{2,1,0:T(8,128)S(1)}, u32[]{:S(2)}, u32[]{:S(2)}) collective-permute-start(f32[2,32,512]{2,1,0:T(8,128)S(1)} %get-tuple-element.64), channel_id=1, source_target_pairs={{0,481},{32,1},{64,33},{96,65},{128,97},{160,129},{192,161},{224,1... | collective-permute-start | bytes 393224 | tf_op jit(solution)/shard_map/ppermute | solution.py:388
  82.5 12.8 %all_to_all.43.refs_0_ = f32[32,4,128]{2,1,0:T(4,128)S(1)} all-to-all(f32[32,4,128]{2,1,0:T(4,128)S(1)} %get-tuple-element.63), channel_id=1, replica_groups=mesh['sector'=16,'block'=16,'flame'=2] {'block','flame'}, dimensions={0} | all-to-all | bytes 131072 | tf_op jit(solution)/shard_map/all_to_all | solution.py:393
  95.3 3.0 %step.7 = (f32[4,32,512]{2,1,0:T(8,128)S(1)}, f32[4,32,512]{2,1,0:T(8,128)S(1)}, f32[2,3,32,512]{3,2,1,0:T(8,128)S(1)}, f32[2,32,512]{2,1,0:T(8,128)S(1)}, f32[32,4,128]{2,1,0:T(4,128)S(1)}) custom-call(s32[3]{0:T(128)S(1)} %pad_add_fusion.scal_ref, f32[32,4,128]{2,1,0:T(4,128)S(1)} %all_to_all.43.refs_0_, f32[2,32,512]{2,1,0:T(8,128)S(1)} %collective-permute-done.6.refs_1_, ...), custom_call_target="tpu_custom_call" | custom-call | tf_op jit(solution)/shard_map/step/pallas_call | solution.py:401
  100.6 2.8 %collective-permute-start.7 = (f32[2,32,512]{2,1,0:T(8,128)S(1)}, f32[2,32,512]{2,1,0:T(8,128)S(1)}, u32[]{:S(2)}, u32[]{:S(2)}) collective-permute-start(f32[2,32,512]{2,1,0:T(8,128)S(1)} %get-tuple-element.69), channel_id=1, source_target_pairs={{0,481},{32,1},{64,33},{96,65},{128,97},{160,129},{192,161},{224,1... | collective-permute-start | bytes 393224 | tf_op jit(solution)/shard_map/ppermute | solution.py:388
  103.4 13.5 %all_to_all.44.refs_0_ = f32[32,4,128]{2,1,0:T(4,128)S(1)} all-to-all(f32[32,4,128]{2,1,0:T(4,128)S(1)} %get-tuple-element.68), channel_id=1, replica_groups=mesh['sector'=16,'block'=16,'flame'=2] {'block','flame'}, dimensions={0} | all-to-all | bytes 131072 | tf_op jit(solution)/shard_map/all_to_all | solution.py:393
  117.0 3.1 %step.8 = (f32[4,32,512]{2,1,0:T(8,128)S(1)}, f32[4,32,512]{2,1,0:T(8,128)S(1)}, f32[2,3,32,512]{3,2,1,0:T(8,128)S(1)}, f32[2,32,512]{2,1,0:T(8,128)S(1)}, f32[32,4,128]{2,1,0:T(4,128)S(1)}) custom-call(s32[3]{0:T(128)S(1)} %pad_add_fusion.scal_ref, f32[32,4,128]{2,1,0:T(4,128)S(1)} %all_to_all.44.refs_0_, f32[2,32,512]{2,1,0:T(8,128)S(1)} %collective-permute-done.7.refs_1_, ...), custom_call_target="tpu_custom_call" | custom-call | tf_op jit(solution)/shard_map/step/pallas_call | solution.py:401
  120.1 4.2 %collective-permute-start.9 = (f32[2,32,512]{2,1,0:T(8,128)S(1)}, f32[2,32,512]{2,1,0:T(8,128)S(1)}, u32[]{:S(2)}, u32[]{:S(2)}) collective-permute-start(f32[2,32,512]{2,1,0:T(8,128)S(1)} %get-tuple-element.74), channel_id=1, source_target_pairs={{0,481},{32,1},{64,33},{96,65},{128,97},{160,129},{192,161},{224,1... | collective-permute-start | bytes 393224 | tf_op jit(solution)/shard_map/ppermute | solution.py:388
  124.3 12.7 %all_to_all.45.refs_0_ = f32[32,4,128]{2,1,0:T(4,128)S(1)} all-to-all(f32[32,4,128]{2,1,0:T(4,128)S(1)} %get-tuple-element.73), channel_id=1, replica_groups=mesh['sector'=16,'block'=16,'flame'=2] {'block','flame'}, dimensions={0} | all-to-all | bytes 131072 | tf_op jit(solution)/shard_map/all_to_all | solution.py:393
  137.0 3.1 %step.9 = (f32[4,32,512]{2,1,0:T(8,128)S(1)}, f32[4,32,512]{2,1,0:T(8,128)S(1)}, f32[2,3,32,512]{3,2,1,0:T(8,128)S(1)}, f32[2,32,512]{2,1,0:T(8,128)S(1)}, f32[32,4,128]{2,1,0:T(4,128)S(1)}) custom-call(s32[3]{0:T(128)S(1)} %pad_add_fusion.scal_ref, f32[32,4,128]{2,1,0:T(4,128)S(1)} %all_to_all.45.refs_0_, f32[2,32,512]{2,1,0:T(8,128)S(1)} %collective-permute-done.9.refs_1_, ...), custom_call_target="tpu_custom_call" | custom-call | tf_op jit(solution)/shard_map/step/pallas_call | solution.py:401
  140.1 3.7 %collective-permute-start.10 = (f32[2,32,512]{2,1,0:T(8,128)S(1)}, f32[2,32,512]{2,1,0:T(8,128)S(1)}, u32[]{:S(2)}, u32[]{:S(2)}) collective-permute-start(f32[2,32,512]{2,1,0:T(8,128)S(1)} %get-tuple-element.79), channel_id=1, source_target_pairs={{0,481},{32,1},{64,33},{96,65},{128,97},{160,129},{192,161},{224,1... | collective-permute-start | bytes 393224 | tf_op jit(solution)/shard_map/ppermute | solution.py:388
  143.8 12.8 %all_to_all.46.refs_0_ = f32[32,4,128]{2,1,0:T(4,128)S(1)} all-to-all(f32[32,4,128]{2,1,0:T(4,128)S(1)} %get-tuple-element.78), channel_id=1, replica_groups=mesh['sector'=16,'block'=16,'flame'=2] {'block','flame'}, dimensions={0} | all-to-all | bytes 131072 | tf_op jit(solution)/shard_map/all_to_all | solution.py:393
  158.4 10.0 %all-to-all-start.6 = ((f32[512,1,128]{2,1,0:T(1,128)}), f32[512,1,128]{2,1,0:T(1,128)S(1)}, u32[]{:S(2)}, u32[]{:S(2)}) async-start(f32[512,1,128]{2,1,0:T(1,128)} %bitcast.4), calls=%async_computation.6 | async-start | bytes 524288 | tf_op jit(solution)/shard_map/all_to_all | solution.py:410
  168.5 6.2 %collective-permute-start.11 = (f32[2,4,16,256]{3,2,1,0:T(8,128)S(1)}, f32[2,4,16,256]{3,2,1,0:T(8,128)S(1)}, u32[]{:S(2)}, u32[]{:S(2)}) collective-permute-start(f32[2,4,16,256]{3,2,1,0:T(8,128)S(1)} %get-tuple-element.85), channel_id=1, source_target_pairs={{0,1},{1,0},{2,3},{3,2},{4,5},{5,4},{6,7},{7,6},{8,9},{9,8},{10,11... | collective-permute-start | bytes 393224 | tf_op jit(solution)/shard_map/ppermute | solution.py:409
  175.6 10.3 %all-to-all-done.6 = f32[512,1,128]{2,1,0:T(1,128)S(1)} async-done(((f32[512,1,128]{2,1,0:T(1,128)}), f32[512,1,128]{2,1,0:T(1,128)S(1)}, u32[]{:S(2)}, u32[]{:S(2)}) %all-to-all-start.6) | async-done | bytes 262176 | tf_op jit(solution)/shard_map/all_to_all | solution.py:410
  (24 shorter events, 16.5 us)
Async XLA Ops:
  2.7 10.0 %collective-permute-start = (f32[5,4,16,256]{3,2,1,0:T(8,128)S(1)}, f32[5,4,16,256]{3,2,1,0:T(8,128)S(1)}, u32[]{:S(2)}, u32[]{:S(2)}) collective-permute-start(f32[5,4,16,256]{3,2,1,0:T(8,128)S(1)} %get-tuple-element.45), channel_id=1, source_target_pairs={{0,1},{1,0},{2,3},{3,2},{4,5},{5,4},{6,7},{7,6},{8,9},{9,8},{10,11... | collective-permute-start | bytes 983048 | tf_op jit(solution)/shard_map/ppermute | solution.py:365
  13.3 6.5 %collective-permute-start.1 = (f32[5,24,512]{2,1,0:T(8,128)S(1)}, f32[5,24,512]{2,1,0:T(8,128)S(1)}, u32[]{:S(2)}, u32[]{:S(2)}) collective-permute-start(f32[5,24,512]{2,1,0:T(8,128)S(1)} %get-tuple-element.46), channel_id=1, source_target_pairs={{0,2},{2,4},{4,6},{6,8},{8,10},{10,12},{12,14},{14,16},{16,18},{18... | collective-permute-start | bytes 737288 | tf_op jit(solution)/shard_map/ppermute | solution.py:368
  14.6 9.0 %collective-permute-start.2 = (f32[5,24,512]{2,1,0:T(8,128)S(1)}, f32[5,24,512]{2,1,0:T(8,128)S(1)}, u32[]{:S(2)}, u32[]{:S(2)}) collective-permute-start(f32[5,24,512]{2,1,0:T(8,128)S(1)} %get-tuple-element.47), channel_id=1, source_target_pairs={{2,0},{4,2},{6,4},{8,6},{10,8},{12,10},{14,12},{16,14},{18,16},{20... | collective-permute-start | bytes 737288 | tf_op jit(solution)/shard_map/ppermute | solution.py:369
  26.7 29.1 %collective-permute-start.4 = (f32[5,3,32,512]{3,2,1,0:T(8,128)S(1)}, f32[5,3,32,512]{3,2,1,0:T(8,128)S(1)}, u32[]{:S(2)}, u32[]{:S(2)}) collective-permute-start(f32[5,3,32,512]{3,2,1,0:T(8,128)S(1)} %get-tuple-element.57), channel_id=1, source_target_pairs={{0,1},{1,0},{2,3},{3,2},{4,5},{5,4},{6,7},{7,6},{8,9},{9,8},{10,11... | collective-permute-start | bytes 2949128 | tf_op jit(solution)/shard_map/ppermute | solution.py:390
  29.8 26.0 %collective-permute-start.3 = (f32[2,32,512]{2,1,0:T(8,128)S(1)}, f32[2,32,512]{2,1,0:T(8,128)S(1)}, u32[]{:S(2)}, u32[]{:S(2)}) collective-permute-start(f32[2,32,512]{2,1,0:T(8,128)S(1)} %get-tuple-element.49), channel_id=1, source_target_pairs={{0,481},{32,1},{64,33},{96,65},{128,97},{160,129},{192,161},{224,1... | collective-permute-start | bytes 393224 | tf_op jit(solution)/shard_map/ppermute | solution.py:388
  59.0 15.4 %collective-permute-start.5 = (f32[2,32,512]{2,1,0:T(8,128)S(1)}, f32[2,32,512]{2,1,0:T(8,128)S(1)}, u32[]{:S(2)}, u32[]{:S(2)}) collective-permute-start(f32[2,32,512]{2,1,0:T(8,128)S(1)} %get-tuple-element.59), channel_id=1, source_target_pairs={{0,481},{32,1},{64,33},{96,65},{128,97},{160,129},{192,161},{224,1... | collective-permute-start | bytes 393224 | tf_op jit(solution)/shard_map/ppermute | solution.py:388
  77.5 17.8 %collective-permute-start.6 = (f32[2,32,512]{2,1,0:T(8,128)S(1)}, f32[2,32,512]{2,1,0:T(8,128)S(1)}, u32[]{:S(2)}, u32[]{:S(2)}) collective-permute-start(f32[2,32,512]{2,1,0:T(8,128)S(1)} %get-tuple-element.64), channel_id=1, source_target_pairs={{0,481},{32,1},{64,33},{96,65},{128,97},{160,129},{192,161},{224,1... | collective-permute-start | bytes 393224 | tf_op jit(solution)/shard_map/ppermute | solution.py:388
  98.3 18.6 %collective-permute-start.8 = (f32[2,3,32,512]{3,2,1,0:T(8,128)S(1)}, f32[2,3,32,512]{3,2,1,0:T(8,128)S(1)}, u32[]{:S(2)}, u32[]{:S(2)}) collective-permute-start(f32[2,3,32,512]{3,2,1,0:T(8,128)S(1)} %get-tuple-element.72), channel_id=1, source_target_pairs={{0,1},{1,0},{2,3},{3,2},{4,5},{5,4},{6,7},{7,6},{8,9},{9,8},{10,11... | collective-permute-start | bytes 1179656 | tf_op jit(solution)/shard_map/ppermute | solution.py:392
  100.6 16.3 %collective-permute-start.7 = (f32[2,32,512]{2,1,0:T(8,128)S(1)}, f32[2,32,512]{2,1,0:T(8,128)S(1)}, u32[]{:S(2)}, u32[]{:S(2)}) collective-permute-start(f32[2,32,512]{2,1,0:T(8,128)S(1)} %get-tuple-element.69), channel_id=1, source_target_pairs={{0,481},{32,1},{64,33},{96,65},{128,97},{160,129},{192,161},{224,1... | collective-permute-start | bytes 393224 | tf_op jit(solution)/shard_map/ppermute | solution.py:388
  120.1 65.8 %copy-start = (f32[8,16,256]{2,1,0:T(8,128)S(1)}, f32[8,16,256]{2,1,0:T(8,128)}, u32[]{:S(2)}) copy-start(f32[8,16,256]{2,1,0:T(8,128)} %gain_ref.1) | copy-start | bytes 393220
  120.1 65.8 %copy-start.1 = (s32[8,16,256]{2,1,0:T(8,128)S(1)}, s32[8,16,256]{2,1,0:T(8,128)}, u32[]{:S(2)}) copy-start(s32[8,16,256]{2,1,0:T(8,128)} %own_ref.1) | copy-start | bytes 393220
  120.1 16.9 %collective-permute-start.9 = (f32[2,32,512]{2,1,0:T(8,128)S(1)}, f32[2,32,512]{2,1,0:T(8,128)S(1)}, u32[]{:S(2)}, u32[]{:S(2)}) collective-permute-start(f32[2,32,512]{2,1,0:T(8,128)S(1)} %get-tuple-element.74), channel_id=1, source_target_pairs={{0,481},{32,1},{64,33},{96,65},{128,97},{160,129},{192,161},{224,1... | collective-permute-start | bytes 393224 | tf_op jit(solution)/shard_map/ppermute | solution.py:388
  140.1 16.5 %collective-permute-start.10 = (f32[2,32,512]{2,1,0:T(8,128)S(1)}, f32[2,32,512]{2,1,0:T(8,128)S(1)}, u32[]{:S(2)}, u32[]{:S(2)}) collective-permute-start(f32[2,32,512]{2,1,0:T(8,128)S(1)} %get-tuple-element.79), channel_id=1, source_target_pairs={{0,481},{32,1},{64,33},{96,65},{128,97},{160,129},{192,161},{224,1... | collective-permute-start | bytes 393224 | tf_op jit(solution)/shard_map/ppermute | solution.py:388
  158.4 27.5 %all-to-all-start.6 = ((f32[512,1,128]{2,1,0:T(1,128)}), f32[512,1,128]{2,1,0:T(1,128)S(1)}, u32[]{:S(2)}, u32[]{:S(2)}) async-start(f32[512,1,128]{2,1,0:T(1,128)} %bitcast.4), calls=%async_computation.6 | async-start | bytes 524288 | tf_op jit(solution)/shard_map/all_to_all | solution.py:410
  168.5 7.2 %collective-permute-start.11 = (f32[2,4,16,256]{3,2,1,0:T(8,128)S(1)}, f32[2,4,16,256]{3,2,1,0:T(8,128)S(1)}, u32[]{:S(2)}, u32[]{:S(2)}) collective-permute-start(f32[2,4,16,256]{3,2,1,0:T(8,128)S(1)} %get-tuple-element.85), channel_id=1, source_target_pairs={{0,1},{1,0},{2,3},{3,2},{4,5},{5,4},{6,7},{7,6},{8,9},{9,8},{10,11... | collective-permute-start | bytes 393224 | tf_op jit(solution)/shard_map/ppermute | solution.py:409

commit v5 on v4

--- a/solution.py
+++ b/solution.py
@@ -9,6 +9,7 @@
 
 ITERS = 6
 REF_DEV = 8
+GROUP = 16
 INNER = 3
 PAD = 8
 HALO = 6
@@ -80,31 +81,40 @@
                 ref[i, to, radial:] = jnp.where(core == 0, other, mine)
 
 
-def hot_kernel(scal_ref, keep_ref, got_ref, hot_ref):
+def hot_kernel(scal_ref, keep_ref, got_ref, high_ref, low_ref, out_ref, d_ref, a_ref, gain_ref):
     core = scal_ref[0]
     count, half, axial, radial = keep_ref.shape
-    ids = lax.broadcasted_iota(jnp.int32, (16, radial), 0).astype(jnp.float32)
-    one = jnp.ones((16, radial), jnp.bfloat16)
-    zero = jnp.zeros((16, radial), jnp.bfloat16)
-    groups = [(ids + 16.0 * g).astype(jnp.bfloat16) for g in range(LANES // 16)]
+    width = 2 * radial
+    ids = lax.broadcasted_iota(jnp.int32, (GROUP, width), 0).astype(jnp.float32)
     for p in range(half):
         for t in range(axial // 8):
-            mine, other = (r[count - 1, p, 8 * t : 8 * t + 8] for r in (keep_ref, got_ref))
-            for h in (0, 1):
-                owner = jnp.where(core == h, mine, other)
-                low = jnp.where(owner >= LANES, owner - LANES, owner)
+            rng = slice(8 * t, 8 * t + 8)
+            bd, ba, shift, gain, owner = (
+                jnp.concatenate(
+                    [jnp.where(core == h, keep_ref[i, p, rng], got_ref[i, p, rng]) for h in (0, 1)], axis=1
+                )
+                for i in range(count)
+            )
+            inv = 1.0 / (6.0 + shift)
+            if p == 0:
+                d_ref[0, rng] = bd * inv
+            a_ref[p, rng] = ba * inv
+            gain_ref[p, rng] = gain
+            owner = owner.astype(jnp.int32)
+            for part, ref in ((owner // GROUP, high_ref), (owner % GROUP, low_ref)):
+                part = part.astype(jnp.float32)
                 for x in range(8):
-                    line = jnp.broadcast_to(low[x : x + 1], (16, radial)).astype(jnp.bfloat16)
-                    for g, group in enumerate(groups):
-                        hot_ref[
-                            (p * (axial // 8) + t) * 8 + x, 16 * g : 16 * g + 16,
-                            radial * h : radial * (h + 1),
-                        ] = jnp.where(line == group, one, zero)
-
-
-def init_kernel(scal_ref, keep_ref, got_ref, before_ref, after_ref, hot_ref, bd_ref, ba_ref, gain_ref,
-                inv_ref, own_ref, d_ref, a_ref, inner_ref, outer_ref, out_ref,
-                shift_ref, id_ref, *split_refs, blocks):
+                    hit = jnp.broadcast_to(part[x : x + 1], (GROUP, width)) == ids
+                    ref[(p * (axial // 8) + t) * 8 + x] = jnp.where(hit, 1.0, 0.0).astype(jnp.bfloat16)
+    collect = _Collect(a_ref, gain_ref, high_ref, low_ref, 0)
+    for p in range(half):
+        collect.plane(p)
+    collect.finish(out_ref)
+    _write_refs(scal_ref, d_ref, out_ref, 0)
+
+
+def init_kernel(scal_ref, keep_ref, got_ref, before_ref, after_ref, bd_ref, ba_ref, gain_ref,
+                inv_ref, own_ref, d_ref, a_ref, inner_ref, outer_ref, shift_ref, id_ref, *, blocks):
     core, block = scal_ref[0], scal_ref[1]
     _, half, axial, radial = keep_ref.shape
     rows = axial + 2 * PAD
@@ -133,7 +143,6 @@
         for depth in range(INNER):
             inner_ref[i, depth] = ref[half - 1 - depth]
     _send(outer_ref, d_ref, a_ref)
-    _collect(scal_ref, d_ref, a_ref, gain_ref, own_ref, hot_ref, out_ref, split_refs)
 
 
 def _send(outer_ref, d_ref, a_ref):
@@ -145,24 +154,26 @@
     refs = list(refs)
     ins = [refs.pop(0) for _ in range(10)]
     halo_ref = None if first else refs.pop(0)
-    hot_ref = refs.pop(0)
+    high_ref, low_ref = refs.pop(0), refs.pop(0)
     dn_ref, an_ref, hn_ref, outer_ref, out_ref = [refs.pop(0) for _ in range(5)]
     if first:
         halo_ref = refs.pop(0)
         for i in (0, 1):
             for depth in range(INNER):
                 halo_ref[i, depth] = ins[9][i, depth] * ins[9][2, depth]
-    _sweep(scal_ref, *ins, halo_ref, dn_ref, an_ref, hn_ref, extra)
+    collect = _Collect(an_ref, ins[6], high_ref, low_ref, PAD)
+    _sweep(scal_ref, *ins, halo_ref, dn_ref, an_ref, hn_ref, extra, 0, collect)
     if not extra:
         for i, ref in enumerate((dn_ref, an_ref)):
             for depth in range(INNER):
                 hn_ref[i, depth] = ref[ref.shape[0] - 1 - depth]
     _send(outer_ref, dn_ref, an_ref)
-    _collect(scal_ref, dn_ref, an_ref, ins[6], ins[8], hot_ref, out_ref, refs)
+    collect.finish(out_ref)
+    _write_refs(scal_ref, dn_ref, out_ref, PAD)
 
 
 def _sweep(scal_ref, recv_ref, outer_ref, d_ref, a_ref, bd_ref, ba_ref, gain_ref,
-           inv_ref, own_ref, deep_ref, halo_ref, dn_ref, an_ref, hn_ref, extra, pad=0):
+           inv_ref, own_ref, deep_ref, halo_ref, dn_ref, an_ref, hn_ref, extra, pad=0, collect=None):
     core, block = scal_ref[0], scal_ref[1]
     planes, rows, width = d_ref.shape
     tiles = rows // 8
@@ -226,12 +237,16 @@
             if p == 0 and t == tiles - PAD // 8:
                 acc = acc + source(block + 1)
             to_a[...] = acc * inv
-
-
-def _ref_values(d_ref):
+            if collect is not None:
+                collect.some()
+        if collect is not None and p < planes:
+            collect.plane(p)
+
+
+def _ref_values(d_ref, pad=PAD):
     width = d_ref.shape[2]
     lane = lax.broadcasted_iota(jnp.int32, (8, LANES), 1)
-    row = d_ref[0, PAD : PAD + 8]
+    row = d_ref[0, pad : pad + 8]
     got = jnp.zeros((8, LANES), jnp.float32)
     for j in range(width // LANES):
         part = jnp.broadcast_to(row[0:1, LANES * j : LANES * (j + 1)], (8, LANES))
@@ -240,9 +255,9 @@
     return lane, got
 
 
-def _write_refs(scal_ref, d_ref, out_ref):
+def _write_refs(scal_ref, d_ref, out_ref, pad):
     core, block = scal_ref[0], scal_ref[1]
-    lane, got = _ref_values(d_ref)
+    lane, got = _ref_values(d_ref, pad)
     for half in (0, 1):
         mine = (lane // 16 + 8 * half == block) & (core == 0)
         out_ref[:, half] = jnp.broadcast_to(
@@ -250,37 +265,50 @@
         )
 
 
-def _collect(scal_ref, d_ref, a_ref, gain_ref, own_ref, hot_ref, out_ref, split_refs):
-    planes, rows, width = d_ref.shape
-    tiles = (rows - 2 * PAD) // 8
-    _write_refs(scal_ref, d_ref, out_ref)
-    for p in range(planes):
+class _Collect:
+
+    def __init__(self, a_ref, gain_ref, high_ref, low_ref, pad):
+        self.refs, self.hot, self.pad = (a_ref, gain_ref), (high_ref, low_ref), pad
+        self.todo = []
+        self.acc = jnp.zeros((2 * GROUP, GROUP), jnp.float32)
+
+    def plane(self, p):
+        a_ref, gain_ref = self.refs
+        tiles = (a_ref.shape[1] - 2 * self.pad) // 8
         for t in range(tiles):
-            at = (p, slice(PAD + 8 * t, PAD + 8 * t + 8))
+            at = (p, slice(self.pad + 8 * t, self.pad + 8 * t + 8))
             y = gain_ref[at] * a_ref[at]
             coarse = y.astype(jnp.bfloat16).astype(jnp.float32)
-            fine = y - coarse
-            upper = own_ref[at] >= LANES
-            base = (p * tiles + t) * 64
-            terms = (
-                jnp.where(upper, 0.0, coarse),
-                jnp.where(upper, 0.0, fine),
-                jnp.where(upper, coarse, 0.0),
-                jnp.where(upper, fine, 0.0),
-            )
-            for j in range(width // LANES):
-                for k, term in enumerate(terms):
-                    split_refs[j][pl.ds(base + k, 8, stride=8), :] = term[:, LANES * j : LANES * (j + 1)]
-    acc = jnp.zeros((8, LANES), jnp.float32)
-    for line in range(hot_ref.shape[0]):
-        vals = jnp.concatenate([ref[8 * line : 8 * line + 8, :] for ref in split_refs], axis=1)
-        acc = acc + lax.dot_general(
-            vals.astype(jnp.bfloat16), hot_ref[line], (((1,), (1,)), ((), ())),
-            preferred_element_type=jnp.float32,
-        )
-    count = out_ref.shape[0]
-    out_ref[:, 2] = jnp.broadcast_to(acc[0:1] + acc[1:2], (count, LANES))
-    out_ref[:, 3] = jnp.broadcast_to(acc[2:3] + acc[3:4], (count, LANES))
+            self.todo += [((p * tiles + t) * 8 + x, x, coarse, y - coarse) for x in range(8)]
+
+    def some(self, count=4):
+        now, self.todo = self.todo[:count], self.todo[count:]
+        for line, x, coarse, fine in now:
+            high = self.hot[0][line]
+            vals = jnp.concatenate(
+                [
+                    high * jnp.broadcast_to(v[x : x + 1], high.shape).astype(jnp.bfloat16)
+                    for v in (coarse, fine)
+                ],
+                axis=0,
+            )
+            self.acc = self.acc + lax.dot_general(
+                vals, self.hot[1][line], (((1,), (1,)), ((), ())), preferred_element_type=jnp.float32
+            )
+
+    def finish(self, out_ref):
+        self.some(len(self.todo))
+        both = self.acc[:GROUP] + self.acc[GROUP:]
+        both = jnp.concatenate([both, jnp.zeros((GROUP, LANES - GROUP), jnp.float32)], axis=1)
+        sub = lax.broadcasted_iota(jnp.int32, (8, LANES), 0)
+        for h in (0, 1):
+            part = both[8 * h : 8 * h + 8]
+            flat = part
+            for i in range(1, 8):
+                flat = jnp.where(sub == i, pltpu.roll(part, GROUP * i, 1), flat)
+            out_ref[:, 2 + h] = jnp.broadcast_to(
+                jnp.sum(flat, axis=0, keepdims=True), (out_ref.shape[0], LANES)
+            )
 
 
 def last_kernel(scal_ref, *refs):
@@ -370,17 +398,20 @@
 
     field, plane = arr(half, rows, width), arr(2, rows, width)
     full = pltpu.VMEM((half, rows, width), jnp.float32)
-    split = [pltpu.VMEM((half * axial * 8, LANES), jnp.float32)] * (width // LANES)
     message = arr(2 * blocks, 4, LANES)
     owners = arr(half, rows, width, dtype=jnp.int32)
-    hot = _call(hot_kernel, arr(half * axial, LANES, width, dtype=jnp.bfloat16), 2, name="hot")(
-        scal, keep, got
-    )
-    bd, ba, gain, inverse, owner, direct, adjoint, inner, outer, sent = _call(
+    own_cells = pltpu.VMEM((half, axial, width), jnp.float32)
+    hot = arr(half * axial, GROUP, width, dtype=jnp.bfloat16)
+    high, low, sent = _call(
+        hot_kernel, (hot, hot, message), 2,
+        [pltpu.VMEM((1, axial, width), jnp.float32), own_cells, own_cells], name="hot",
+    )(scal, keep, got)
+    bd, ba, gain, inverse, owner, direct, adjoint, inner, outer = _call(
         functools.partial(init_kernel, blocks=blocks),
-        (field, field, field, field, owners, field, field, arr(5, INNER, rows, width), plane, message),
-        5, [full, full] + split, name="init",
-    )(scal, keep, got, before, after, hot)
+        (field, field, field, field, owners, field, field, arr(5, INNER, rows, width), plane),
+        4, [full, full], name="init",
+    )(scal, keep, got, before, after)
+    sent, outer, inner = lax.optimization_barrier((sent, outer, inner))
     cut, layers = arr(2, half, axial, radial), (2, INNER, rows, width)
     everyone = 2 * blocks * sectors
     deep = halo = None
@@ -397,10 +428,10 @@
             step = functools.partial(
                 step_kernel, extra=INNER - 1 - sweep % INNER, first=sweep == 0
             )
-            scratch = ([pltpu.VMEM(layers, jnp.float32)] if sweep == 0 else []) + split
+            scratch = [pltpu.VMEM(layers, jnp.float32)] if sweep == 0 else []
             direct, adjoint, halo, outer, sent = _call(
-                step, (field, field, arr(*layers), plane, message), len(args), scratch, name="step"
-            )(*args, hot)
+                step, (field, field, arr(*layers), plane, message), len(args) + 1, scratch, name="step"
+            )(*args, high, low)
         else:
             keep, give, sent = _call(
                 last_kernel, (cut, cut, arr(everyone, LANES)), 11, [full, full], name="last"

time: 188 us -> 180 us (0.957)
  Pallas kernels: 25.9 us -> 18 us
    pallas_call x6, Pallas kernels: 17 us -> 11.2 us  [the longest x5 9.5 us: on_device(): _call(step, (field, field, arr(*layers), plane, message), len(args) + 1,...]
    pallas_call x1, Pallas kernels: 3.06 us -> 0.84 us  [on_device(): _call(functools.partial(init_kernel, blocks=blocks), (field, field, field...]
where the time goes in v5:
time: 180 us; the launch traced here: 179 us
  blocking collectives  84.2 us (47%)
  starting transfers between devices  57.5 us (32%)
  waiting for transfers between devices  18.4 us (10%)
  Pallas kernels  18 us (10%)
    all_to_all x6, blocking collectives, on_device(): recv = lax.all_to_all(sent, BF, 0, 0, tiled=True)  84.2 us
    ppermute x6, starting transfers between devices, on_device(): outer_in = lax.ppermute(outer, ('sector', 'flame'), ring)  24.5 us
    ppermute x2, starting transfers between devices, on_device(): got = lax.ppermute(give, 'flame', swap)  15 us
    all_to_all x1, waiting for transfers between devices, on_device(): recv = lax.all_to_all(sent, ('sector',) + BF, 0, 0, tiled=True)  10.2 us
    all_to_all x1, starting transfers between devices, on_device(): recv = lax.all_to_all(sent, ('sector',) + BF, 0, 0, tiled=True)  10.1 us
    pallas_call x5, Pallas kernels, on_device(): _call(step, (field, field, arr(*layers), plane, message), len(args) + 1,...  9.5 us
    ppermute x1, waiting for transfers between devices, on_device(): lax.ppermute(first_rows, 'block', [(i + 1, i) for i in range(blocks - 1)])  3.85 us
  transfers between devices with their start and end apart: 13, of which 5 were waited for; matrix products, arithmetic and copies ran while one was open for 0% of the time, Pallas kernels for 1%

profile of v5, /device:TPU:1, one launch (start us, length us, event | category | flops | bytes accessed | tf_op | source)
XLA Modules:
  0.0 179.0 jit_solution(4880533765271184439)
XLA Ops:
  0.7 1.9 %pack.1 = (f32[5,4,16,256]{3,2,1,0:T(8,128)S(1)}, f32[5,4,16,256]{3,2,1,0:T(8,128)S(1)}) custom-call(s32[3]{0:T(128)S(1)} %pad_add_fusion.scal_ref, f32[8,16,256]{2,1,0:T(8,128)} %refs_0_.1, f32[8,16,256]{2,1,0:T(8,128)} %refs_1_.1, f32[8,16,256]{2,1,0:T(8,128)} %refs_2_.1, f32[8,16,256]{2,1,0:T(8,128)} %gain_ref.1, s32[8,16,256]{2,1,0:T(8,128)} %own_ref.1), custom_call_target="tpu_custom_call" | custom-call | tf_op jit(solution)/shard_map/pack/pallas_call | solution.py:36
  2.7 8.7 %collective-permute-start = (f32[5,4,16,256]{3,2,1,0:T(8,128)S(1)}, f32[5,4,16,256]{3,2,1,0:T(8,128)S(1)}, u32[]{:S(2)}, u32[]{:S(2)}) collective-permute-start(f32[5,4,16,256]{3,2,1,0:T(8,128)S(1)} %get-tuple-element.50), channel_id=1, source_target_pairs={{0,1},{1,0},{2,3},{3,2},{4,5},{5,4},{6,7},{7,6},{8,9},{9,8},{10,11... | collective-permute-start | bytes 983048 | tf_op jit(solution)/shard_map/ppermute | solution.py:393
  17.6 2.1 %collective-permute-done.1.before_ref = f32[5,24,512]{2,1,0:T(8,128)S(1)} collective-permute-done((f32[5,24,512]{2,1,0:T(8,128)S(1)}, f32[5,24,512]{2,1,0:T(8,128)S(1)}, u32[]{:S(2)}, u32[]{:S(2)}) %collective-permute-start.1) | collective-permute-done | bytes 245792 | tf_op jit(solution)/shard_map/ppermute | solution.py:396
  19.8 3.8 %collective-permute-done.2.after_ref = f32[5,24,512]{2,1,0:T(8,128)S(1)} collective-permute-done((f32[5,24,512]{2,1,0:T(8,128)S(1)}, f32[5,24,512]{2,1,0:T(8,128)S(1)}, u32[]{:S(2)}, u32[]{:S(2)}) %collective-permute-start.2) | collective-permute-done | bytes 245792 | tf_op jit(solution)/shard_map/ppermute | solution.py:397
  24.5 3.1 %collective-permute-start.4 = (f32[5,3,32,512]{3,2,1,0:T(8,128)S(1)}, f32[5,3,32,512]{3,2,1,0:T(8,128)S(1)}, u32[]{:S(2)}, u32[]{:S(2)}) collective-permute-start(f32[5,3,32,512]{3,2,1,0:T(8,128)S(1)} %get-tuple-element.65), channel_id=1, source_target_pairs={{0,1},{1,0},{2,3},{3,2},{4,5},{5,4},{6,7},{7,6},{8,9},{9,8},{10,11... | collective-permute-start | bytes 2949128 | tf_op jit(solution)/shard_map/ppermute | solution.py:421
  27.6 7.0 %collective-permute-start.3 = (f32[2,32,512]{2,1,0:T(8,128)S(1)}, f32[2,32,512]{2,1,0:T(8,128)S(1)}, u32[]{:S(2)}, u32[]{:S(2)}) collective-permute-start(f32[2,32,512]{2,1,0:T(8,128)S(1)} %get-tuple-element.57), channel_id=1, source_target_pairs={{0,481},{32,1},{64,33},{96,65},{128,97},{160,129},{192,161},{224,1... | collective-permute-start | bytes 393224 | tf_op jit(solution)/shard_map/ppermute | solution.py:419
  34.6 18.9 %all_to_all.41.refs_0_ = f32[32,4,128]{2,1,0:T(4,128)S(1)} all-to-all(f32[32,4,128]{2,1,0:T(4,128)S(1)} %get-tuple-element.56), channel_id=1, replica_groups=mesh['sector'=16,'block'=16,'flame'=2] {'block','flame'}, dimensions={0} | all-to-all | bytes 131072 | tf_op jit(solution)/shard_map/all_to_all | solution.py:424
  53.6 1.9 %step.5 = (f32[4,32,512]{2,1,0:T(8,128)S(1)}, f32[4,32,512]{2,1,0:T(8,128)S(1)}, f32[2,3,32,512]{3,2,1,0:T(8,128)S(1)}, f32[2,32,512]{2,1,0:T(8,128)S(1)}, f32[32,4,128]{2,1,0:T(4,128)S(1)}) custom-call(s32[3]{0:T(128)S(1)} %pad_add_fusion.scal_ref, f32[32,4,128]{2,1,0:T(4,128)S(1)} %all_to_all.41.refs_0_, f32[2,32,512]{2,1,0:T(8,128)S(1)} %collective-permute-done.3.refs_1_, ...), custom_call_target="tpu_custom_call" | custom-call | tf_op jit(solution)/shard_map/step/pallas_call | solution.py:432
  55.5 1.9 %collective-permute-start.5 = (f32[2,32,512]{2,1,0:T(8,128)S(1)}, f32[2,32,512]{2,1,0:T(8,128)S(1)}, u32[]{:S(2)}, u32[]{:S(2)}) collective-permute-start(f32[2,32,512]{2,1,0:T(8,128)S(1)} %get-tuple-element.69), channel_id=1, source_target_pairs={{0,481},{32,1},{64,33},{96,65},{128,97},{160,129},{192,161},{224,1... | collective-permute-start | bytes 393224 | tf_op jit(solution)/shard_map/ppermute | solution.py:419
  57.5 13.5 %all_to_all.42.refs_0_ = f32[32,4,128]{2,1,0:T(4,128)S(1)} all-to-all(f32[32,4,128]{2,1,0:T(4,128)S(1)} %get-tuple-element.68), channel_id=1, replica_groups=mesh['sector'=16,'block'=16,'flame'=2] {'block','flame'}, dimensions={0} | all-to-all | bytes 131072 | tf_op jit(solution)/shard_map/all_to_all | solution.py:424
  71.0 1.9 %step.6 = (f32[4,32,512]{2,1,0:T(8,128)S(1)}, f32[4,32,512]{2,1,0:T(8,128)S(1)}, f32[2,3,32,512]{3,2,1,0:T(8,128)S(1)}, f32[2,32,512]{2,1,0:T(8,128)S(1)}, f32[32,4,128]{2,1,0:T(4,128)S(1)}) custom-call(s32[3]{0:T(128)S(1)} %pad_add_fusion.scal_ref, f32[32,4,128]{2,1,0:T(4,128)S(1)} %all_to_all.42.refs_0_, f32[2,32,512]{2,1,0:T(8,128)S(1)} %collective-permute-done.5.refs_1_, ...), custom_call_target="tpu_custom_call" | custom-call | tf_op jit(solution)/shard_map/step/pallas_call | solution.py:432
  72.9 5.0 %collective-permute-start.6 = (f32[2,32,512]{2,1,0:T(8,128)S(1)}, f32[2,32,512]{2,1,0:T(8,128)S(1)}, u32[]{:S(2)}, u32[]{:S(2)}) collective-permute-start(f32[2,32,512]{2,1,0:T(8,128)S(1)} %get-tuple-element.74), channel_id=1, source_target_pairs={{0,481},{32,1},{64,33},{96,65},{128,97},{160,129},{192,161},{224,1... | collective-permute-start | bytes 393224 | tf_op jit(solution)/shard_map/ppermute | solution.py:419
  77.9 12.8 %all_to_all.43.refs_0_ = f32[32,4,128]{2,1,0:T(4,128)S(1)} all-to-all(f32[32,4,128]{2,1,0:T(4,128)S(1)} %get-tuple-element.73), channel_id=1, replica_groups=mesh['sector'=16,'block'=16,'flame'=2] {'block','flame'}, dimensions={0} | all-to-all | bytes 131072 | tf_op jit(solution)/shard_map/all_to_all | solution.py:424
  92.5 2.3 %collective-permute-start.8 = (f32[2,3,32,512]{3,2,1,0:T(8,128)S(1)}, f32[2,3,32,512]{3,2,1,0:T(8,128)S(1)}, u32[]{:S(2)}, u32[]{:S(2)}) collective-permute-start(f32[2,3,32,512]{3,2,1,0:T(8,128)S(1)} %get-tuple-element.82), channel_id=1, source_target_pairs={{0,1},{1,0},{2,3},{3,2},{4,5},{5,4},{6,7},{7,6},{8,9},{9,8},{10,11... | collective-permute-start | bytes 1179656 | tf_op jit(solution)/shard_map/ppermute | solution.py:423
  94.8 2.8 %collective-permute-start.7 = (f32[2,32,512]{2,1,0:T(8,128)S(1)}, f32[2,32,512]{2,1,0:T(8,128)S(1)}, u32[]{:S(2)}, u32[]{:S(2)}) collective-permute-start(f32[2,32,512]{2,1,0:T(8,128)S(1)} %get-tuple-element.79), channel_id=1, source_target_pairs={{0,481},{32,1},{64,33},{96,65},{128,97},{160,129},{192,161},{224,1... | collective-permute-start | bytes 393224 | tf_op jit(solution)/shard_map/ppermute | solution.py:419
  97.6 13.5 %all_to_all.44.refs_0_ = f32[32,4,128]{2,1,0:T(4,128)S(1)} all-to-all(f32[32,4,128]{2,1,0:T(4,128)S(1)} %get-tuple-element.78), channel_id=1, replica_groups=mesh['sector'=16,'block'=16,'flame'=2] {'block','flame'}, dimensions={0} | all-to-all | bytes 131072 | tf_op jit(solution)/shard_map/all_to_all | solution.py:424
  111.1 1.9 %step.8 = (f32[4,32,512]{2,1,0:T(8,128)S(1)}, f32[4,32,512]{2,1,0:T(8,128)S(1)}, f32[2,3,32,512]{3,2,1,0:T(8,128)S(1)}, f32[2,32,512]{2,1,0:T(8,128)S(1)}, f32[32,4,128]{2,1,0:T(4,128)S(1)}) custom-call(s32[3]{0:T(128)S(1)} %pad_add_fusion.scal_ref, f32[32,4,128]{2,1,0:T(4,128)S(1)} %all_to_all.44.refs_0_, f32[2,32,512]{2,1,0:T(8,128)S(1)} %collective-permute-done.7.refs_1_, ...), custom_call_target="tpu_custom_call" | custom-call | tf_op jit(solution)/shard_map/step/pallas_call | solution.py:432
  113.1 4.1 %collective-permute-start.9 = (f32[2,32,512]{2,1,0:T(8,128)S(1)}, f32[2,32,512]{2,1,0:T(8,128)S(1)}, u32[]{:S(2)}, u32[]{:S(2)}) collective-permute-start(f32[2,32,512]{2,1,0:T(8,128)S(1)} %get-tuple-element.84), channel_id=1, source_target_pairs={{0,481},{32,1},{64,33},{96,65},{128,97},{160,129},{192,161},{224,1... | collective-permute-start | bytes 393224 | tf_op jit(solution)/shard_map/ppermute | solution.py:419
  117.2 12.7 %all_to_all.45.refs_0_ = f32[32,4,128]{2,1,0:T(4,128)S(1)} all-to-all(f32[32,4,128]{2,1,0:T(4,128)S(1)} %get-tuple-element.83), channel_id=1, replica_groups=mesh['sector'=16,'block'=16,'flame'=2] {'block','flame'}, dimensions={0} | all-to-all | bytes 131072 | tf_op jit(solution)/shard_map/all_to_all | solution.py:424
  131.7 3.7 %collective-permute-start.10 = (f32[2,32,512]{2,1,0:T(8,128)S(1)}, f32[2,32,512]{2,1,0:T(8,128)S(1)}, u32[]{:S(2)}, u32[]{:S(2)}) collective-permute-start(f32[2,32,512]{2,1,0:T(8,128)S(1)} %get-tuple-element.89), channel_id=1, source_target_pairs={{0,481},{32,1},{64,33},{96,65},{128,97},{160,129},{192,161},{224,1... | collective-permute-start | bytes 393224 | tf_op jit(solution)/shard_map/ppermute | solution.py:419
  135.4 12.8 %all_to_all.46.refs_0_ = f32[32,4,128]{2,1,0:T(4,128)S(1)} all-to-all(f32[32,4,128]{2,1,0:T(4,128)S(1)} %get-tuple-element.88), channel_id=1, replica_groups=mesh['sector'=16,'block'=16,'flame'=2] {'block','flame'}, dimensions={0} | all-to-all | bytes 131072 | tf_op jit(solution)/shard_map/all_to_all | solution.py:424
  150.0 10.1 %all-to-all-start.6 = ((f32[512,1,128]{2,1,0:T(1,128)}), f32[512,1,128]{2,1,0:T(1,128)S(1)}, u32[]{:S(2)}, u32[]{:S(2)}) async-start(f32[512,1,128]{2,1,0:T(1,128)} %bitcast.4), calls=%async_computation.6 | async-start | bytes 524288 | tf_op jit(solution)/shard_map/all_to_all | solution.py:441
  160.1 6.2 %collective-permute-start.11 = (f32[2,4,16,256]{3,2,1,0:T(8,128)S(1)}, f32[2,4,16,256]{3,2,1,0:T(8,128)S(1)}, u32[]{:S(2)}, u32[]{:S(2)}) collective-permute-start(f32[2,4,16,256]{3,2,1,0:T(8,128)S(1)} %get-tuple-element.95), channel_id=1, source_target_pairs={{0,1},{1,0},{2,3},{3,2},{4,5},{5,4},{6,7},{7,6},{8,9},{9,8},{10,11... | collective-permute-start | bytes 393224 | tf_op jit(solution)/shard_map/ppermute | solution.py:440
  167.3 10.2 %all-to-all-done.6 = f32[512,1,128]{2,1,0:T(1,128)S(1)} async-done(((f32[512,1,128]{2,1,0:T(1,128)}), f32[512,1,128]{2,1,0:T(1,128)S(1)}, u32[]{:S(2)}, u32[]{:S(2)}) %all-to-all-start.6) | async-done | bytes 262176 | tf_op jit(solution)/shard_map/all_to_all | solution.py:441
  (24 shorter events, 15.2 us)
Async XLA Ops:
  2.7 10.0 %collective-permute-start = (f32[5,4,16,256]{3,2,1,0:T(8,128)S(1)}, f32[5,4,16,256]{3,2,1,0:T(8,128)S(1)}, u32[]{:S(2)}, u32[]{:S(2)}) collective-permute-start(f32[5,4,16,256]{3,2,1,0:T(8,128)S(1)} %get-tuple-element.50), channel_id=1, source_target_pairs={{0,1},{1,0},{2,3},{3,2},{4,5},{5,4},{6,7},{7,6},{8,9},{9,8},{10,11... | collective-permute-start | bytes 983048 | tf_op jit(solution)/shard_map/ppermute | solution.py:393
  13.3 6.5 %collective-permute-start.1 = (f32[5,24,512]{2,1,0:T(8,128)S(1)}, f32[5,24,512]{2,1,0:T(8,128)S(1)}, u32[]{:S(2)}, u32[]{:S(2)}) collective-permute-start(f32[5,24,512]{2,1,0:T(8,128)S(1)} %get-tuple-element.52), channel_id=1, source_target_pairs={{0,2},{2,4},{4,6},{6,8},{8,10},{10,12},{12,14},{14,16},{16,18},{18... | collective-permute-start | bytes 737288 | tf_op jit(solution)/shard_map/ppermute | solution.py:396
  14.6 9.0 %collective-permute-start.2 = (f32[5,24,512]{2,1,0:T(8,128)S(1)}, f32[5,24,512]{2,1,0:T(8,128)S(1)}, u32[]{:S(2)}, u32[]{:S(2)}) collective-permute-start(f32[5,24,512]{2,1,0:T(8,128)S(1)} %get-tuple-element.53), channel_id=1, source_target_pairs={{2,0},{4,2},{6,4},{8,6},{10,8},{12,10},{14,12},{16,14},{18,16},{20... | collective-permute-start | bytes 737288 | tf_op jit(solution)/shard_map/ppermute | solution.py:397
  24.5 29.1 %collective-permute-start.4 = (f32[5,3,32,512]{3,2,1,0:T(8,128)S(1)}, f32[5,3,32,512]{3,2,1,0:T(8,128)S(1)}, u32[]{:S(2)}, u32[]{:S(2)}) collective-permute-start(f32[5,3,32,512]{3,2,1,0:T(8,128)S(1)} %get-tuple-element.65), channel_id=1, source_target_pairs={{0,1},{1,0},{2,3},{3,2},{4,5},{5,4},{6,7},{7,6},{8,9},{9,8},{10,11... | collective-permute-start | bytes 2949128 | tf_op jit(solution)/shard_map/ppermute | solution.py:421
  27.6 26.0 %collective-permute-start.3 = (f32[2,32,512]{2,1,0:T(8,128)S(1)}, f32[2,32,512]{2,1,0:T(8,128)S(1)}, u32[]{:S(2)}, u32[]{:S(2)}) collective-permute-start(f32[2,32,512]{2,1,0:T(8,128)S(1)} %get-tuple-element.57), channel_id=1, source_target_pairs={{0,481},{32,1},{64,33},{96,65},{128,97},{160,129},{192,161},{224,1... | collective-permute-start | bytes 393224 | tf_op jit(solution)/shard_map/ppermute | solution.py:419
  55.5 15.4 %collective-permute-start.5 = (f32[2,32,512]{2,1,0:T(8,128)S(1)}, f32[2,32,512]{2,1,0:T(8,128)S(1)}, u32[]{:S(2)}, u32[]{:S(2)}) collective-permute-start(f32[2,32,512]{2,1,0:T(8,128)S(1)} %get-tuple-element.69), channel_id=1, source_target_pairs={{0,481},{32,1},{64,33},{96,65},{128,97},{160,129},{192,161},{224,1... | collective-permute-start | bytes 393224 | tf_op jit(solution)/shard_map/ppermute | solution.py:419
  72.9 17.8 %collective-permute-start.6 = (f32[2,32,512]{2,1,0:T(8,128)S(1)}, f32[2,32,512]{2,1,0:T(8,128)S(1)}, u32[]{:S(2)}, u32[]{:S(2)}) collective-permute-start(f32[2,32,512]{2,1,0:T(8,128)S(1)} %get-tuple-element.74), channel_id=1, source_target_pairs={{0,481},{32,1},{64,33},{96,65},{128,97},{160,129},{192,161},{224,1... | collective-permute-start | bytes 393224 | tf_op jit(solution)/shard_map/ppermute | solution.py:419
  92.5 18.6 %collective-permute-start.8 = (f32[2,3,32,512]{3,2,1,0:T(8,128)S(1)}, f32[2,3,32,512]{3,2,1,0:T(8,128)S(1)}, u32[]{:S(2)}, u32[]{:S(2)}) collective-permute-start(f32[2,3,32,512]{3,2,1,0:T(8,128)S(1)} %get-tuple-element.82), channel_id=1, source_target_pairs={{0,1},{1,0},{2,3},{3,2},{4,5},{5,4},{6,7},{7,6},{8,9},{9,8},{10,11... | collective-permute-start | bytes 1179656 | tf_op jit(solution)/shard_map/ppermute | solution.py:423
  94.8 16.3 %collective-permute-start.7 = (f32[2,32,512]{2,1,0:T(8,128)S(1)}, f32[2,32,512]{2,1,0:T(8,128)S(1)}, u32[]{:S(2)}, u32[]{:S(2)}) collective-permute-start(f32[2,32,512]{2,1,0:T(8,128)S(1)} %get-tuple-element.79), channel_id=1, source_target_pairs={{0,481},{32,1},{64,33},{96,65},{128,97},{160,129},{192,161},{224,1... | collective-permute-start | bytes 393224 | tf_op jit(solution)/shard_map/ppermute | solution.py:419
  113.1 16.8 %collective-permute-start.9 = (f32[2,32,512]{2,1,0:T(8,128)S(1)}, f32[2,32,512]{2,1,0:T(8,128)S(1)}, u32[]{:S(2)}, u32[]{:S(2)}) collective-permute-start(f32[2,32,512]{2,1,0:T(8,128)S(1)} %get-tuple-element.84), channel_id=1, source_target_pairs={{0,481},{32,1},{64,33},{96,65},{128,97},{160,129},{192,161},{224,1... | collective-permute-start | bytes 393224 | tf_op jit(solution)/shard_map/ppermute | solution.py:419
  131.7 16.5 %collective-permute-start.10 = (f32[2,32,512]{2,1,0:T(8,128)S(1)}, f32[2,32,512]{2,1,0:T(8,128)S(1)}, u32[]{:S(2)}, u32[]{:S(2)}) collective-permute-start(f32[2,32,512]{2,1,0:T(8,128)S(1)} %get-tuple-element.89), channel_id=1, source_target_pairs={{0,481},{32,1},{64,33},{96,65},{128,97},{160,129},{192,161},{224,1... | collective-permute-start | bytes 393224 | tf_op jit(solution)/shard_map/ppermute | solution.py:419
  150.0 27.5 %copy-start = (f32[8,16,256]{2,1,0:T(8,128)S(1)}, f32[8,16,256]{2,1,0:T(8,128)}, u32[]{:S(2)}) copy-start(f32[8,16,256]{2,1,0:T(8,128)} %gain_ref.1) | copy-start | bytes 393220
  150.0 27.5 %copy-start.1 = (s32[8,16,256]{2,1,0:T(8,128)S(1)}, s32[8,16,256]{2,1,0:T(8,128)}, u32[]{:S(2)}) copy-start(s32[8,16,256]{2,1,0:T(8,128)} %own_ref.1) | copy-start | bytes 393220
  150.0 27.5 %all-to-all-start.6 = ((f32[512,1,128]{2,1,0:T(1,128)}), f32[512,1,128]{2,1,0:T(1,128)S(1)}, u32[]{:S(2)}, u32[]{:S(2)}) async-start(f32[512,1,128]{2,1,0:T(1,128)} %bitcast.4), calls=%async_computation.6 | async-start | bytes 524288 | tf_op jit(solution)/shard_map/all_to_all | solution.py:441
  160.1 7.2 %collective-permute-start.11 = (f32[2,4,16,256]{3,2,1,0:T(8,128)S(1)}, f32[2,4,16,256]{3,2,1,0:T(8,128)S(1)}, u32[]{:S(2)}, u32[]{:S(2)}) collective-permute-start(f32[2,4,16,256]{3,2,1,0:T(8,128)S(1)} %get-tuple-element.95), channel_id=1, source_target_pairs={{0,1},{1,0},{2,3},{3,2},{4,5},{5,4},{6,7},{7,6},{8,9},{9,8},{10,11... | collective-permute-start | bytes 393224 | tf_op jit(solution)/shard_map/ppermute | solution.py:440

commit v6 on v5

--- a/solution.py
+++ b/solution.py
@@ -21,10 +21,14 @@
 def _call(kernel, out_shape, n_in, scratch=(), name=None, space=pltpu.VMEM):
     vmem = pl.BlockSpec(memory_space=pltpu.VMEM)
     single = not isinstance(out_shape, (tuple, list))
+
+    def body(*refs):
+        kernel([lax.axis_index(axis) for axis in ("flame", "block", "sector")], *refs)
+
     call = pl.pallas_call(
-        kernel,
+        body,
         out_shape=out_shape,
-        in_specs=[pl.BlockSpec(memory_space=pltpu.SMEM)] + [pl.BlockSpec(memory_space=space)] * n_in,
+        in_specs=[pl.BlockSpec(memory_space=space)] * n_in,
         out_specs=vmem if single else [vmem] * len(out_shape),
         scratch_shapes=list(scratch),
         interpret=INTERPRET,
@@ -33,9 +37,7 @@
     )
     if space is pltpu.VMEM or INTERPRET:
         return call
-    return lambda scal, *args: call(
-        scal, *(pltpu.with_memory_space_constraint(x, space) for x in args)
-    )
+    return lambda *args: call(*(pltpu.with_memory_space_constraint(x, space) for x in args))
 
 
 def _lookup(table, owner):
@@ -48,8 +50,8 @@
     return [jnp.broadcast_to(total[row + j : row + j + 1], (8, LANES)) for j in (0, 1)]
 
 
-def pack_kernel(scal_ref, *refs):
-    core = scal_ref[0]
+def pack_kernel(here, *refs):
+    core = here[0]
     ins, (keep_ref, give_ref, keep_id, give_id, sems) = refs[:5], refs[5:]
     half = keep_ref.shape[1]
     copies = []
@@ -69,8 +71,8 @@
     give_ref[4] = give_id[...].astype(jnp.float32)
 
 
-def edges_kernel(scal_ref, keep_ref, got_ref, after_ref, before_ref):
-    core = scal_ref[0]
+def edges_kernel(here, keep_ref, got_ref, after_ref, before_ref):
+    core = here[0]
     count, half, axial, radial = keep_ref.shape
     for i in range(count):
         for p in range(half):
@@ -81,8 +83,8 @@
                 ref[i, to, radial:] = jnp.where(core == 0, other, mine)
 
 
-def hot_kernel(scal_ref, keep_ref, got_ref, high_ref, low_ref, out_ref, d_ref, a_ref, gain_ref):
-    core = scal_ref[0]
+def hot_kernel(here, keep_ref, got_ref, high_ref, low_ref, out_ref, d_ref, a_ref, gain_ref):
+    core = here[0]
     count, half, axial, radial = keep_ref.shape
     width = 2 * radial
     ids = lax.broadcasted_iota(jnp.int32, (GROUP, width), 0).astype(jnp.float32)
@@ -106,16 +108,17 @@
                 for x in range(8):
                     hit = jnp.broadcast_to(part[x : x + 1], (GROUP, width)) == ids
                     ref[(p * (axial // 8) + t) * 8 + x] = jnp.where(hit, 1.0, 0.0).astype(jnp.bfloat16)
-    collect = _Collect(a_ref, gain_ref, high_ref, low_ref, 0)
+    collect = _Collect(gain_ref, high_ref, low_ref, 0)
     for p in range(half):
-        collect.plane(p)
+        for t in range(axial // 8):
+            collect.tile(p, t, a_ref[p, 8 * t : 8 * t + 8])
     collect.finish(out_ref)
-    _write_refs(scal_ref, d_ref, out_ref, 0)
-
-
-def init_kernel(scal_ref, keep_ref, got_ref, before_ref, after_ref, bd_ref, ba_ref, gain_ref,
+    _write_refs(here, d_ref, out_ref, 0)
+
+
+def init_kernel(here, keep_ref, got_ref, before_ref, after_ref, bd_ref, ba_ref, gain_ref,
                 inv_ref, own_ref, d_ref, a_ref, inner_ref, outer_ref, shift_ref, id_ref, *, blocks):
-    core, block = scal_ref[0], scal_ref[1]
+    core, block = here[0], here[1]
     _, half, axial, radial = keep_ref.shape
     rows = axial + 2 * PAD
     for i, ref in enumerate((bd_ref, ba_ref, shift_ref, gain_ref, id_ref)):
@@ -150,7 +153,7 @@
     outer_ref[1] = a_ref[0]
 
 
-def step_kernel(scal_ref, *refs, extra, first):
+def step_kernel(here, *refs, extra, first):
     refs = list(refs)
     ins = [refs.pop(0) for _ in range(10)]
     halo_ref = None if first else refs.pop(0)
@@ -161,20 +164,20 @@
         for i in (0, 1):
             for depth in range(INNER):
                 halo_ref[i, depth] = ins[9][i, depth] * ins[9][2, depth]
-    collect = _Collect(an_ref, ins[6], high_ref, low_ref, PAD)
-    _sweep(scal_ref, *ins, halo_ref, dn_ref, an_ref, hn_ref, extra, 0, collect)
+    collect = _Collect(ins[6], high_ref, low_ref, PAD)
+    _sweep(here, *ins, halo_ref, dn_ref, an_ref, hn_ref, extra, 0, collect)
     if not extra:
         for i, ref in enumerate((dn_ref, an_ref)):
             for depth in range(INNER):
                 hn_ref[i, depth] = ref[ref.shape[0] - 1 - depth]
     _send(outer_ref, dn_ref, an_ref)
     collect.finish(out_ref)
-    _write_refs(scal_ref, dn_ref, out_ref, PAD)
-
-
-def _sweep(scal_ref, recv_ref, outer_ref, d_ref, a_ref, bd_ref, ba_ref, gain_ref,
+    _write_refs(here, dn_ref, out_ref, PAD)
+
+
+def _sweep(here, recv_ref, outer_ref, d_ref, a_ref, bd_ref, ba_ref, gain_ref,
            inv_ref, own_ref, deep_ref, halo_ref, dn_ref, an_ref, hn_ref, extra, pad=0, collect=None):
-    core, block = scal_ref[0], scal_ref[1]
+    core, block = here[0], here[1]
     planes, rows, width = d_ref.shape
     tiles = rows // 8
     total = jnp.sum(recv_ref[...], axis=0)
@@ -200,25 +203,25 @@
             return outer_ref[field, rng]
         return ref[p, rng] if p < planes else halo_ref[field, p - planes, rng]
 
-    def near(ref, field, p, t):
-        rng = slice(8 * t, 8 * t + 8)
-        here = plane(ref, field, p, rng)
-        below, above = plane(ref, field, p - 1, rng), plane(ref, field, p + 1, rng)
+    def near(ref, field, p, t, below, mid, above):
         if t == 0:
-            back = pltpu.roll(here, 1, 0)
+            back = pltpu.roll(mid, 1, 0)
         else:
             back = plane(ref, field, p, slice(8 * t - 1, 8 * t + 7))
         if t == tiles - 1:
-            front = pltpu.roll(here, 7, 0)
+            front = pltpu.roll(mid, 7, 0)
         else:
             front = plane(ref, field, p, slice(8 * t + 1, 8 * t + 9))
-        left = jnp.where(first, 0.0, pltpu.roll(here, 1, 1))
-        right = jnp.where(last, 0.0, pltpu.roll(here, width - 1, 1))
+        left = jnp.where(first, 0.0, pltpu.roll(mid, 1, 1))
+        right = jnp.where(last, 0.0, pltpu.roll(mid, width - 1, 1))
         return (below + above) + (back + front) + (left + right)
 
-    for p in range(planes + extra):
-        for t in range(pad // 8, tiles - pad // 8):
-            rng = slice(8 * t, 8 * t + 8)
+    own_tiles = range(PAD // 8, tiles - PAD // 8)
+    rest = [t for t in range(tiles) if t not in own_tiles] if pad == 0 else []
+    for t in list(own_tiles) + rest:
+        rng = slice(8 * t, 8 * t + 8)
+        window = [[plane(r, i, p, rng) for p in (-1, 0)] for i, r in enumerate((d_ref, a_ref))]
+        for p in range(planes + extra):
             if p < planes:
                 to_d, to_a = dn_ref.at[p, rng], an_ref.at[p, rng]
                 bd, ba, gain, inv, own = (r[p, rng] for r in (bd_ref, ba_ref, gain_ref, inv_ref, own_ref))
@@ -226,21 +229,24 @@
                 to_d, to_a = hn_ref.at[0, p - planes, rng], hn_ref.at[1, p - planes, rng]
                 bd, ba, inv, gain, own = (deep_ref[i, p - planes, rng] for i in range(5))
                 own = own.astype(jnp.int32)
+            for i, r in enumerate((d_ref, a_ref)):
+                window[i] = window[i][-2:] + [plane(r, i, p + 1, rng)]
             looked = jnp.concatenate(
                 [_lookup(table, own[:, LANES * j : LANES * (j + 1)]) for j in range(width // LANES)],
                 axis=1,
             )
-            to_d[...] = (bd + near(d_ref, 0, p, t) + gain * looked) * inv
-            acc = ba + near(a_ref, 1, p, t)
+            to_d[...] = (bd + near(d_ref, 0, p, t, *window[0]) + gain * looked) * inv
+            acc = ba + near(a_ref, 1, p, t, *window[1])
             if p == 0 and t == PAD // 8:
                 acc = acc + source(block)
             if p == 0 and t == tiles - PAD // 8:
                 acc = acc + source(block + 1)
-            to_a[...] = acc * inv
+            acc = acc * inv
+            to_a[...] = acc
             if collect is not None:
                 collect.some()
-        if collect is not None and p < planes:
-            collect.plane(p)
+                if p < planes and t in own_tiles:
+                    collect.tile(p, t - PAD // 8, acc)
 
 
 def _ref_values(d_ref, pad=PAD):
@@ -255,8 +261,8 @@
     return lane, got
 
 
-def _write_refs(scal_ref, d_ref, out_ref, pad):
-    core, block = scal_ref[0], scal_ref[1]
+def _write_refs(here, d_ref, out_ref, pad):
+    core, block = here[0], here[1]
     lane, got = _ref_values(d_ref, pad)
     for half in (0, 1):
         mine = (lane // 16 + 8 * half == block) & (core == 0)
@@ -267,19 +273,16 @@
 
 class _Collect:
 
-    def __init__(self, a_ref, gain_ref, high_ref, low_ref, pad):
-        self.refs, self.hot, self.pad = (a_ref, gain_ref), (high_ref, low_ref), pad
+    def __init__(self, gain_ref, high_ref, low_ref, pad):
+        self.gain, self.hot, self.pad = gain_ref, (high_ref, low_ref), pad
         self.todo = []
         self.acc = jnp.zeros((2 * GROUP, GROUP), jnp.float32)
 
-    def plane(self, p):
-        a_ref, gain_ref = self.refs
-        tiles = (a_ref.shape[1] - 2 * self.pad) // 8
-        for t in range(tiles):
-            at = (p, slice(self.pad + 8 * t, self.pad + 8 * t + 8))
-            y = gain_ref[at] * a_ref[at]
-            coarse = y.astype(jnp.bfloat16).astype(jnp.float32)
-            self.todo += [((p * tiles + t) * 8 + x, x, coarse, y - coarse) for x in range(8)]
+    def tile(self, p, t, a):
+        gain_ref, tiles = self.gain, (self.gain.shape[1] - 2 * self.pad) // 8
+        y = gain_ref[p, self.pad + 8 * t : self.pad + 8 * t + 8] * a
+        coarse = y.astype(jnp.bfloat16).astype(jnp.float32)
+        self.todo += [((p * tiles + t) * 8 + x, x, coarse, y - coarse) for x in range(8)]
 
     def some(self, count=4):
         now, self.todo = self.todo[:count], self.todo[count:]
@@ -311,10 +314,10 @@
             )
 
 
-def last_kernel(scal_ref, *refs):
+def last_kernel(here, *refs):
     ins, (keep_ref, give_ref, out_ref, dn_ref, an_ref) = refs[:-5], refs[-5:]
-    core, block = scal_ref[0], scal_ref[1]
-    _sweep(scal_ref, *ins, dn_ref, an_ref, None, 0, PAD)
+    core, block = here[0], here[1]
+    _sweep(here, *ins, dn_ref, an_ref, None, 0, PAD)
     planes, rows, width = dn_ref.shape
     radial = width // 2
     lane, values = _ref_values(dn_ref)
@@ -335,9 +338,9 @@
     out_ref[...] = jnp.broadcast_to(line, out_ref.shape)
 
 
-def fields_kernel(scal_ref, recv_ref, keep_ref, got_ref, gain_ref, own_ref, first_ref, second_ref,
+def fields_kernel(here, recv_ref, keep_ref, got_ref, gain_ref, own_ref, first_ref, second_ref,
                   *, cells, group):
-    core, sector = scal_ref[0], scal_ref[2]
+    core, sector = here[0], here[2]
     planes, axial, radial = gain_ref.shape
     half = planes // 2
     lane = lax.broadcasted_iota(jnp.int32, (8, LANES), 1)
@@ -374,8 +377,6 @@
 def on_device(rhs_direct, rhs_adjoint, diag_shift, flame_gain, ref_owner):
     planes, axial, radial = rhs_direct.shape
     sectors, blocks = lax.axis_size("sector"), lax.axis_size("block")
-    core, block = lax.axis_index("flame"), lax.axis_index("block")
-    scal = jnp.stack([core, block, lax.axis_index("sector")]).astype(jnp.int32)
     half, width, rows = planes // 2, 2 * radial, axial + 2 * PAD
     swap = [(0, 1), (1, 0)]
     ring = [(2 * s, (2 * s - 1) % (2 * sectors)) for s in range(sectors)]
@@ -389,10 +390,10 @@
     keep, give = _call(
         pack_kernel, (quarter, quarter), 5, [ids, ids, pltpu.SemaphoreType.DMA((5, half, 2))],
         name="pack", space=pltpu.HBM,
-    )(scal, rhs_direct, rhs_adjoint, diag_shift, flame_gain, ref_owner)
+    )(rhs_direct, rhs_adjoint, diag_shift, flame_gain, ref_owner)
     got = lax.ppermute(give, "flame", swap)
     edge = arr(5, half * HALO, width)
-    first_rows, last_rows = _call(edges_kernel, (edge, edge), 2, name="edges")(scal, keep, got)
+    first_rows, last_rows = _call(edges_kernel, (edge, edge), 2, name="edges")(keep, got)
     before = lax.ppermute(last_rows, "block", [(i, i + 1) for i in range(blocks - 1)])
     after = lax.ppermute(first_rows, "block", [(i + 1, i) for i in range(blocks - 1)])
 
@@ -405,12 +406,12 @@
     high, low, sent = _call(
         hot_kernel, (hot, hot, message), 2,
         [pltpu.VMEM((1, axial, width), jnp.float32), own_cells, own_cells], name="hot",
-    )(scal, keep, got)
+    )(keep, got)
     bd, ba, gain, inverse, owner, direct, adjoint, inner, outer = _call(
         functools.partial(init_kernel, blocks=blocks),
         (field, field, field, field, owners, field, field, arr(5, INNER, rows, width), plane),
         4, [full, full], name="init",
-    )(scal, keep, got, before, after)
+    )(keep, got, before, after)
     sent, outer, inner = lax.optimization_barrier((sent, outer, inner))
     cut, layers = arr(2, half, axial, radial), (2, INNER, rows, width)
     everyone = 2 * blocks * sectors
@@ -422,7 +423,7 @@
         elif sweep % INNER == 0:
             halo = lax.ppermute(halo, "flame", swap)
         recv = lax.all_to_all(sent, BF, 0, 0, tiled=True)
-        args = (scal, recv, outer_in, direct, adjoint, bd, ba, gain, inverse, owner, deep)
+        args = (recv, outer_in, direct, adjoint, bd, ba, gain, inverse, owner, deep)
         args += () if halo is None else (halo,)
         if sweep < ITERS - 1:
             step = functools.partial(
@@ -430,7 +431,7 @@
             )
             scratch = [pltpu.VMEM(layers, jnp.float32)] if sweep == 0 else []
             direct, adjoint, halo, outer, sent = _call(
-                step, (field, field, arr(*layers), plane, message), len(args) + 1, scratch, name="step"
+                step, (field, field, arr(*layers), plane, message), len(args) + 2, scratch, name="step"
             )(*args, high, low)
         else:
             keep, give, sent = _call(
@@ -444,7 +445,7 @@
     return tuple(
         _call(
             functools.partial(fields_kernel, cells=cells, group=2 * blocks), (out, out), 5, name="fields"
-        )(scal, recv, keep, got, flame_gain, ref_owner)
+        )(recv, keep, got, flame_gain, ref_owner)
     )
 
 

time: 180 us -> 174 us (0.967)
  Pallas kernels: 18 us -> 11.7 us
    pallas_call x7, Pallas kernels: 12.1 us -> 7.98 us  [the longest x5 6.5 us: on_device(): _call(step, (field, field, arr(*layers), plane, message), len(args) + 2,...]
where the time goes in v6:
time: 174 us; the launch traced here: 173 us
  blocking collectives  84.2 us (48%)
  starting transfers between devices  57.5 us (33%)
  waiting for transfers between devices  19 us (11%)
  Pallas kernels  11.7 us (7%)
    all_to_all x6, blocking collectives, on_device(): recv = lax.all_to_all(sent, BF, 0, 0, tiled=True)  84.2 us
    ppermute x6, starting transfers between devices, on_device(): outer_in = lax.ppermute(outer, ('sector', 'flame'), ring)  24.5 us
    ppermute x2, starting transfers between devices, on_device(): got = lax.ppermute(give, 'flame', swap)  15 us
    all_to_all x1, waiting for transfers between devices, on_device(): recv = lax.all_to_all(sent, ('sector',) + BF, 0, 0, tiled=True)  10.2 us
    all_to_all x1, starting transfers between devices, on_device(): recv = lax.all_to_all(sent, ('sector',) + BF, 0, 0, tiled=True)  10 us
    pallas_call x5, Pallas kernels, on_device(): _call(step, (field, field, arr(*layers), plane, message), len(args) + 2,...  6.5 us
    ppermute x1, waiting for transfers between devices, on_device(): lax.ppermute(first_rows, 'block', [(i + 1, i) for i in range(blocks - 1)])  3.85 us
  transfers between devices with their start and end apart: 13, of which 5 were waited for; matrix products, arithmetic and copies ran while one was open for 0% of the time, Pallas kernels for 1%

profile of v6, /device:TPU:1, one launch (start us, length us, event | category | flops | bytes accessed | tf_op | source)
XLA Modules:
  0.0 173.2 jit_solution(16830528520250938875)
XLA Ops:
  0.6 1.4 pack.1
  2.0 8.7 %collective-permute-start = (f32[5,4,16,256]{3,2,1,0:T(8,128)S(1)}, f32[5,4,16,256]{3,2,1,0:T(8,128)S(1)}, u32[]{:S(2)}, u32[]{:S(2)}) collective-permute-start(f32[5,4,16,256]{3,2,1,0:T(8,128)S(1)} %get-tuple-element.50), channel_id=1, source_target_pairs={{0,1},{1,0},{2,3},{3,2},{4,5},{5,4},{6,7},{7,6},{8,9},{9,8},{10,11... | collective-permute-start | bytes 983048 | tf_op jit(solution)/shard_map/ppermute | solution.py:394
  12.1 1.3 collective-permute-start.1
  15.9 2.7 %collective-permute-done.1.refs_2_ = f32[5,24,512]{2,1,0:T(8,128)S(1)} collective-permute-done((f32[5,24,512]{2,1,0:T(8,128)S(1)}, f32[5,24,512]{2,1,0:T(8,128)S(1)}, u32[]{:S(2)}, u32[]{:S(2)}) %collective-permute-start.1) | collective-permute-done | bytes 245792 | tf_op jit(solution)/shard_map/ppermute | solution.py:397
  18.6 3.8 %collective-permute-done.2.refs_3_ = f32[5,24,512]{2,1,0:T(8,128)S(1)} collective-permute-done((f32[5,24,512]{2,1,0:T(8,128)S(1)}, f32[5,24,512]{2,1,0:T(8,128)S(1)}, u32[]{:S(2)}, u32[]{:S(2)}) %collective-permute-start.2) | collective-permute-done | bytes 245792 | tf_op jit(solution)/shard_map/ppermute | solution.py:398
  22.8 3.1 %collective-permute-start.4 = (f32[5,3,32,512]{3,2,1,0:T(8,128)S(1)}, f32[5,3,32,512]{3,2,1,0:T(8,128)S(1)}, u32[]{:S(2)}, u32[]{:S(2)}) collective-permute-start(f32[5,3,32,512]{3,2,1,0:T(8,128)S(1)} %get-tuple-element.65), channel_id=1, source_target_pairs={{0,1},{1,0},{2,3},{3,2},{4,5},{5,4},{6,7},{7,6},{8,9},{9,8},{10,11... | collective-permute-start | bytes 2949128 | tf_op jit(solution)/shard_map/ppermute | solution.py:422
  25.9 7.0 %collective-permute-start.3 = (f32[2,32,512]{2,1,0:T(8,128)S(1)}, f32[2,32,512]{2,1,0:T(8,128)S(1)}, u32[]{:S(2)}, u32[]{:S(2)}) collective-permute-start(f32[2,32,512]{2,1,0:T(8,128)S(1)} %get-tuple-element.57), channel_id=1, source_target_pairs={{0,481},{32,1},{64,33},{96,65},{128,97},{160,129},{192,161},{224,1... | collective-permute-start | bytes 393224 | tf_op jit(solution)/shard_map/ppermute | solution.py:420
  32.9 18.9 %all_to_all.41.refs_0_ = f32[32,4,128]{2,1,0:T(4,128)S(1)} all-to-all(f32[32,4,128]{2,1,0:T(4,128)S(1)} %get-tuple-element.56), channel_id=1, replica_groups=mesh['sector'=16,'block'=16,'flame'=2] {'block','flame'}, dimensions={0} | all-to-all | bytes 131072 | tf_op jit(solution)/shard_map/all_to_all | solution.py:425
  51.9 1.3 step.5
  53.2 1.9 %collective-permute-start.5 = (f32[2,32,512]{2,1,0:T(8,128)S(1)}, f32[2,32,512]{2,1,0:T(8,128)S(1)}, u32[]{:S(2)}, u32[]{:S(2)}) collective-permute-start(f32[2,32,512]{2,1,0:T(8,128)S(1)} %get-tuple-element.69), channel_id=1, source_target_pairs={{0,481},{32,1},{64,33},{96,65},{128,97},{160,129},{192,161},{224,1... | collective-permute-start | bytes 393224 | tf_op jit(solution)/shard_map/ppermute | solution.py:420
  55.1 13.5 %all_to_all.42.refs_0_ = f32[32,4,128]{2,1,0:T(4,128)S(1)} all-to-all(f32[32,4,128]{2,1,0:T(4,128)S(1)} %get-tuple-element.68), channel_id=1, replica_groups=mesh['sector'=16,'block'=16,'flame'=2] {'block','flame'}, dimensions={0} | all-to-all | bytes 131072 | tf_op jit(solution)/shard_map/all_to_all | solution.py:425
  69.9 5.0 %collective-permute-start.6 = (f32[2,32,512]{2,1,0:T(8,128)S(1)}, f32[2,32,512]{2,1,0:T(8,128)S(1)}, u32[]{:S(2)}, u32[]{:S(2)}) collective-permute-start(f32[2,32,512]{2,1,0:T(8,128)S(1)} %get-tuple-element.74), channel_id=1, source_target_pairs={{0,481},{32,1},{64,33},{96,65},{128,97},{160,129},{192,161},{224,1... | collective-permute-start | bytes 393224 | tf_op jit(solution)/shard_map/ppermute | solution.py:420
  74.9 12.8 %all_to_all.43.refs_0_ = f32[32,4,128]{2,1,0:T(4,128)S(1)} all-to-all(f32[32,4,128]{2,1,0:T(4,128)S(1)} %get-tuple-element.73), channel_id=1, replica_groups=mesh['sector'=16,'block'=16,'flame'=2] {'block','flame'}, dimensions={0} | all-to-all | bytes 131072 | tf_op jit(solution)/shard_map/all_to_all | solution.py:425
  89.0 2.3 %collective-permute-start.8 = (f32[2,3,32,512]{3,2,1,0:T(8,128)S(1)}, f32[2,3,32,512]{3,2,1,0:T(8,128)S(1)}, u32[]{:S(2)}, u32[]{:S(2)}) collective-permute-start(f32[2,3,32,512]{3,2,1,0:T(8,128)S(1)} %get-tuple-element.82), channel_id=1, source_target_pairs={{0,1},{1,0},{2,3},{3,2},{4,5},{5,4},{6,7},{7,6},{8,9},{9,8},{10,11... | collective-permute-start | bytes 1179656 | tf_op jit(solution)/shard_map/ppermute | solution.py:424
  91.3 2.8 %collective-permute-start.7 = (f32[2,32,512]{2,1,0:T(8,128)S(1)}, f32[2,32,512]{2,1,0:T(8,128)S(1)}, u32[]{:S(2)}, u32[]{:S(2)}) collective-permute-start(f32[2,32,512]{2,1,0:T(8,128)S(1)} %get-tuple-element.79), channel_id=1, source_target_pairs={{0,481},{32,1},{64,33},{96,65},{128,97},{160,129},{192,161},{224,1... | collective-permute-start | bytes 393224 | tf_op jit(solution)/shard_map/ppermute | solution.py:420
  94.1 13.5 %all_to_all.44.refs_0_ = f32[32,4,128]{2,1,0:T(4,128)S(1)} all-to-all(f32[32,4,128]{2,1,0:T(4,128)S(1)} %get-tuple-element.78), channel_id=1, replica_groups=mesh['sector'=16,'block'=16,'flame'=2] {'block','flame'}, dimensions={0} | all-to-all | bytes 131072 | tf_op jit(solution)/shard_map/all_to_all | solution.py:425
  107.6 1.3 step.8
  109.0 4.1 %collective-permute-start.9 = (f32[2,32,512]{2,1,0:T(8,128)S(1)}, f32[2,32,512]{2,1,0:T(8,128)S(1)}, u32[]{:S(2)}, u32[]{:S(2)}) collective-permute-start(f32[2,32,512]{2,1,0:T(8,128)S(1)} %get-tuple-element.84), channel_id=1, source_target_pairs={{0,481},{32,1},{64,33},{96,65},{128,97},{160,129},{192,161},{224,1... | collective-permute-start | bytes 393224 | tf_op jit(solution)/shard_map/ppermute | solution.py:420
  113.1 12.7 %all_to_all.45.refs_0_ = f32[32,4,128]{2,1,0:T(4,128)S(1)} all-to-all(f32[32,4,128]{2,1,0:T(4,128)S(1)} %get-tuple-element.83), channel_id=1, replica_groups=mesh['sector'=16,'block'=16,'flame'=2] {'block','flame'}, dimensions={0} | all-to-all | bytes 131072 | tf_op jit(solution)/shard_map/all_to_all | solution.py:425
  127.0 3.7 %collective-permute-start.10 = (f32[2,32,512]{2,1,0:T(8,128)S(1)}, f32[2,32,512]{2,1,0:T(8,128)S(1)}, u32[]{:S(2)}, u32[]{:S(2)}) collective-permute-start(f32[2,32,512]{2,1,0:T(8,128)S(1)} %get-tuple-element.89), channel_id=1, source_target_pairs={{0,481},{32,1},{64,33},{96,65},{128,97},{160,129},{192,161},{224,1... | collective-permute-start | bytes 393224 | tf_op jit(solution)/shard_map/ppermute | solution.py:420
  130.7 12.8 %all_to_all.46.refs_0_ = f32[32,4,128]{2,1,0:T(4,128)S(1)} all-to-all(f32[32,4,128]{2,1,0:T(4,128)S(1)} %get-tuple-element.88), channel_id=1, replica_groups=mesh['sector'=16,'block'=16,'flame'=2] {'block','flame'}, dimensions={0} | all-to-all | bytes 131072 | tf_op jit(solution)/shard_map/all_to_all | solution.py:425
  144.8 10.0 %all-to-all-start.6 = ((f32[512,1,128]{2,1,0:T(1,128)}), f32[512,1,128]{2,1,0:T(1,128)S(1)}, u32[]{:S(2)}, u32[]{:S(2)}) async-start(f32[512,1,128]{2,1,0:T(1,128)} %bitcast.1), calls=%async_computation.6 | async-start | bytes 524288 | tf_op jit(solution)/shard_map/all_to_all | solution.py:442
  154.8 6.2 %collective-permute-start.11 = (f32[2,4,16,256]{3,2,1,0:T(8,128)S(1)}, f32[2,4,16,256]{3,2,1,0:T(8,128)S(1)}, u32[]{:S(2)}, u32[]{:S(2)}) collective-permute-start(f32[2,4,16,256]{3,2,1,0:T(8,128)S(1)} %get-tuple-element.95), channel_id=1, source_target_pairs={{0,1},{1,0},{2,3},{3,2},{4,5},{5,4},{6,7},{7,6},{8,9},{9,8},{10,11... | collective-permute-start | bytes 393224 | tf_op jit(solution)/shard_map/ppermute | solution.py:441
  162.0 10.2 %all-to-all-done.6 = f32[512,1,128]{2,1,0:T(1,128)S(1)} async-done(((f32[512,1,128]{2,1,0:T(1,128)}), f32[512,1,128]{2,1,0:T(1,128)S(1)}, u32[]{:S(2)}, u32[]{:S(2)}) %all-to-all-start.6) | async-done | bytes 262176 | tf_op jit(solution)/shard_map/all_to_all | solution.py:442
  (23 shorter events, 11.2 us)
Async XLA Ops:
  2.0 10.0 %collective-permute-start = (f32[5,4,16,256]{3,2,1,0:T(8,128)S(1)}, f32[5,4,16,256]{3,2,1,0:T(8,128)S(1)}, u32[]{:S(2)}, u32[]{:S(2)}) collective-permute-start(f32[5,4,16,256]{3,2,1,0:T(8,128)S(1)} %get-tuple-element.50), channel_id=1, source_target_pairs={{0,1},{1,0},{2,3},{3,2},{4,5},{5,4},{6,7},{7,6},{8,9},{9,8},{10,11... | collective-permute-start | bytes 983048 | tf_op jit(solution)/shard_map/ppermute | solution.py:394
  12.1 6.5 %collective-permute-start.1 = (f32[5,24,512]{2,1,0:T(8,128)S(1)}, f32[5,24,512]{2,1,0:T(8,128)S(1)}, u32[]{:S(2)}, u32[]{:S(2)}) collective-permute-start(f32[5,24,512]{2,1,0:T(8,128)S(1)} %get-tuple-element.52), channel_id=1, source_target_pairs={{0,2},{2,4},{4,6},{6,8},{8,10},{10,12},{12,14},{14,16},{16,18},{18... | collective-permute-start | bytes 737288 | tf_op jit(solution)/shard_map/ppermute | solution.py:397
  13.4 9.0 %collective-permute-start.2 = (f32[5,24,512]{2,1,0:T(8,128)S(1)}, f32[5,24,512]{2,1,0:T(8,128)S(1)}, u32[]{:S(2)}, u32[]{:S(2)}) collective-permute-start(f32[5,24,512]{2,1,0:T(8,128)S(1)} %get-tuple-element.53), channel_id=1, source_target_pairs={{2,0},{4,2},{6,4},{8,6},{10,8},{12,10},{14,12},{16,14},{18,16},{20... | collective-permute-start | bytes 737288 | tf_op jit(solution)/shard_map/ppermute | solution.py:398
  22.8 29.1 %collective-permute-start.4 = (f32[5,3,32,512]{3,2,1,0:T(8,128)S(1)}, f32[5,3,32,512]{3,2,1,0:T(8,128)S(1)}, u32[]{:S(2)}, u32[]{:S(2)}) collective-permute-start(f32[5,3,32,512]{3,2,1,0:T(8,128)S(1)} %get-tuple-element.65), channel_id=1, source_target_pairs={{0,1},{1,0},{2,3},{3,2},{4,5},{5,4},{6,7},{7,6},{8,9},{9,8},{10,11... | collective-permute-start | bytes 2949128 | tf_op jit(solution)/shard_map/ppermute | solution.py:422
  25.9 26.0 %collective-permute-start.3 = (f32[2,32,512]{2,1,0:T(8,128)S(1)}, f32[2,32,512]{2,1,0:T(8,128)S(1)}, u32[]{:S(2)}, u32[]{:S(2)}) collective-permute-start(f32[2,32,512]{2,1,0:T(8,128)S(1)} %get-tuple-element.57), channel_id=1, source_target_pairs={{0,481},{32,1},{64,33},{96,65},{128,97},{160,129},{192,161},{224,1... | collective-permute-start | bytes 393224 | tf_op jit(solution)/shard_map/ppermute | solution.py:420
  53.2 15.4 %collective-permute-start.5 = (f32[2,32,512]{2,1,0:T(8,128)S(1)}, f32[2,32,512]{2,1,0:T(8,128)S(1)}, u32[]{:S(2)}, u32[]{:S(2)}) collective-permute-start(f32[2,32,512]{2,1,0:T(8,128)S(1)} %get-tuple-element.69), channel_id=1, source_target_pairs={{0,481},{32,1},{64,33},{96,65},{128,97},{160,129},{192,161},{224,1... | collective-permute-start | bytes 393224 | tf_op jit(solution)/shard_map/ppermute | solution.py:420
  69.9 17.8 %collective-permute-start.6 = (f32[2,32,512]{2,1,0:T(8,128)S(1)}, f32[2,32,512]{2,1,0:T(8,128)S(1)}, u32[]{:S(2)}, u32[]{:S(2)}) collective-permute-start(f32[2,32,512]{2,1,0:T(8,128)S(1)} %get-tuple-element.74), channel_id=1, source_target_pairs={{0,481},{32,1},{64,33},{96,65},{128,97},{160,129},{192,161},{224,1... | collective-permute-start | bytes 393224 | tf_op jit(solution)/shard_map/ppermute | solution.py:420
  89.0 18.6 %collective-permute-start.8 = (f32[2,3,32,512]{3,2,1,0:T(8,128)S(1)}, f32[2,3,32,512]{3,2,1,0:T(8,128)S(1)}, u32[]{:S(2)}, u32[]{:S(2)}) collective-permute-start(f32[2,3,32,512]{3,2,1,0:T(8,128)S(1)} %get-tuple-element.82), channel_id=1, source_target_pairs={{0,1},{1,0},{2,3},{3,2},{4,5},{5,4},{6,7},{7,6},{8,9},{9,8},{10,11... | collective-permute-start | bytes 1179656 | tf_op jit(solution)/shard_map/ppermute | solution.py:424
  91.3 16.3 %collective-permute-start.7 = (f32[2,32,512]{2,1,0:T(8,128)S(1)}, f32[2,32,512]{2,1,0:T(8,128)S(1)}, u32[]{:S(2)}, u32[]{:S(2)}) collective-permute-start(f32[2,32,512]{2,1,0:T(8,128)S(1)} %get-tuple-element.79), channel_id=1, source_target_pairs={{0,481},{32,1},{64,33},{96,65},{128,97},{160,129},{192,161},{224,1... | collective-permute-start | bytes 393224 | tf_op jit(solution)/shard_map/ppermute | solution.py:420
  109.0 16.8 %collective-permute-start.9 = (f32[2,32,512]{2,1,0:T(8,128)S(1)}, f32[2,32,512]{2,1,0:T(8,128)S(1)}, u32[]{:S(2)}, u32[]{:S(2)}) collective-permute-start(f32[2,32,512]{2,1,0:T(8,128)S(1)} %get-tuple-element.84), channel_id=1, source_target_pairs={{0,481},{32,1},{64,33},{96,65},{128,97},{160,129},{192,161},{224,1... | collective-permute-start | bytes 393224 | tf_op jit(solution)/shard_map/ppermute | solution.py:420
  127.0 16.5 %collective-permute-start.10 = (f32[2,32,512]{2,1,0:T(8,128)S(1)}, f32[2,32,512]{2,1,0:T(8,128)S(1)}, u32[]{:S(2)}, u32[]{:S(2)}) collective-permute-start(f32[2,32,512]{2,1,0:T(8,128)S(1)} %get-tuple-element.89), channel_id=1, source_target_pairs={{0,481},{32,1},{64,33},{96,65},{128,97},{160,129},{192,161},{224,1... | collective-permute-start | bytes 393224 | tf_op jit(solution)/shard_map/ppermute | solution.py:420
  144.8 27.5 %copy-start = (f32[8,16,256]{2,1,0:T(8,128)S(1)}, f32[8,16,256]{2,1,0:T(8,128)}, u32[]{:S(2)}) copy-start(f32[8,16,256]{2,1,0:T(8,128)} %refs_3_.3) | copy-start | bytes 393220
  144.8 27.5 %copy-start.1 = (s32[8,16,256]{2,1,0:T(8,128)S(1)}, s32[8,16,256]{2,1,0:T(8,128)}, u32[]{:S(2)}) copy-start(s32[8,16,256]{2,1,0:T(8,128)} %refs_4_.3) | copy-start | bytes 393220
  144.8 27.5 %all-to-all-start.6 = ((f32[512,1,128]{2,1,0:T(1,128)}), f32[512,1,128]{2,1,0:T(1,128)S(1)}, u32[]{:S(2)}, u32[]{:S(2)}) async-start(f32[512,1,128]{2,1,0:T(1,128)} %bitcast.1), calls=%async_computation.6 | async-start | bytes 524288 | tf_op jit(solution)/shard_map/all_to_all | solution.py:442
  154.8 7.2 %collective-permute-start.11 = (f32[2,4,16,256]{3,2,1,0:T(8,128)S(1)}, f32[2,4,16,256]{3,2,1,0:T(8,128)S(1)}, u32[]{:S(2)}, u32[]{:S(2)}) collective-permute-start(f32[2,4,16,256]{3,2,1,0:T(8,128)S(1)} %get-tuple-element.95), channel_id=1, source_target_pairs={{0,1},{1,0},{2,3},{3,2},{4,5},{5,4},{6,7},{7,6},{8,9},{9,8},{10,11... | collective-permute-start | bytes 393224 | tf_op jit(solution)/shard_map/ppermute | solution.py:441

commit v7 on v6

--- a/solution.py
+++ b/solution.py
@@ -71,16 +71,23 @@
     give_ref[4] = give_id[...].astype(jnp.float32)
 
 
+def _halo_rows(half):
+    at = 0
+    for i in range(5):
+        depth = HALO if i < 3 else HALO - 1
+        for p in range(half):
+            yield i, p, depth, at
+            at += depth
+
+
 def edges_kernel(here, keep_ref, got_ref, after_ref, before_ref):
     core = here[0]
-    count, half, axial, radial = keep_ref.shape
-    for i in range(count):
-        for p in range(half):
-            to = slice(p * HALO, (p + 1) * HALO)
-            for ref, rng in ((after_ref, slice(0, HALO)), (before_ref, slice(axial - HALO, axial))):
-                mine, other = keep_ref[i, p, rng], got_ref[i, p, rng]
-                ref[i, to, :radial] = jnp.where(core == 0, mine, other)
-                ref[i, to, radial:] = jnp.where(core == 0, other, mine)
+    _, half, axial, radial = keep_ref.shape
+    for i, p, depth, at in _halo_rows(half):
+        for ref, rng in ((after_ref, slice(0, depth)), (before_ref, slice(axial - depth, axial))):
+            mine, other = keep_ref[i, p, rng], got_ref[i, p, rng]
+            ref[at : at + depth, :radial] = jnp.where(core == 0, mine, other)
+            ref[at : at + depth, radial:] = jnp.where(core == 0, other, mine)
 
 
 def hot_kernel(here, keep_ref, got_ref, high_ref, low_ref, out_ref, d_ref, a_ref, gain_ref):
@@ -121,15 +128,16 @@
     core, block = here[0], here[1]
     _, half, axial, radial = keep_ref.shape
     rows = axial + 2 * PAD
-    for i, ref in enumerate((bd_ref, ba_ref, shift_ref, gain_ref, id_ref)):
-        for p in range(half):
-            ref[p, :PAD] = jnp.zeros((PAD, 2 * radial), jnp.float32)
-            ref[p, rows - PAD :] = jnp.zeros((PAD, 2 * radial), jnp.float32)
-            ref[p, PAD - HALO : PAD] = before_ref[i, p * HALO : (p + 1) * HALO]
-            ref[p, rows - PAD : rows - PAD + HALO] = after_ref[i, p * HALO : (p + 1) * HALO]
-            mine, other = keep_ref[i, p], got_ref[i, p]
-            ref[p, PAD : PAD + axial, :radial] = jnp.where(core == 0, mine, other)
-            ref[p, PAD : PAD + axial, radial:] = jnp.where(core == 0, other, mine)
+    arrays = (bd_ref, ba_ref, shift_ref, gain_ref, id_ref)
+    for i, p, depth, at in _halo_rows(half):
+        ref = arrays[i]
+        ref[p, :PAD] = jnp.zeros((PAD, 2 * radial), jnp.float32)
+        ref[p, rows - PAD :] = jnp.zeros((PAD, 2 * radial), jnp.float32)
+        ref[p, PAD - depth : PAD] = before_ref[at : at + depth]
+        ref[p, rows - PAD : rows - PAD + depth] = after_ref[at : at + depth]
+        mine, other = keep_ref[i, p], got_ref[i, p]
+        ref[p, PAD : PAD + axial, :radial] = jnp.where(core == 0, mine, other)
+        ref[p, PAD : PAD + axial, radial:] = jnp.where(core == 0, other, mine)
     for p in range(half):
         for t in range(rows // 8):
             at = (p, slice(8 * t, 8 * t + 8))
@@ -143,9 +151,13 @@
             d_ref[at] = bd_ref[at] * inv
             a_ref[at] = ba_ref[at] * inv
     for i, ref in enumerate((bd_ref, ba_ref, inv_ref, gain_ref, id_ref)):
-        for depth in range(INNER):
-            inner_ref[i, depth] = ref[half - 1 - depth]
+        for depth in range(INNER if i < 3 else INNER - 1):
+            inner_ref[_deep(i, depth)] = ref[half - 1 - depth]
     _send(outer_ref, d_ref, a_ref)
+
+
+def _deep(i, depth):
+    return INNER * i + depth if i < 3 else 3 * INNER + (INNER - 1) * (i - 3) + depth
 
 
 def _send(outer_ref, d_ref, a_ref):
@@ -163,7 +175,7 @@
         halo_ref = refs.pop(0)
         for i in (0, 1):
             for depth in range(INNER):
-                halo_ref[i, depth] = ins[9][i, depth] * ins[9][2, depth]
+                halo_ref[i, depth] = ins[9][_deep(i, depth)] * ins[9][_deep(2, depth)]
     collect = _Collect(ins[6], high_ref, low_ref, PAD)
     _sweep(here, *ins, halo_ref, dn_ref, an_ref, hn_ref, extra, 0, collect)
     if not extra:
@@ -227,7 +239,7 @@
                 bd, ba, gain, inv, own = (r[p, rng] for r in (bd_ref, ba_ref, gain_ref, inv_ref, own_ref))
             else:
                 to_d, to_a = hn_ref.at[0, p - planes, rng], hn_ref.at[1, p - planes, rng]
-                bd, ba, inv, gain, own = (deep_ref[i, p - planes, rng] for i in range(5))
+                bd, ba, inv, gain, own = (deep_ref[_deep(i, p - planes), rng] for i in range(5))
                 own = own.astype(jnp.int32)
             for i, r in enumerate((d_ref, a_ref)):
                 window[i] = window[i][-2:] + [plane(r, i, p + 1, rng)]
@@ -392,7 +404,7 @@
         name="pack", space=pltpu.HBM,
     )(rhs_direct, rhs_adjoint, diag_shift, flame_gain, ref_owner)
     got = lax.ppermute(give, "flame", swap)
-    edge = arr(5, half * HALO, width)
+    edge = arr(half * (5 * HALO - 2), width)
     first_rows, last_rows = _call(edges_kernel, (edge, edge), 2, name="edges")(keep, got)
     before = lax.ppermute(last_rows, "block", [(i, i + 1) for i in range(blocks - 1)])
     after = lax.ppermute(first_rows, "block", [(i + 1, i) for i in range(blocks - 1)])
@@ -409,7 +421,7 @@
     )(keep, got)
     bd, ba, gain, inverse, owner, direct, adjoint, inner, outer = _call(
         functools.partial(init_kernel, blocks=blocks),
-        (field, field, field, field, owners, field, field, arr(5, INNER, rows, width), plane),
+        (field, field, field, field, owners, field, field, arr(5 * INNER - 2, rows, width), plane),
         4, [full, full], name="init",
     )(keep, got, before, after)
     sent, outer, inner = lax.optimization_barrier((sent, outer, inner))

time: 174 us -> 174 us (level)
  no operation moved by 1% of the time
where the time goes in v7:
time: 174 us; the launch traced here: 173 us
  blocking collectives  84.2 us (48%)
  starting transfers between devices  57.6 us (33%)
  waiting for transfers between devices  18.6 us (11%)
  Pallas kernels  11.7 us (7%)
    all_to_all x6, blocking collectives, on_device(): recv = lax.all_to_all(sent, BF, 0, 0, tiled=True)  84.2 us
    ppermute x6, starting transfers between devices, on_device(): outer_in = lax.ppermute(outer, ('sector', 'flame'), ring)  24.5 us
    ppermute x2, starting transfers between devices, on_device(): got = lax.ppermute(give, 'flame', swap)  15 us
    all_to_all x1, waiting for transfers between devices, on_device(): recv = lax.all_to_all(sent, ('sector',) + BF, 0, 0, tiled=True)  10.2 us
    all_to_all x1, starting transfers between devices, on_device(): recv = lax.all_to_all(sent, ('sector',) + BF, 0, 0, tiled=True)  10.1 us
    pallas_call x5, Pallas kernels, on_device(): _call(step, (field, field, arr(*layers), plane, message), len(args) + 2,...  6.5 us
    ppermute x1, waiting for transfers between devices, on_device(): lax.ppermute(first_rows, 'block', [(i + 1, i) for i in range(blocks - 1)])  3.85 us
  transfers between devices with their start and end apart: 13, of which 5 were waited for; matrix products, arithmetic and copies ran while one was open for 0% of the time, Pallas kernels for 1%

profile of v7, /device:TPU:1, one launch (start us, length us, event | category | flops | bytes accessed | tf_op | source)
XLA Modules:
  0.0 172.9 jit_solution(7120182339976915677)
XLA Ops:
  0.6 1.4 pack.1
  2.0 8.7 %collective-permute-start = (f32[5,4,16,256]{3,2,1,0:T(8,128)S(1)}, f32[5,4,16,256]{3,2,1,0:T(8,128)S(1)}, u32[]{:S(2)}, u32[]{:S(2)}) collective-permute-start(f32[5,4,16,256]{3,2,1,0:T(8,128)S(1)} %get-tuple-element.50), channel_id=1, source_target_pairs={{0,1},{1,0},{2,3},{3,2},{4,5},{5,4},{6,7},{7,6},{8,9},{9,8},{10,11... | collective-permute-start | bytes 983048 | tf_op jit(solution)/shard_map/ppermute | solution.py:406
  12.1 1.3 collective-permute-start.1
  15.9 2.3 %collective-permute-done.1.refs_2_ = f32[112,512]{1,0:T(8,128)S(1)} collective-permute-done((f32[112,512]{1,0:T(8,128)S(1)}, f32[112,512]{1,0:T(8,128)S(1)}, u32[]{:S(2)}, u32[]{:S(2)}) %collective-permute-start.1) | collective-permute-done | bytes 229408 | tf_op jit(solution)/shard_map/ppermute | solution.py:409
  18.3 3.8 %collective-permute-done.2.refs_3_ = f32[112,512]{1,0:T(8,128)S(1)} collective-permute-done((f32[112,512]{1,0:T(8,128)S(1)}, f32[112,512]{1,0:T(8,128)S(1)}, u32[]{:S(2)}, u32[]{:S(2)}) %collective-permute-start.2) | collective-permute-done | bytes 229408 | tf_op jit(solution)/shard_map/ppermute | solution.py:410
  22.4 3.1 %collective-permute-start.4 = (f32[13,32,512]{2,1,0:T(8,128)S(1)}, f32[13,32,512]{2,1,0:T(8,128)S(1)}, u32[]{:S(2)}, u32[]{:S(2)}) collective-permute-start(f32[13,32,512]{2,1,0:T(8,128)S(1)} %get-tuple-element.65), channel_id=1, source_target_pairs={{0,1},{1,0},{2,3},{3,2},{4,5},{5,4},{6,7},{7,6},{8,9},{9,8},{10,11... | collective-permute-start | bytes 2555912 | tf_op jit(solution)/shard_map/ppermute | solution.py:434
  25.5 7.0 %collective-permute-start.3 = (f32[2,32,512]{2,1,0:T(8,128)S(1)}, f32[2,32,512]{2,1,0:T(8,128)S(1)}, u32[]{:S(2)}, u32[]{:S(2)}) collective-permute-start(f32[2,32,512]{2,1,0:T(8,128)S(1)} %get-tuple-element.57), channel_id=1, source_target_pairs={{0,481},{32,1},{64,33},{96,65},{128,97},{160,129},{192,161},{224,1... | collective-permute-start | bytes 393224 | tf_op jit(solution)/shard_map/ppermute | solution.py:432
  32.6 18.9 %all_to_all.41.refs_0_ = f32[32,4,128]{2,1,0:T(4,128)S(1)} all-to-all(f32[32,4,128]{2,1,0:T(4,128)S(1)} %get-tuple-element.56), channel_id=1, replica_groups=mesh['sector'=16,'block'=16,'flame'=2] {'block','flame'}, dimensions={0} | all-to-all | bytes 131072 | tf_op jit(solution)/shard_map/all_to_all | solution.py:437
  51.5 1.3 step.5
  52.8 1.9 %collective-permute-start.5 = (f32[2,32,512]{2,1,0:T(8,128)S(1)}, f32[2,32,512]{2,1,0:T(8,128)S(1)}, u32[]{:S(2)}, u32[]{:S(2)}) collective-permute-start(f32[2,32,512]{2,1,0:T(8,128)S(1)} %get-tuple-element.69), channel_id=1, source_target_pairs={{0,481},{32,1},{64,33},{96,65},{128,97},{160,129},{192,161},{224,1... | collective-permute-start | bytes 393224 | tf_op jit(solution)/shard_map/ppermute | solution.py:432
  54.8 13.5 %all_to_all.42.refs_0_ = f32[32,4,128]{2,1,0:T(4,128)S(1)} all-to-all(f32[32,4,128]{2,1,0:T(4,128)S(1)} %get-tuple-element.68), channel_id=1, replica_groups=mesh['sector'=16,'block'=16,'flame'=2] {'block','flame'}, dimensions={0} | all-to-all | bytes 131072 | tf_op jit(solution)/shard_map/all_to_all | solution.py:437
  69.6 5.0 %collective-permute-start.6 = (f32[2,32,512]{2,1,0:T(8,128)S(1)}, f32[2,32,512]{2,1,0:T(8,128)S(1)}, u32[]{:S(2)}, u32[]{:S(2)}) collective-permute-start(f32[2,32,512]{2,1,0:T(8,128)S(1)} %get-tuple-element.74), channel_id=1, source_target_pairs={{0,481},{32,1},{64,33},{96,65},{128,97},{160,129},{192,161},{224,1... | collective-permute-start | bytes 393224 | tf_op jit(solution)/shard_map/ppermute | solution.py:432
  74.6 12.8 %all_to_all.43.refs_0_ = f32[32,4,128]{2,1,0:T(4,128)S(1)} all-to-all(f32[32,4,128]{2,1,0:T(4,128)S(1)} %get-tuple-element.73), channel_id=1, replica_groups=mesh['sector'=16,'block'=16,'flame'=2] {'block','flame'}, dimensions={0} | all-to-all | bytes 131072 | tf_op jit(solution)/shard_map/all_to_all | solution.py:437
  88.6 2.3 %collective-permute-start.8 = (f32[2,3,32,512]{3,2,1,0:T(8,128)S(1)}, f32[2,3,32,512]{3,2,1,0:T(8,128)S(1)}, u32[]{:S(2)}, u32[]{:S(2)}) collective-permute-start(f32[2,3,32,512]{3,2,1,0:T(8,128)S(1)} %get-tuple-element.82), channel_id=1, source_target_pairs={{0,1},{1,0},{2,3},{3,2},{4,5},{5,4},{6,7},{7,6},{8,9},{9,8},{10,11... | collective-permute-start | bytes 1179656 | tf_op jit(solution)/shard_map/ppermute | solution.py:436
  90.9 2.8 %collective-permute-start.7 = (f32[2,32,512]{2,1,0:T(8,128)S(1)}, f32[2,32,512]{2,1,0:T(8,128)S(1)}, u32[]{:S(2)}, u32[]{:S(2)}) collective-permute-start(f32[2,32,512]{2,1,0:T(8,128)S(1)} %get-tuple-element.79), channel_id=1, source_target_pairs={{0,481},{32,1},{64,33},{96,65},{128,97},{160,129},{192,161},{224,1... | collective-permute-start | bytes 393224 | tf_op jit(solution)/shard_map/ppermute | solution.py:432
  93.7 13.5 %all_to_all.44.refs_0_ = f32[32,4,128]{2,1,0:T(4,128)S(1)} all-to-all(f32[32,4,128]{2,1,0:T(4,128)S(1)} %get-tuple-element.78), channel_id=1, replica_groups=mesh['sector'=16,'block'=16,'flame'=2] {'block','flame'}, dimensions={0} | all-to-all | bytes 131072 | tf_op jit(solution)/shard_map/all_to_all | solution.py:437
  107.3 1.3 step.8
  108.6 4.1 %collective-permute-start.9 = (f32[2,32,512]{2,1,0:T(8,128)S(1)}, f32[2,32,512]{2,1,0:T(8,128)S(1)}, u32[]{:S(2)}, u32[]{:S(2)}) collective-permute-start(f32[2,32,512]{2,1,0:T(8,128)S(1)} %get-tuple-element.84), channel_id=1, source_target_pairs={{0,481},{32,1},{64,33},{96,65},{128,97},{160,129},{192,161},{224,1... | collective-permute-start | bytes 393224 | tf_op jit(solution)/shard_map/ppermute | solution.py:432
  112.7 12.7 %all_to_all.45.refs_0_ = f32[32,4,128]{2,1,0:T(4,128)S(1)} all-to-all(f32[32,4,128]{2,1,0:T(4,128)S(1)} %get-tuple-element.83), channel_id=1, replica_groups=mesh['sector'=16,'block'=16,'flame'=2] {'block','flame'}, dimensions={0} | all-to-all | bytes 131072 | tf_op jit(solution)/shard_map/all_to_all | solution.py:437
  126.7 3.7 %collective-permute-start.10 = (f32[2,32,512]{2,1,0:T(8,128)S(1)}, f32[2,32,512]{2,1,0:T(8,128)S(1)}, u32[]{:S(2)}, u32[]{:S(2)}) collective-permute-start(f32[2,32,512]{2,1,0:T(8,128)S(1)} %get-tuple-element.89), channel_id=1, source_target_pairs={{0,481},{32,1},{64,33},{96,65},{128,97},{160,129},{192,161},{224,1... | collective-permute-start | bytes 393224 | tf_op jit(solution)/shard_map/ppermute | solution.py:432
  130.4 12.8 %all_to_all.46.refs_0_ = f32[32,4,128]{2,1,0:T(4,128)S(1)} all-to-all(f32[32,4,128]{2,1,0:T(4,128)S(1)} %get-tuple-element.88), channel_id=1, replica_groups=mesh['sector'=16,'block'=16,'flame'=2] {'block','flame'}, dimensions={0} | all-to-all | bytes 131072 | tf_op jit(solution)/shard_map/all_to_all | solution.py:437
  144.4 10.1 %all-to-all-start.6 = ((f32[512,1,128]{2,1,0:T(1,128)}), f32[512,1,128]{2,1,0:T(1,128)S(1)}, u32[]{:S(2)}, u32[]{:S(2)}) async-start(f32[512,1,128]{2,1,0:T(1,128)} %bitcast.1), calls=%async_computation.6 | async-start | bytes 524288 | tf_op jit(solution)/shard_map/all_to_all | solution.py:454
  154.5 6.2 %collective-permute-start.11 = (f32[2,4,16,256]{3,2,1,0:T(8,128)S(1)}, f32[2,4,16,256]{3,2,1,0:T(8,128)S(1)}, u32[]{:S(2)}, u32[]{:S(2)}) collective-permute-start(f32[2,4,16,256]{3,2,1,0:T(8,128)S(1)} %get-tuple-element.95), channel_id=1, source_target_pairs={{0,1},{1,0},{2,3},{3,2},{4,5},{5,4},{6,7},{7,6},{8,9},{9,8},{10,11... | collective-permute-start | bytes 393224 | tf_op jit(solution)/shard_map/ppermute | solution.py:453
  161.7 10.2 %all-to-all-done.6 = f32[512,1,128]{2,1,0:T(1,128)S(1)} async-done(((f32[512,1,128]{2,1,0:T(1,128)}), f32[512,1,128]{2,1,0:T(1,128)S(1)}, u32[]{:S(2)}, u32[]{:S(2)}) %all-to-all-start.6) | async-done | bytes 262176 | tf_op jit(solution)/shard_map/all_to_all | solution.py:454
  (23 shorter events, 11.2 us)
Async XLA Ops:
  2.0 10.0 %collective-permute-start = (f32[5,4,16,256]{3,2,1,0:T(8,128)S(1)}, f32[5,4,16,256]{3,2,1,0:T(8,128)S(1)}, u32[]{:S(2)}, u32[]{:S(2)}) collective-permute-start(f32[5,4,16,256]{3,2,1,0:T(8,128)S(1)} %get-tuple-element.50), channel_id=1, source_target_pairs={{0,1},{1,0},{2,3},{3,2},{4,5},{5,4},{6,7},{7,6},{8,9},{9,8},{10,11... | collective-permute-start | bytes 983048 | tf_op jit(solution)/shard_map/ppermute | solution.py:406
  12.1 6.1 %collective-permute-start.1 = (f32[112,512]{1,0:T(8,128)S(1)}, f32[112,512]{1,0:T(8,128)S(1)}, u32[]{:S(2)}, u32[]{:S(2)}) collective-permute-start(f32[112,512]{1,0:T(8,128)S(1)} %get-tuple-element.52), channel_id=1, source_target_pairs={{0,2},{2,4},{4,6},{6,8},{8,10},{10,12},{12,14},{14,16},{16,18},{18... | collective-permute-start | bytes 688136 | tf_op jit(solution)/shard_map/ppermute | solution.py:409
  13.4 8.7 %collective-permute-start.2 = (f32[112,512]{1,0:T(8,128)S(1)}, f32[112,512]{1,0:T(8,128)S(1)}, u32[]{:S(2)}, u32[]{:S(2)}) collective-permute-start(f32[112,512]{1,0:T(8,128)S(1)} %get-tuple-element.53), channel_id=1, source_target_pairs={{2,0},{4,2},{6,4},{8,6},{10,8},{12,10},{14,12},{16,14},{18,16},{20... | collective-permute-start | bytes 688136 | tf_op jit(solution)/shard_map/ppermute | solution.py:410
  22.4 29.1 %collective-permute-start.4 = (f32[13,32,512]{2,1,0:T(8,128)S(1)}, f32[13,32,512]{2,1,0:T(8,128)S(1)}, u32[]{:S(2)}, u32[]{:S(2)}) collective-permute-start(f32[13,32,512]{2,1,0:T(8,128)S(1)} %get-tuple-element.65), channel_id=1, source_target_pairs={{0,1},{1,0},{2,3},{3,2},{4,5},{5,4},{6,7},{7,6},{8,9},{9,8},{10,11... | collective-permute-start | bytes 2555912 | tf_op jit(solution)/shard_map/ppermute | solution.py:434
  25.5 26.0 %collective-permute-start.3 = (f32[2,32,512]{2,1,0:T(8,128)S(1)}, f32[2,32,512]{2,1,0:T(8,128)S(1)}, u32[]{:S(2)}, u32[]{:S(2)}) collective-permute-start(f32[2,32,512]{2,1,0:T(8,128)S(1)} %get-tuple-element.57), channel_id=1, source_target_pairs={{0,481},{32,1},{64,33},{96,65},{128,97},{160,129},{192,161},{224,1... | collective-permute-start | bytes 393224 | tf_op jit(solution)/shard_map/ppermute | solution.py:432
  52.8 15.4 %collective-permute-start.5 = (f32[2,32,512]{2,1,0:T(8,128)S(1)}, f32[2,32,512]{2,1,0:T(8,128)S(1)}, u32[]{:S(2)}, u32[]{:S(2)}) collective-permute-start(f32[2,32,512]{2,1,0:T(8,128)S(1)} %get-tuple-element.69), channel_id=1, source_target_pairs={{0,481},{32,1},{64,33},{96,65},{128,97},{160,129},{192,161},{224,1... | collective-permute-start | bytes 393224 | tf_op jit(solution)/shard_map/ppermute | solution.py:432
  69.6 17.8 %collective-permute-start.6 = (f32[2,32,512]{2,1,0:T(8,128)S(1)}, f32[2,32,512]{2,1,0:T(8,128)S(1)}, u32[]{:S(2)}, u32[]{:S(2)}) collective-permute-start(f32[2,32,512]{2,1,0:T(8,128)S(1)} %get-tuple-element.74), channel_id=1, source_target_pairs={{0,481},{32,1},{64,33},{96,65},{128,97},{160,129},{192,161},{224,1... | collective-permute-start | bytes 393224 | tf_op jit(solution)/shard_map/ppermute | solution.py:432
  88.6 18.6 %collective-permute-start.8 = (f32[2,3,32,512]{3,2,1,0:T(8,128)S(1)}, f32[2,3,32,512]{3,2,1,0:T(8,128)S(1)}, u32[]{:S(2)}, u32[]{:S(2)}) collective-permute-start(f32[2,3,32,512]{3,2,1,0:T(8,128)S(1)} %get-tuple-element.82), channel_id=1, source_target_pairs={{0,1},{1,0},{2,3},{3,2},{4,5},{5,4},{6,7},{7,6},{8,9},{9,8},{10,11... | collective-permute-start | bytes 1179656 | tf_op jit(solution)/shard_map/ppermute | solution.py:436
  90.9 16.3 %collective-permute-start.7 = (f32[2,32,512]{2,1,0:T(8,128)S(1)}, f32[2,32,512]{2,1,0:T(8,128)S(1)}, u32[]{:S(2)}, u32[]{:S(2)}) collective-permute-start(f32[2,32,512]{2,1,0:T(8,128)S(1)} %get-tuple-element.79), channel_id=1, source_target_pairs={{0,481},{32,1},{64,33},{96,65},{128,97},{160,129},{192,161},{224,1... | collective-permute-start | bytes 393224 | tf_op jit(solution)/shard_map/ppermute | solution.py:432
  108.6 16.8 %collective-permute-start.9 = (f32[2,32,512]{2,1,0:T(8,128)S(1)}, f32[2,32,512]{2,1,0:T(8,128)S(1)}, u32[]{:S(2)}, u32[]{:S(2)}) collective-permute-start(f32[2,32,512]{2,1,0:T(8,128)S(1)} %get-tuple-element.84), channel_id=1, source_target_pairs={{0,481},{32,1},{64,33},{96,65},{128,97},{160,129},{192,161},{224,1... | collective-permute-start | bytes 393224 | tf_op jit(solution)/shard_map/ppermute | solution.py:432
  126.7 16.5 %collective-permute-start.10 = (f32[2,32,512]{2,1,0:T(8,128)S(1)}, f32[2,32,512]{2,1,0:T(8,128)S(1)}, u32[]{:S(2)}, u32[]{:S(2)}) collective-permute-start(f32[2,32,512]{2,1,0:T(8,128)S(1)} %get-tuple-element.89), channel_id=1, source_target_pairs={{0,481},{32,1},{64,33},{96,65},{128,97},{160,129},{192,161},{224,1... | collective-permute-start | bytes 393224 | tf_op jit(solution)/shard_map/ppermute | solution.py:432
  144.4 27.5 %copy-start = (f32[8,16,256]{2,1,0:T(8,128)S(1)}, f32[8,16,256]{2,1,0:T(8,128)}, u32[]{:S(2)}) copy-start(f32[8,16,256]{2,1,0:T(8,128)} %refs_3_.3) | copy-start | bytes 393220
  144.4 27.5 %copy-start.1 = (s32[8,16,256]{2,1,0:T(8,128)S(1)}, s32[8,16,256]{2,1,0:T(8,128)}, u32[]{:S(2)}) copy-start(s32[8,16,256]{2,1,0:T(8,128)} %refs_4_.3) | copy-start | bytes 393220
  144.4 27.5 %all-to-all-start.6 = ((f32[512,1,128]{2,1,0:T(1,128)}), f32[512,1,128]{2,1,0:T(1,128)S(1)}, u32[]{:S(2)}, u32[]{:S(2)}) async-start(f32[512,1,128]{2,1,0:T(1,128)} %bitcast.1), calls=%async_computation.6 | async-start | bytes 524288 | tf_op jit(solution)/shard_map/all_to_all | solution.py:454
  154.5 7.2 %collective-permute-start.11 = (f32[2,4,16,256]{3,2,1,0:T(8,128)S(1)}, f32[2,4,16,256]{3,2,1,0:T(8,128)S(1)}, u32[]{:S(2)}, u32[]{:S(2)}) collective-permute-start(f32[2,4,16,256]{3,2,1,0:T(8,128)S(1)} %get-tuple-element.95), channel_id=1, source_target_pairs={{0,1},{1,0},{2,3},{3,2},{4,5},{5,4},{6,7},{7,6},{8,9},{9,8},{10,11... | collective-permute-start | bytes 393224 | tf_op jit(solution)/shard_map/ppermute | solution.py:453

commit v8 on v7

--- a/solution.py
+++ b/solution.py
@@ -424,7 +424,6 @@
         (field, field, field, field, owners, field, field, arr(5 * INNER - 2, rows, width), plane),
         4, [full, full], name="init",
     )(keep, got, before, after)
-    sent, outer, inner = lax.optimization_barrier((sent, outer, inner))
     cut, layers = arr(2, half, axial, radial), (2, INNER, rows, width)
     everyone = 2 * blocks * sectors
     deep = halo = None

time: 174 us -> 175 us (level)
  no operation moved by 1% of the time
where the time goes in v8:
time: 175 us; the launch traced here: 174 us
  blocking collectives  84.3 us (48%)
  starting transfers between devices  57.6 us (33%)
  waiting for transfers between devices  19.8 us (11%)
  Pallas kernels  11.7 us (7%)
    all_to_all x6, blocking collectives, on_device(): recv = lax.all_to_all(sent, BF, 0, 0, tiled=True)  84.3 us
    ppermute x6, starting transfers between devices, on_device(): outer_in = lax.ppermute(outer, ('sector', 'flame'), ring)  24.4 us
    ppermute x2, starting transfers between devices, on_device(): got = lax.ppermute(give, 'flame', swap)  15 us
    all_to_all x1, starting transfers between devices, on_device(): recv = lax.all_to_all(sent, ('sector',) + BF, 0, 0, tiled=True)  10.2 us
    all_to_all x1, waiting for transfers between devices, on_device(): recv = lax.all_to_all(sent, ('sector',) + BF, 0, 0, tiled=True)  10.2 us
    pallas_call x5, Pallas kernels, on_device(): _call(step, (field, field, arr(*layers), plane, message), len(args) + 2,...  6.5 us
    ppermute x1, waiting for transfers between devices, on_device(): lax.ppermute(first_rows, 'block', [(i + 1, i) for i in range(blocks - 1)])  3.85 us
    ppermute x1, waiting for transfers between devices, on_device(): lax.ppermute(last_rows, 'block', [(i, i + 1) for i in range(blocks - 1)])  3.54 us
  transfers between devices with their start and end apart: 13, of which 5 were waited for; matrix products, arithmetic and copies ran while one was open for 0% of the time, Pallas kernels for 1%

profile of v8, /device:TPU:1, one launch (start us, length us, event | category | flops | bytes accessed | tf_op | source)
XLA Modules:
  0.0 174.3 jit_solution(14207722981089925816)
XLA Ops:
  0.6 1.4 pack.1
  2.0 8.7 %collective-permute-start = (f32[5,4,16,256]{3,2,1,0:T(8,128)S(1)}, f32[5,4,16,256]{3,2,1,0:T(8,128)S(1)}, u32[]{:S(2)}, u32[]{:S(2)}) collective-permute-start(f32[5,4,16,256]{3,2,1,0:T(8,128)S(1)} %get-tuple-element.47), channel_id=1, source_target_pairs={{0,1},{1,0},{2,3},{3,2},{4,5},{5,4},{6,7},{7,6},{8,9},{9,8},{10,11... | collective-permute-start | bytes 983048 | tf_op jit(solution)/shard_map/ppermute | solution.py:406
  12.1 1.3 collective-permute-start.1
  14.7 3.5 %collective-permute-done.1.refs_2_ = f32[112,512]{1,0:T(8,128)S(1)} collective-permute-done((f32[112,512]{1,0:T(8,128)S(1)}, f32[112,512]{1,0:T(8,128)S(1)}, u32[]{:S(2)}, u32[]{:S(2)}) %collective-permute-start.1) | collective-permute-done | bytes 229408 | tf_op jit(solution)/shard_map/ppermute | solution.py:409
  18.3 3.8 %collective-permute-done.2.refs_3_ = f32[112,512]{1,0:T(8,128)S(1)} collective-permute-done((f32[112,512]{1,0:T(8,128)S(1)}, f32[112,512]{1,0:T(8,128)S(1)}, u32[]{:S(2)}, u32[]{:S(2)}) %collective-permute-start.2) | collective-permute-done | bytes 229408 | tf_op jit(solution)/shard_map/ppermute | solution.py:410
  22.4 3.1 %collective-permute-start.4 = (f32[13,32,512]{2,1,0:T(8,128)S(1)}, f32[13,32,512]{2,1,0:T(8,128)S(1)}, u32[]{:S(2)}, u32[]{:S(2)}) collective-permute-start(f32[13,32,512]{2,1,0:T(8,128)S(1)} %get-tuple-element.59), channel_id=1, source_target_pairs={{0,1},{1,0},{2,3},{3,2},{4,5},{5,4},{6,7},{7,6},{8,9},{9,8},{10,11... | collective-permute-start | bytes 2555912 | tf_op jit(solution)/shard_map/ppermute | solution.py:433
  25.5 7.0 %collective-permute-start.3 = (f32[2,32,512]{2,1,0:T(8,128)S(1)}, f32[2,32,512]{2,1,0:T(8,128)S(1)}, u32[]{:S(2)}, u32[]{:S(2)}) collective-permute-start(f32[2,32,512]{2,1,0:T(8,128)S(1)} %get-tuple-element.51), channel_id=1, source_target_pairs={{0,481},{32,1},{64,33},{96,65},{128,97},{160,129},{192,161},{224,1... | collective-permute-start | bytes 393224 | tf_op jit(solution)/shard_map/ppermute | solution.py:431
  33.8 18.9 %all_to_all.41.refs_0_ = f32[32,4,128]{2,1,0:T(4,128)S(1)} all-to-all(f32[32,4,128]{2,1,0:T(4,128)S(1)} %get-tuple-element.48), channel_id=1, replica_groups=mesh['sector'=16,'block'=16,'flame'=2] {'block','flame'}, dimensions={0} | all-to-all | bytes 131072 | tf_op jit(solution)/shard_map/all_to_all | solution.py:436
  52.7 1.3 step.5
  54.1 1.9 %collective-permute-start.5 = (f32[2,32,512]{2,1,0:T(8,128)S(1)}, f32[2,32,512]{2,1,0:T(8,128)S(1)}, u32[]{:S(2)}, u32[]{:S(2)}) collective-permute-start(f32[2,32,512]{2,1,0:T(8,128)S(1)} %get-tuple-element.63), channel_id=1, source_target_pairs={{0,481},{32,1},{64,33},{96,65},{128,97},{160,129},{192,161},{224,1... | collective-permute-start | bytes 393224 | tf_op jit(solution)/shard_map/ppermute | solution.py:431
  56.0 13.5 %all_to_all.42.refs_0_ = f32[32,4,128]{2,1,0:T(4,128)S(1)} all-to-all(f32[32,4,128]{2,1,0:T(4,128)S(1)} %get-tuple-element.62), channel_id=1, replica_groups=mesh['sector'=16,'block'=16,'flame'=2] {'block','flame'}, dimensions={0} | all-to-all | bytes 131072 | tf_op jit(solution)/shard_map/all_to_all | solution.py:436
  70.8 5.0 %collective-permute-start.6 = (f32[2,32,512]{2,1,0:T(8,128)S(1)}, f32[2,32,512]{2,1,0:T(8,128)S(1)}, u32[]{:S(2)}, u32[]{:S(2)}) collective-permute-start(f32[2,32,512]{2,1,0:T(8,128)S(1)} %get-tuple-element.68), channel_id=1, source_target_pairs={{0,481},{32,1},{64,33},{96,65},{128,97},{160,129},{192,161},{224,1... | collective-permute-start | bytes 393224 | tf_op jit(solution)/shard_map/ppermute | solution.py:431
  75.8 12.8 %all_to_all.43.refs_0_ = f32[32,4,128]{2,1,0:T(4,128)S(1)} all-to-all(f32[32,4,128]{2,1,0:T(4,128)S(1)} %get-tuple-element.67), channel_id=1, replica_groups=mesh['sector'=16,'block'=16,'flame'=2] {'block','flame'}, dimensions={0} | all-to-all | bytes 131072 | tf_op jit(solution)/shard_map/all_to_all | solution.py:436
  89.8 2.3 %collective-permute-start.8 = (f32[2,3,32,512]{3,2,1,0:T(8,128)S(1)}, f32[2,3,32,512]{3,2,1,0:T(8,128)S(1)}, u32[]{:S(2)}, u32[]{:S(2)}) collective-permute-start(f32[2,3,32,512]{3,2,1,0:T(8,128)S(1)} %get-tuple-element.76), channel_id=1, source_target_pairs={{0,1},{1,0},{2,3},{3,2},{4,5},{5,4},{6,7},{7,6},{8,9},{9,8},{10,11... | collective-permute-start | bytes 1179656 | tf_op jit(solution)/shard_map/ppermute | solution.py:435
  92.2 2.7 %collective-permute-start.7 = (f32[2,32,512]{2,1,0:T(8,128)S(1)}, f32[2,32,512]{2,1,0:T(8,128)S(1)}, u32[]{:S(2)}, u32[]{:S(2)}) collective-permute-start(f32[2,32,512]{2,1,0:T(8,128)S(1)} %get-tuple-element.73), channel_id=1, source_target_pairs={{0,481},{32,1},{64,33},{96,65},{128,97},{160,129},{192,161},{224,1... | collective-permute-start | bytes 393224 | tf_op jit(solution)/shard_map/ppermute | solution.py:431
  94.9 13.7 %all_to_all.44.refs_0_ = f32[32,4,128]{2,1,0:T(4,128)S(1)} all-to-all(f32[32,4,128]{2,1,0:T(4,128)S(1)} %get-tuple-element.72), channel_id=1, replica_groups=mesh['sector'=16,'block'=16,'flame'=2] {'block','flame'}, dimensions={0} | all-to-all | bytes 131072 | tf_op jit(solution)/shard_map/all_to_all | solution.py:436
  108.5 1.3 step.8
  109.8 4.1 %collective-permute-start.9 = (f32[2,32,512]{2,1,0:T(8,128)S(1)}, f32[2,32,512]{2,1,0:T(8,128)S(1)}, u32[]{:S(2)}, u32[]{:S(2)}) collective-permute-start(f32[2,32,512]{2,1,0:T(8,128)S(1)} %get-tuple-element.78), channel_id=1, source_target_pairs={{0,481},{32,1},{64,33},{96,65},{128,97},{160,129},{192,161},{224,1... | collective-permute-start | bytes 393224 | tf_op jit(solution)/shard_map/ppermute | solution.py:431
  113.9 12.7 %all_to_all.45.refs_0_ = f32[32,4,128]{2,1,0:T(4,128)S(1)} all-to-all(f32[32,4,128]{2,1,0:T(4,128)S(1)} %get-tuple-element.77), channel_id=1, replica_groups=mesh['sector'=16,'block'=16,'flame'=2] {'block','flame'}, dimensions={0} | all-to-all | bytes 131072 | tf_op jit(solution)/shard_map/all_to_all | solution.py:436
  127.9 3.7 %collective-permute-start.10 = (f32[2,32,512]{2,1,0:T(8,128)S(1)}, f32[2,32,512]{2,1,0:T(8,128)S(1)}, u32[]{:S(2)}, u32[]{:S(2)}) collective-permute-start(f32[2,32,512]{2,1,0:T(8,128)S(1)} %get-tuple-element.83), channel_id=1, source_target_pairs={{0,481},{32,1},{64,33},{96,65},{128,97},{160,129},{192,161},{224,1... | collective-permute-start | bytes 393224 | tf_op jit(solution)/shard_map/ppermute | solution.py:431
  131.6 12.8 %all_to_all.46.refs_0_ = f32[32,4,128]{2,1,0:T(4,128)S(1)} all-to-all(f32[32,4,128]{2,1,0:T(4,128)S(1)} %get-tuple-element.82), channel_id=1, replica_groups=mesh['sector'=16,'block'=16,'flame'=2] {'block','flame'}, dimensions={0} | all-to-all | bytes 131072 | tf_op jit(solution)/shard_map/all_to_all | solution.py:436
  145.6 10.2 %all-to-all-start.6 = ((f32[512,1,128]{2,1,0:T(1,128)}), f32[512,1,128]{2,1,0:T(1,128)S(1)}, u32[]{:S(2)}, u32[]{:S(2)}) async-start(f32[512,1,128]{2,1,0:T(1,128)} %bitcast.1), calls=%async_computation.6 | async-start | bytes 524288 | tf_op jit(solution)/shard_map/all_to_all | solution.py:453
  155.9 6.2 %collective-permute-start.11 = (f32[2,4,16,256]{3,2,1,0:T(8,128)S(1)}, f32[2,4,16,256]{3,2,1,0:T(8,128)S(1)}, u32[]{:S(2)}, u32[]{:S(2)}) collective-permute-start(f32[2,4,16,256]{3,2,1,0:T(8,128)S(1)} %get-tuple-element.89), channel_id=1, source_target_pairs={{0,1},{1,0},{2,3},{3,2},{4,5},{5,4},{6,7},{7,6},{8,9},{9,8},{10,11... | collective-permute-start | bytes 393224 | tf_op jit(solution)/shard_map/ppermute | solution.py:452
  163.1 10.2 %all-to-all-done.6 = f32[512,1,128]{2,1,0:T(1,128)S(1)} async-done(((f32[512,1,128]{2,1,0:T(1,128)}), f32[512,1,128]{2,1,0:T(1,128)S(1)}, u32[]{:S(2)}, u32[]{:S(2)}) %all-to-all-start.6) | async-done | bytes 262176 | tf_op jit(solution)/shard_map/all_to_all | solution.py:453
  (23 shorter events, 11.2 us)
Async XLA Ops:
  2.0 10.0 %collective-permute-start = (f32[5,4,16,256]{3,2,1,0:T(8,128)S(1)}, f32[5,4,16,256]{3,2,1,0:T(8,128)S(1)}, u32[]{:S(2)}, u32[]{:S(2)}) collective-permute-start(f32[5,4,16,256]{3,2,1,0:T(8,128)S(1)} %get-tuple-element.47), channel_id=1, source_target_pairs={{0,1},{1,0},{2,3},{3,2},{4,5},{5,4},{6,7},{7,6},{8,9},{9,8},{10,11... | collective-permute-start | bytes 983048 | tf_op jit(solution)/shard_map/ppermute | solution.py:406
  12.1 6.1 %collective-permute-start.1 = (f32[112,512]{1,0:T(8,128)S(1)}, f32[112,512]{1,0:T(8,128)S(1)}, u32[]{:S(2)}, u32[]{:S(2)}) collective-permute-start(f32[112,512]{1,0:T(8,128)S(1)} %get-tuple-element.49), channel_id=1, source_target_pairs={{0,2},{2,4},{4,6},{6,8},{8,10},{10,12},{12,14},{14,16},{16,18},{18... | collective-permute-start | bytes 688136 | tf_op jit(solution)/shard_map/ppermute | solution.py:409
  13.4 8.7 %collective-permute-start.2 = (f32[112,512]{1,0:T(8,128)S(1)}, f32[112,512]{1,0:T(8,128)S(1)}, u32[]{:S(2)}, u32[]{:S(2)}) collective-permute-start(f32[112,512]{1,0:T(8,128)S(1)} %get-tuple-element.50), channel_id=1, source_target_pairs={{2,0},{4,2},{6,4},{8,6},{10,8},{12,10},{14,12},{16,14},{18,16},{20... | collective-permute-start | bytes 688136 | tf_op jit(solution)/shard_map/ppermute | solution.py:410
  22.4 30.3 %collective-permute-start.4 = (f32[13,32,512]{2,1,0:T(8,128)S(1)}, f32[13,32,512]{2,1,0:T(8,128)S(1)}, u32[]{:S(2)}, u32[]{:S(2)}) collective-permute-start(f32[13,32,512]{2,1,0:T(8,128)S(1)} %get-tuple-element.59), channel_id=1, source_target_pairs={{0,1},{1,0},{2,3},{3,2},{4,5},{5,4},{6,7},{7,6},{8,9},{9,8},{10,11... | collective-permute-start | bytes 2555912 | tf_op jit(solution)/shard_map/ppermute | solution.py:433
  25.5 27.2 %collective-permute-start.3 = (f32[2,32,512]{2,1,0:T(8,128)S(1)}, f32[2,32,512]{2,1,0:T(8,128)S(1)}, u32[]{:S(2)}, u32[]{:S(2)}) collective-permute-start(f32[2,32,512]{2,1,0:T(8,128)S(1)} %get-tuple-element.51), channel_id=1, source_target_pairs={{0,481},{32,1},{64,33},{96,65},{128,97},{160,129},{192,161},{224,1... | collective-permute-start | bytes 393224 | tf_op jit(solution)/shard_map/ppermute | solution.py:431
  54.1 15.4 %collective-permute-start.5 = (f32[2,32,512]{2,1,0:T(8,128)S(1)}, f32[2,32,512]{2,1,0:T(8,128)S(1)}, u32[]{:S(2)}, u32[]{:S(2)}) collective-permute-start(f32[2,32,512]{2,1,0:T(8,128)S(1)} %get-tuple-element.63), channel_id=1, source_target_pairs={{0,481},{32,1},{64,33},{96,65},{128,97},{160,129},{192,161},{224,1... | collective-permute-start | bytes 393224 | tf_op jit(solution)/shard_map/ppermute | solution.py:431
  70.8 17.8 %collective-permute-start.6 = (f32[2,32,512]{2,1,0:T(8,128)S(1)}, f32[2,32,512]{2,1,0:T(8,128)S(1)}, u32[]{:S(2)}, u32[]{:S(2)}) collective-permute-start(f32[2,32,512]{2,1,0:T(8,128)S(1)} %get-tuple-element.68), channel_id=1, source_target_pairs={{0,481},{32,1},{64,33},{96,65},{128,97},{160,129},{192,161},{224,1... | collective-permute-start | bytes 393224 | tf_op jit(solution)/shard_map/ppermute | solution.py:431
  89.8 18.7 %collective-permute-start.8 = (f32[2,3,32,512]{3,2,1,0:T(8,128)S(1)}, f32[2,3,32,512]{3,2,1,0:T(8,128)S(1)}, u32[]{:S(2)}, u32[]{:S(2)}) collective-permute-start(f32[2,3,32,512]{3,2,1,0:T(8,128)S(1)} %get-tuple-element.76), channel_id=1, source_target_pairs={{0,1},{1,0},{2,3},{3,2},{4,5},{5,4},{6,7},{7,6},{8,9},{9,8},{10,11... | collective-permute-start | bytes 1179656 | tf_op jit(solution)/shard_map/ppermute | solution.py:435
  92.2 16.4 %collective-permute-start.7 = (f32[2,32,512]{2,1,0:T(8,128)S(1)}, f32[2,32,512]{2,1,0:T(8,128)S(1)}, u32[]{:S(2)}, u32[]{:S(2)}) collective-permute-start(f32[2,32,512]{2,1,0:T(8,128)S(1)} %get-tuple-element.73), channel_id=1, source_target_pairs={{0,481},{32,1},{64,33},{96,65},{128,97},{160,129},{192,161},{224,1... | collective-permute-start | bytes 393224 | tf_op jit(solution)/shard_map/ppermute | solution.py:431
  109.8 16.7 %collective-permute-start.9 = (f32[2,32,512]{2,1,0:T(8,128)S(1)}, f32[2,32,512]{2,1,0:T(8,128)S(1)}, u32[]{:S(2)}, u32[]{:S(2)}) collective-permute-start(f32[2,32,512]{2,1,0:T(8,128)S(1)} %get-tuple-element.78), channel_id=1, source_target_pairs={{0,481},{32,1},{64,33},{96,65},{128,97},{160,129},{192,161},{224,1... | collective-permute-start | bytes 393224 | tf_op jit(solution)/shard_map/ppermute | solution.py:431
  127.9 16.5 %collective-permute-start.10 = (f32[2,32,512]{2,1,0:T(8,128)S(1)}, f32[2,32,512]{2,1,0:T(8,128)S(1)}, u32[]{:S(2)}, u32[]{:S(2)}) collective-permute-start(f32[2,32,512]{2,1,0:T(8,128)S(1)} %get-tuple-element.83), channel_id=1, source_target_pairs={{0,481},{32,1},{64,33},{96,65},{128,97},{160,129},{192,161},{224,1... | collective-permute-start | bytes 393224 | tf_op jit(solution)/shard_map/ppermute | solution.py:431
  145.6 27.7 %copy-start = (f32[8,16,256]{2,1,0:T(8,128)S(1)}, f32[8,16,256]{2,1,0:T(8,128)}, u32[]{:S(2)}) copy-start(f32[8,16,256]{2,1,0:T(8,128)} %refs_3_.3) | copy-start | bytes 393220
  145.6 27.7 %copy-start.1 = (s32[8,16,256]{2,1,0:T(8,128)S(1)}, s32[8,16,256]{2,1,0:T(8,128)}, u32[]{:S(2)}) copy-start(s32[8,16,256]{2,1,0:T(8,128)} %refs_4_.3) | copy-start | bytes 393220
  145.6 27.7 %all-to-all-start.6 = ((f32[512,1,128]{2,1,0:T(1,128)}), f32[512,1,128]{2,1,0:T(1,128)S(1)}, u32[]{:S(2)}, u32[]{:S(2)}) async-start(f32[512,1,128]{2,1,0:T(1,128)} %bitcast.1), calls=%async_computation.6 | async-start | bytes 524288 | tf_op jit(solution)/shard_map/all_to_all | solution.py:453
  155.9 7.2 %collective-permute-start.11 = (f32[2,4,16,256]{3,2,1,0:T(8,128)S(1)}, f32[2,4,16,256]{3,2,1,0:T(8,128)S(1)}, u32[]{:S(2)}, u32[]{:S(2)}) collective-permute-start(f32[2,4,16,256]{3,2,1,0:T(8,128)S(1)} %get-tuple-element.89), channel_id=1, source_target_pairs={{0,1},{1,0},{2,3},{3,2},{4,5},{5,4},{6,7},{7,6},{8,9},{9,8},{10,11... | collective-permute-start | bytes 393224 | tf_op jit(solution)/shard_map/ppermute | solution.py:452
